TPU v7x, 256 devices: a whole 4x4x8 slice. The times are simulated.
256 devices in a mesh: cores: 4 (over x), row: 32 (over z, y), tensor: 2 (over core).
Axes of the slice: x: 4, y: 4, z: 8, core: 2. Of those that a mesh axis runs over, the one named last changes fastest.
Arguments:
- cores: float32 [2, 4, 128, 256, 256], P('tensor', 'cores', 'row'), may hold values from -1 to 1, as said below
- incoming: float32 [2, 256, 256], P('tensor'), may hold values from -1 to 2, as said below
Outputs:
- frames: float32 [2, 4, 128, 256, 256], P('tensor', 'cores', 'row')
- tail: float32 [2, 256, 256], P('tensor', 'cores')
- correlation: float32 [2, 256, 256], P('tensor', 'cores')
Inputs may be any that keep to these rules, and one draw needn't show every extreme that they name: `cores`: each core's unfolding over (mode index, left rank) has full column rank and is well conditioned. `incoming`: upper triangular, diagonal entries from 1 to 2.
All inputs are finite; a program needn't handle non-finite values.
Results may differ from a plain program's by a relative error of at most 0.0001.
Values sent between devices are 32-bit elements; how exact they have to be, the bound alone decides.
No kernel may reach another device: no remote copies, remote signals or barrier semaphores. Data moves between devices by JAX's collectives and lax.ppermute only.
A program may use at most 64 MiB of HBM per device.

v0:
```python
import jax
import jax.numpy as jnp
from jax import lax
from jax.sharding import PartitionSpec as P

RANK = 256
MODE = 128


HIGH_PRECISION = lax.Precision.HIGHEST


def swapped(value, axis, distance):
    mask = 2**distance
    pairs = [(source, source ^ mask) for source in range(lax.axis_size(axis))]
    return lax.ppermute(value, axis, pairs)


def passed_along(value, axis, steps):
    count = lax.axis_size(axis)
    first, last = (max(0, -steps), min(count, count - steps))
    return lax.ppermute(value, axis, [(source, source + steps) for source in range(first, last)])


def cut_along(x, dim, length):
    before, after = (x.shape[:dim], x.shape[dim + 1 :])
    return jnp.moveaxis(x.reshape(*before, length, -1, *after), dim, 0)


def sent_and_summed(x, axis, dim):
    tiles = cut_along(x, dim, lax.axis_size(axis))
    arrived = lax.all_to_all(tiles, axis, split_axis=0, concat_axis=0, tiled=True)
    return arrived.sum(axis=0)


def filled_up(lines, length):
    spare = -lines.shape[0] % length
    if not spare:
        return lines
    return jnp.concatenate([lines, jnp.zeros((spare, *lines.shape[1:]), lines.dtype)])


def in_order(tiles, dim):
    tiles = jnp.moveaxis(tiles, 0, dim)
    dims = tiles.shape
    return tiles.reshape(*dims[:dim], dims[dim] * dims[dim + 1], *dims[dim + 2 :])


def copy_for_each(x, axis):
    length = lax.axis_size(axis)
    return lax.all_to_all(jnp.broadcast_to(x[None], (length, *x.shape)), axis, 0, 0, tiled=True)


def collect(x, axis, dim):
    return in_order(copy_for_each(x, axis), dim)


def nested_sum(x, axes):
    own = sent_and_summed(filled_up(x, lax.axis_size(axes)), axes, 0)
    whole = collect(own, axes, 0)
    return whole[: len(x)].reshape(x.shape)


def in_one(arrays, axis):
    ends = [0]
    for a in arrays:
        ends.append(ends[-1] + a.size)
    total = nested_sum(jnp.concatenate([a.ravel() for a in arrays]), axis)
    return tuple((total[b:e].reshape(a.shape) for a, b, e in zip(arrays, ends, ends[1:])))


def picked(x, axis, root):
    return lax.dynamic_index_in_dim(lax.all_gather(x, axis), root, 0, keepdims=False)


def mix_block(upper, block):
    return jnp.einsum("ab,ibc->iac", upper, block, precision=HIGH_PRECISION)


def gram_of(mixed_gram):
    return jnp.einsum("bgk,bgj->kj", mixed_gram, mixed_gram, precision=HIGH_PRECISION)


def link_part(link, left, right):
    middle = jnp.einsum("bc,icd->ibd", link, right, precision=HIGH_PRECISION)
    return jnp.einsum("iba,ibd->ad", left, middle, precision=HIGH_PRECISION)


def make_frame(mixed_gram, gram_matrix):
    lower = jnp.linalg.cholesky(gram_matrix)
    flat = mixed_gram.reshape(-1, gram_matrix.shape[0])
    solved = lax.linalg.triangular_solve(lower, flat.T, left_side=True, lower=True)
    basis_frame = solved.T.reshape(mixed_gram.shape)
    return (basis_frame, lower.T)


def shards(cores, incoming):
    rank = cores.shape[-1]
    factor = float(MODE * RANK) ** 0.5
    section = lax.axis_index("cores")
    train_sections = lax.axis_size("cores")
    own = cores[0]
    upper_start = incoming[0]
    partner, partner_in = swapped((cores, incoming), "tensor", 0)
    partner_blocks = partner[0]
    link_start = jnp.dot(upper_start.T, partner_in[0], precision=HIGH_PRECISION)
    upper = upper_start
    link = link_start
    result = jnp.zeros_like(own)
    for tick in range(train_sections):
        if tick > 0:
            got_upper, got_link = passed_along((upper, link), "cores", 1)
            upper = jnp.where(section < tick, upper_start, got_upper)
            link = jnp.where(section < tick, link_start, got_link)
        active = section == tick
        block = own[0]
        other_block = partner_blocks[0]

        def busy_terms(operands):
            upper_now, link_now = operands
            mixed_now = mix_block(upper_now, block)
            return (mixed_now, gram_of(mixed_now), link_part(link_now, block, other_block))

        def quiet_terms(operands):
            upper_now, link_now = operands
            return (jnp.zeros_like(block), jnp.zeros_like(upper_now), jnp.zeros_like(link_now))

        mixed_gram, local_gram, partial_bond = lax.cond(
            active, busy_terms, quiet_terms, (upper, link)
        )

        def busy_frame(operands):
            mixed_now, gram_now, upper_now = operands
            return make_frame(mixed_now, gram_now)

        def quiet_frame(operands):
            mixed_now, gram_now, upper_now = operands
            return (jnp.zeros_like(mixed_now), upper_now)

        gram_matrix, summed_bond = in_one((local_gram, partial_bond), "row")
        basis_frame, upper = lax.cond(
            active, busy_frame, quiet_frame, (mixed_gram, gram_matrix, upper)
        )
        link = jnp.where(active, summed_bond, link)
        new_blocks = [basis_frame]
        stacked = jnp.stack(new_blocks)
        result = jnp.where(active, stacked, result)
    tail, link = (
        picked(upper, "cores", train_sections - 1),
        picked(link, "cores", train_sections - 1),
    )
    share = rank // train_sections
    tail_rows = lax.dynamic_slice_in_dim(tail, section * share, share, 0)
    correlation_rows = lax.dynamic_slice_in_dim(link, section * share, share, 0)
    return ((result * factor)[None], tail_rows[None], correlation_rows[None])


def solution(mesh):
    in_specs = (P("tensor", "cores", "row", None, None), P("tensor", None, None))
    out_specs = (
        P("tensor", "cores", "row", None, None),
        P("tensor", "cores", None),
        P("tensor", "cores", None),
    )
    return jax.shard_map(shards, mesh=mesh, in_specs=in_specs, out_specs=out_specs, check_vma=False)
```

profile of v0, /device:TPU:1, one launch (start us, length us, event | category | flops | bytes accessed | tf_op | source)
XLA Modules:
  0.0 640.8 jit_solution(18073268108796015389)
XLA Ops:
  7.2 1.7 copy.81
  8.8 3.3 collective-permute-start
  12.3 2.7 collective-permute-done.1
  14.9 2.2 fusion.52
  17.2 12.5 %conditional.8 = (f32[4,256,256]{1,2,0:T(8,128)S(1)}, f32[16,4096]{1,0:T(8,128)}, f32[16,4096]{1,0:T(8,128)}) conditional(s32[]{:T(128)} %convert_element_type.19, () %tuple.90, (f32[4,256,256]{2,1,0:T(8,128)S(1)}, f32[256,256]{1,0:T(8,128)S(1)}, f32[4,256,256]{1,2,0:T(8,128)S(1)}, f32[256,256]{1,0:T(8,128)}) %tuple.244), branch_computations={%region_0.0_spmd, %region_1.0_spmd} | conditional | flops 3221225472 | bytes 18350160 | solution.py:128
  17.2 1.8 convolution_bitcast_fusion.1
  19.0 1.7 convolution_bitcast_fusion.3
  20.8 1.7 concatenate.18
  22.5 2.0 convolution_bitcast_fusion
  24.5 1.7 convolution_bitcast_fusion.2
  26.2 1.8 copy.67
  28.0 1.7 concatenate.19
  31.3 25.9 %all_to_all.60 = f32[32,1,4096]{2,1,0:T(1,128)} all-to-all(f32[32,1,4096]{2,1,0:T(1,128)S(1)} %all_to_all.40), channel_id=1, replica_groups=mesh['cores'=4,'row'=32,'tensor'=2] {'row'}, dimensions={0} | all-to-all | bytes 1048576 | tf_op jit(solution)/shard_map/all_to_all | solution.py:32
  57.3 1.4 reduce_sum.36
  59.9 5.2 all-to-all-start.1
  65.1 15.2 %all-to-all-done.1 = f32[32,1,4096]{2,1,0:T(1,128)} async-done(((f32[32,1,4096]{2,1,0:T(1,128)}), f32[32,1,4096]{2,1,0:T(1,128)}, u32[]{:S(2)}, u32[]{:S(2)}) %all-to-all-start.1) | async-done | bytes 524320 | tf_op jit(solution)/shard_map/all_to_all | solution.py:51
  80.3 79.6 %conditional.9 = (f32[256,256]{0,1:T(8,128)}, f32[4,256,256]{2,1,0:T(8,128)}) conditional(s32[]{:T(128)} %convert_element_type.19, (f32[256,256]{1,0:T(8,128)S(1)}) %tuple.245, (f32[32,1,4096]{2,1,0:T(1,128)}, f32[4,256,256]{1,2,0:T(8,128)S(1)}) %tuple.92), branch_computations={%region_3.0_spmd, %region_4.11_spmd} | conditional | flops 655245568 | bytes 18614600 | solution.py:141
  80.5 1.3 copy.83
  82.6 1.7 reshape.181
  84.3 1.8 copy.77
  87.8 11.7 %cholesky.214 = f32[128,128]{1,0:T(8,128)S(1)} custom-call(f32[128,128]{1,0:T(8,128)S(1)} %cholesky.346), custom_call_target="Cholesky" | custom-call | tf_op jit(solution)/shard_map/cond/branch_1_fun/jit(cholesky)/cholesky | solution.py:90
  99.6 10.4 %custom-call.17 = f32[1,128,128]{1,2,0:T(8,128)} custom-call(f32[1,128,128]{2,1,0:T(8,128)S(1)} %get-tuple-element.238), custom_call_target="InvertDiagBlocksLowerTriangular" | custom-call | tf_op jit(solution)/shard_map/cond/branch_1_fun/jit(cholesky)/cholesky | solution.py:90
  112.2 11.7 %cholesky.231 = f32[128,128]{1,0:T(8,128)S(1)} custom-call(f32[128,128]{1,0:T(8,128)S(1)} %convolution_subtract_fusion.1), custom_call_target="Cholesky" | custom-call | tf_op jit(solution)/shard_map/cond/branch_1_fun/jit(cholesky)/cholesky | solution.py:90
  126.4 1.8 fusion.12
  128.3 5.8 while.8
  128.9 2.3 bitcast_dynamic-update-slice_fusion.11
  131.8 2.2 bitcast_dynamic-update-slice_fusion.11
  134.7 20.5 %custom-call.18 = f32[2,128,128]{1,2,0:T(8,128)S(1)} custom-call(f32[2,128,128]{2,1,0:T(8,128)} %copy-done.33), custom_call_target="InvertDiagBlocksLowerTriangular" | custom-call | tf_op jit(solution)/shard_map/cond/branch_1_fun/triangular_solve/custom-call.0 | solution.py:92
  156.0 1.4 convolution_subtract_fusion
  158.1 1.3 copy.122
  161.0 2.0 collective-permute-start.2
  163.0 1.6 slice_reduce_fusion.3
  165.6 1.3 collective-permute-start.3
  167.0 6.0 collective-permute-done.3
  173.8 1.6 conditional.10
  177.0 21.6 %all_to_all.61 = f32[32,1,4096]{2,1,0:T(1,128)} all-to-all(f32[32,1,4096]{2,1,0:T(1,128)S(1)} %all_to_all.43), channel_id=1, replica_groups=mesh['cores'=4,'row'=32,'tensor'=2] {'row'}, dimensions={0} | all-to-all | bytes 1048576 | tf_op jit(solution)/shard_map/all_to_all | solution.py:32
  198.6 1.4 reduce_sum.37
  200.4 20.9 %all_to_all.62 = f32[32,1,4096]{2,1,0:T(1,128)S(1)} all-to-all(f32[32,1,4096]{2,1,0:T(1,128)S(1)} %broadcast_in_dim.14), channel_id=1, replica_groups=mesh['cores'=4,'row'=32,'tensor'=2] {'row'}, dimensions={0} | all-to-all | bytes 1048576 | tf_op jit(solution)/shard_map/all_to_all | solution.py:51
  222.2 1.4 slice_reduce_fusion.2
  223.5 1.7 reshape.198
  225.2 1.7 broadcast_select_fusion.2
  226.9 15.8 %collective-permute-start.5 = (f32[256,256]{1,0:T(8,128)}, f32[256,256]{1,0:T(8,128)}, u32[]{:S(2)}, u32[]{:S(2)}) collective-permute-start(f32[256,256]{1,0:T(8,128)} %broadcast_select_fusion.2), channel_id=1, source_target_pairs={{0,64},{64,128},{128,192},{1,65},{65,129},{129,193},{2,66},{66,130... | collective-permute-start | bytes 786440 | tf_op jit(solution)/shard_map/ppermute | solution.py:22
  242.7 9.5 %conditional.11 = (f32[256,256]{0,1:T(8,128)}, f32[4,256,256]{2,1,0:T(8,128)}) conditional(s32[]{:T(128)} %convert_element_type.18, (f32[256,256]{1,0:T(8,128)}) %tuple.249, (f32[32,1,4096]{2,1,0:T(1,128)}, f32[4,256,256]{1,2,0:T(8,128)S(1)}) %tuple.246), branch_computations={%region_12.15_spmd, %region_13.16_spmd} | conditional | flops 655245568 | bytes 18614600 | solution.py:141
  242.7 1.8 copy.115
  253.3 71.4 %collective-permute-start.4 = (f32[256,256]{1,0:T(8,128)S(1)}, f32[256,256]{1,0:T(8,128)S(1)}, u32[]{:S(2)}, u32[]{:S(2)}) collective-permute-start(f32[256,256]{1,0:T(8,128)S(1)} %copy.89), channel_id=1, source_target_pairs={{0,64},{64,128},{128,192},{1,65},{65,129},{129,193},{2,66},{66,130... | collective-permute-start | bytes 786440 | tf_op jit(solution)/shard_map/ppermute | solution.py:22
  325.6 2.5 collective-permute-done.4
  328.8 1.5 conditional.12
  331.9 22.1 %all_to_all.63 = f32[32,1,4096]{2,1,0:T(1,128)} all-to-all(f32[32,1,4096]{2,1,0:T(1,128)S(1)} %all_to_all.46), channel_id=1, replica_groups=mesh['cores'=4,'row'=32,'tensor'=2] {'row'}, dimensions={0} | all-to-all | bytes 1048576 | tf_op jit(solution)/shard_map/all_to_all | solution.py:32
  354.0 1.4 reduce_sum.38
  355.9 20.5 %all_to_all.64 = f32[32,1,4096]{2,1,0:T(1,128)S(1)} all-to-all(f32[32,1,4096]{2,1,0:T(1,128)S(1)} %broadcast_in_dim.15), channel_id=1, replica_groups=mesh['cores'=4,'row'=32,'tensor'=2] {'row'}, dimensions={0} | all-to-all | bytes 1048576 | tf_op jit(solution)/shard_map/all_to_all | solution.py:51
  377.2 1.4 slice_reduce_fusion.1
  378.6 1.7 reshape.199
  380.3 1.7 broadcast_select_fusion.1
  382.0 4.8 collective-permute-start.7
  386.8 9.3 %conditional.13 = (f32[256,256]{0,1:T(8,128)}, f32[4,256,256]{2,1,0:T(8,128)}) conditional(s32[]{:T(128)} %convert_element_type.17, (f32[256,256]{1,0:T(8,128)}) %tuple.250, (f32[32,1,4096]{2,1,0:T(1,128)}, f32[4,256,256]{1,2,0:T(8,128)S(1)}) %tuple.247), branch_computations={%region_17.20_spmd, %region_18.21_spmd} | conditional | flops 655245568 | bytes 18614600 | solution.py:141
  386.8 1.8 copy.118
  397.2 13.5 %collective-permute-start.6 = (f32[256,256]{1,0:T(8,128)S(1)}, f32[256,256]{1,0:T(8,128)S(1)}, u32[]{:S(2)}, u32[]{:S(2)}) collective-permute-start(f32[256,256]{1,0:T(8,128)S(1)} %copy.93), channel_id=1, source_target_pairs={{0,64},{64,128},{128,192},{1,65},{65,129},{129,193},{2,66},{66,130... | collective-permute-start | bytes 786440 | tf_op jit(solution)/shard_map/ppermute | solution.py:22
  411.5 2.5 collective-permute-done.6
  417.2 21.0 %all_to_all.65 = f32[32,1,4096]{2,1,0:T(1,128)S(1)} all-to-all(f32[32,1,4096]{2,1,0:T(1,128)S(1)} %all_to_all.49), channel_id=1, replica_groups=mesh['cores'=4,'row'=32,'tensor'=2] {'row'}, dimensions={0} | all-to-all | bytes 1048576 | tf_op jit(solution)/shard_map/all_to_all | solution.py:32
  439.0 19.4 %all_to_all.66 = f32[32,1,4096]{2,1,0:T(1,128)S(1)} all-to-all(f32[32,1,4096]{2,1,0:T(1,128)S(1)} %broadcast_in_dim.16), channel_id=1, replica_groups=mesh['cores'=4,'row'=32,'tensor'=2] {'row'}, dimensions={0} | all-to-all | bytes 1048576 | tf_op jit(solution)/shard_map/all_to_all | solution.py:51
  461.7 1.7 conditional.15
  464.1 2.5 multiply_bitcast_fusion
  466.6 98.7 %all-gather.7.cloned.1.call-done = f32[1024,256]{1,0:T(8,128)} async-done(((f32[256,256]{1,0:T(8,128)}), f32[1024,256]{1,0:T(8,128)}) %all-gather.7.cloned.1.call-update) | async-done | bytes 1048592 | tf_op jit(solution)/shard_map/all_gather | solution.py:73
  566.8 64.9 %all-gather.5.cloned.1.call-done = f32[1024,256]{0,1:T(8,128)} async-done(((f32[256,256]{0,1:T(8,128)}), f32[1024,256]{0,1:T(8,128)}) %all-gather.5.cloned.1.call-update) | async-done | bytes 1048592 | tf_op jit(solution)/shard_map/all_gather | solution.py:73
  (115 shorter events, 43.1 us)
Async XLA Ops:
  7.2 10.0 %copy-start = (f32[1,1,4,256,256]{4,3,2,1,0:T(8,128)S(1)}, f32[1,1,4,256,256]{4,3,2,1,0:T(8,128)}, u32[]{:S(2)}) copy-start(f32[1,1,4,256,256]{4,3,2,1,0:T(8,128)} %param.21) | copy-start | bytes 3145732
  7.2 5.0 copy-start.9
  8.8 8.4 %collective-permute-start = (f32[1,1,4,256,256]{3,4,2,1,0:T(8,128)S(1)}, f32[1,1,4,256,256]{3,4,2,1,0:T(8,128)S(1)}, u32[]{:S(2)}, u32[]{:S(2)}) collective-permute-start(f32[1,1,4,256,256]{3,4,2,1,0:T(8,128)S(1)} %copy.81), channel_id=1, source_target_pairs={{0,1},{1,0},{2,3},{3,2},{4,5},{5,4},{6,7},{7,6},{8,9},{9,8},{10,11... | collective-permute-start | bytes 3145736 | tf_op jit(solution)/shard_map/ppermute | solution.py:16
  12.2 2.8 collective-permute-start.1
  19.0 1.7 copy-start.1
  24.4 5.2 copy-start.2
  59.9 20.4 %all-to-all-start.1 = ((f32[32,1,4096]{2,1,0:T(1,128)}), f32[32,1,4096]{2,1,0:T(1,128)}, u32[]{:S(2)}, u32[]{:S(2)}) async-start(f32[32,1,4096]{2,1,0:T(1,128)} %broadcast_in_dim.13), calls=%async_computation.1 | async-start | bytes 1048576 | tf_op jit(solution)/shard_map/all_to_all | solution.py:51
  65.1 500.1 %all-gather.7.cloned.1.call-start = ((), (), s32[]{:S(2)}) async-start(), calls=%async_computation.9 | async-start | bytes 1310720 | tf_op jit(solution)/shard_map/all_gather | solution.py:73
  87.1 0.7 copy-start.24
  110.0 1.0 copy-start.25
  110.0 1.0 copy-start.30
  134.1 0.7 copy-start.33
  161.0 5.9 collective-permute-start.2
  164.6 1.0 copy-start.10
  165.6 7.4 %collective-permute-start.3 = (f32[256,256]{1,0:T(8,128)S(1)}, f32[256,256]{1,0:T(8,128)S(1)}, u32[]{:S(2)}, u32[]{:S(2)}) collective-permute-start(f32[256,256]{1,0:T(8,128)S(1)} %broadcast_select_fusion.3), channel_id=1, source_target_pairs={{0,64},{64,128},{128,192},{1,65},{65,129},{129,193},{2,66},{66,130... | collective-permute-start | bytes 786440 | tf_op jit(solution)/shard_map/ppermute | solution.py:22
  167.0 6.8 %copy-start.17 = (f32[256,256]{1,0:T(8,128)}, f32[256,256]{1,0:T(8,128)S(1)}, u32[]{:S(2)}) copy-start(f32[256,256]{1,0:T(8,128)S(1)} %broadcast_select_fusion.5) | copy-start | bytes 786436
  221.4 0.8 copy-start.13
  226.9 97.9 %collective-permute-start.5 = (f32[256,256]{1,0:T(8,128)}, f32[256,256]{1,0:T(8,128)}, u32[]{:S(2)}, u32[]{:S(2)}) collective-permute-start(f32[256,256]{1,0:T(8,128)} %broadcast_select_fusion.2), channel_id=1, source_target_pairs={{0,64},{64,128},{128,192},{1,65},{65,129},{129,193},{2,66},{66,130... | collective-permute-start | bytes 786440 | tf_op jit(solution)/shard_map/ppermute | solution.py:22
  252.2 72.6 %copy-start.11 = (f32[256,256]{1,0:T(8,128)S(1)}, f32[256,256]{1,0:T(8,128)}, u32[]{:S(2)}) copy-start(f32[256,256]{1,0:T(8,128)} %fusion.52) | copy-start | bytes 786436
  253.3 74.7 %collective-permute-start.4 = (f32[256,256]{1,0:T(8,128)S(1)}, f32[256,256]{1,0:T(8,128)S(1)}, u32[]{:S(2)}, u32[]{:S(2)}) collective-permute-start(f32[256,256]{1,0:T(8,128)S(1)} %copy.89), channel_id=1, source_target_pairs={{0,64},{64,128},{128,192},{1,65},{65,129},{129,193},{2,66},{66,130... | collective-permute-start | bytes 786440 | tf_op jit(solution)/shard_map/ppermute | solution.py:22
  328.1 0.7 copy-start.18
  376.4 0.8 copy-start.14
  382.0 28.8 %collective-permute-start.7 = (f32[256,256]{1,0:T(8,128)}, f32[256,256]{1,0:T(8,128)}, u32[]{:S(2)}, u32[]{:S(2)}) collective-permute-start(f32[256,256]{1,0:T(8,128)} %broadcast_select_fusion.1), channel_id=1, source_target_pairs={{0,64},{64,128},{128,192},{1,65},{65,129},{129,193},{2,66},{66,130... | collective-permute-start | bytes 786440 | tf_op jit(solution)/shard_map/ppermute | solution.py:22
  396.1 14.7 %copy-start.12 = (f32[256,256]{1,0:T(8,128)S(1)}, f32[256,256]{1,0:T(8,128)}, u32[]{:S(2)}) copy-start(f32[256,256]{1,0:T(8,128)} %fusion.52) | copy-start | bytes 786436
  397.2 16.8 %collective-permute-start.6 = (f32[256,256]{1,0:T(8,128)S(1)}, f32[256,256]{1,0:T(8,128)S(1)}, u32[]{:S(2)}, u32[]{:S(2)}) collective-permute-start(f32[256,256]{1,0:T(8,128)S(1)} %copy.93), channel_id=1, source_target_pairs={{0,64},{64,128},{128,192},{1,65},{65,129},{129,193},{2,66},{66,130... | collective-permute-start | bytes 786440 | tf_op jit(solution)/shard_map/ppermute | solution.py:22
  414.1 0.7 copy-start.15
  459.0 1.0 copy-start.19
  460.7 0.9 copy-start.16
  460.7 170.9 %all-gather.5.cloned.1.call-start = ((), (), s32[]{:S(2)}) async-start(), calls=%async_computation.8 | async-start | bytes 1310720 | tf_op jit(solution)/shard_map/all_gather | solution.py:73
  463.3 0.7 copy-start.22
  565.2 0.9 slice-start.1
  631.7 0.9 slice-start
Sparse Core Ops, SparseCore 0:
  460.9 104.3 all-gather.6
  567.0 64.5 all-gather.4
where the time goes:
time: 650 us; the launch traced here: 641 us
  waiting for transfers between devices  192 us (30%)
  blocking collectives  151 us (23%)
  starting transfers between devices  118 us (18%)
  other arithmetic  76.4 us (12%)
  local copies, waits for them, and re-layouts  58.4 us (9%)
  loops' own time  16.5 us (3%)
  between operations  14.9 us (2%)
  matrix products  13.3 us (2%)
    all_gather x2, waiting for transfers between devices, picked(): lax.all_gather(x, axis)  164 us
    ppermute x6, starting transfers between devices, passed_along(): lax.ppermute(value, axis, [(source, source + steps) for source in range(f...  109 us
    all_to_all x4, blocking collectives, sent_and_summed(): lax.all_to_all(tiles, axis, split_axis=0, concat_axis=0, tiled=True)  90.6 us
    all_to_all x3, blocking collectives, copy_for_each(): lax.all_to_all(jnp.broadcast_to(x[None], (length, *x.shape)), axis, 0, 0,...  60.8 us
    another operation x6, other arithmetic, make_frame(): lower = jnp.linalg.cholesky(gram_matrix)  35.2 us
    another operation x4, other arithmetic, make_frame(): lax.linalg.triangular_solve(lower, flat.T, left_side=True, lower=True)  22.3 us
    another operation x4, loops' own time, shards(): lax.cond(active, busy_frame, quiet_frame, (mixed_gram, gram_matrix, upper))  16.4 us
    all_to_all x1, waiting for transfers between devices, copy_for_each(): lax.all_to_all(jnp.broadcast_to(x[None], (length, *x.shape)), axis, 0, 0,...  15.2 us
  transfers between devices with their start and end apart: 11, of which 7 were waited for; matrix products, arithmetic and copies ran while one was open for 3% of the time, Pallas kernels for 0%

commit v1 on v0

v1 whole, which is shorter than its diff:
```python
import functools

import jax
import jax.numpy as jnp
from jax import lax
from jax.experimental import pallas as pl
from jax.experimental.pallas import tpu as pltpu
from jax.sharding import PartitionSpec as P

MODE = 128
BLOCK = 32
VMEM_LIMIT = 48 * 1024 * 1024
F32 = jnp.float32
BF16 = jnp.bfloat16

VMEM = pl.BlockSpec(memory_space=pltpu.VMEM)
SMEM = pl.BlockSpec(memory_space=pltpu.SMEM)


def call(body, outs, in_specs, scratch=()):
    return pl.pallas_call(
        body,
        out_shape=[jax.ShapeDtypeStruct(s, d) for s, d in outs],
        in_specs=in_specs,
        out_specs=[VMEM] * len(outs),
        scratch_shapes=list(scratch),
        compiler_params=pltpu.CompilerParams(vmem_limit_bytes=VMEM_LIMIT),
    )


def split(x):
    hi = x.astype(BF16)
    return hi, (x - hi.astype(F32)).astype(BF16)


def dot(a, b, dims=((1,), (0,))):
    return lax.dot_general(a, b, (dims, ((), ())), preferred_element_type=F32)


def dot3(a, b, dims=((1,), (0,))):
    (ah, al), (bh, bl) = a, b
    return dot(ah, bh, dims) + (dot(ah, bl, dims) + dot(al, bh, dims))


def full(a, b, dims=((1,), (0,))):
    return lax.dot_general(
        a, b, (dims, ((), ())), precision=lax.Precision.HIGHEST, preferred_element_type=F32
    )


def prepare(which, own, other, up, up_other, ch, cl, th, tl, lh, ll, rh, rl, start, beside):
    first = which[0] == 0
    modes, rank = own.shape[0], own.shape[1]
    half = rank // 2
    for i in range(modes):
        at = pl.ds(i * rank, rank)
        at_half = pl.ds(i * half, half)
        mine = own[i]
        theirs = other[i]
        ch[:, at], cl[:, at] = split(mine)
        th[:, at], tl[:, at] = split(mine.T)
        lh[:, at], ll[:, at] = split(jnp.where(first, mine, theirs).T)
        rh[:, at_half], rl[:, at_half] = split(
            jnp.where(first, theirs[:, :half], mine[:, half:])
        )
    u, v = up[...], up_other[...]
    start[:, :rank] = full(u, u, ((0,), (0,)))
    link = full(jnp.where(first, u, v), jnp.where(first, v, u), ((0,), (0,)))
    start[:, rank:] = jnp.where(first, link[:, :half], link[:, half:])
    beside[...] = jnp.where(first, link[:, half:], link[:, :half])


def chain(which, state, beside, ch, cl, th, tl, lh, ll, rh, rl, out):
    first = which[0] == 0
    rank = ch.shape[0]
    half = rank // 2
    modes = ch.shape[1] // rank
    gram = split(state[:, :rank])
    mine, theirs = state[:, rank:], beside[...]
    link = split(
        jnp.concatenate(
            [jnp.where(first, mine, theirs), jnp.where(first, theirs, mine)], axis=1
        )
    )
    total = jnp.zeros((rank, rank), F32)
    total_link = jnp.zeros((rank, half), F32)
    for i in range(modes):
        at = pl.ds(i * rank, rank)
        at_half = pl.ds(i * half, half)
        middle = split(dot3(gram, (ch[:, at], cl[:, at])))
        total += dot3((th[:, at], tl[:, at]), middle)
        middle = split(dot3(link, (rh[:, at_half], rl[:, at_half])))
        total_link += dot3((lh[:, at], ll[:, at]), middle)
    out[:, :rank] = total
    out[:, rank:] = total_link


def factor(active, gram, u_before, x_before, u_out, x_out, work):
    rank = gram.shape[0]

    @pl.when(active[0] == 0)
    def _():
        u_out[...] = u_before[...]
        x_out[...] = x_before[...]

    @pl.when(active[0] != 0)
    def _():
        rows_all = lax.broadcasted_iota(jnp.int32, (rank, rank), 0)
        cols_all = lax.broadcasted_iota(jnp.int32, (rank, rank), 1)
        work[:, :rank] = gram[:, :rank]
        work[:, rank:] = jnp.where(rows_all == cols_all, 1.0, 0.0).astype(F32)
        rows = lax.broadcasted_iota(jnp.int32, (BLOCK, 128), 0)
        lanes = lax.broadcasted_iota(jnp.int32, (BLOCK, 128), 1)
        for b in range(rank // BLOCK):
            r = b * BLOCK
            tile, offset = r // 128 * 128, r % 128
            m = work[r : r + BLOCK, tile : tile + 128]
            e = jnp.where(rows == lanes, 1.0, 0.0).astype(F32)
            pivots = jnp.ones((BLOCK, 128), F32)
            for j in range(BLOCK):
                column = jnp.broadcast_to(m[:, offset + j : offset + j + 1], (BLOCK, 128))
                pivots = jnp.where(rows == j, column, pivots)
                f = jnp.where(rows > j, column / column[j : j + 1, :], 0.0)
                e = e - f * e[j : j + 1, :]
                m = m - f * m[j : j + 1, :]
            x = e * (1.0 / jnp.sqrt(pivots))
            line = full(x[:, :BLOCK], work[r : r + BLOCK, :])
            upper = jnp.where(
                lax.broadcasted_iota(jnp.int32, (BLOCK, rank), 1)
                >= lax.broadcasted_iota(jnp.int32, (BLOCK, rank), 0) + r,
                line[:, :rank],
                0.0,
            )
            u_out[r : r + BLOCK, :] = upper
            x_out[r : r + BLOCK, :] = line[:, rank:]
            if r + BLOCK < rank:
                update = full(upper, line, ((0,), (0,)))
                work[r + BLOCK :, :] = work[r + BLOCK :, :] - update[r + BLOCK :, :]


def frame(scale, own, upper, inverse, out):
    u = split(upper[...])
    x = split(inverse[...] * scale)
    for i in range(own.shape[0]):
        mixed = split(dot3(u, split(own[i])))
        out[i] = dot3(mixed, x, ((1,), (1,)))


def swapped(x):
    return lax.ppermute(x, "tensor", [(0, 1), (1, 0)])


def moved(x, source, target):
    return lax.ppermute(x, "cores", [(source, target)])


def shards(cores, incoming):
    own, up = cores[0, 0], incoming[0]
    modes, rank, _ = own.shape
    half = rank // 2
    section, which = lax.axis_index("cores"), lax.axis_index("tensor")
    sections, rows = lax.axis_size("cores"), lax.axis_size("row")
    last = sections - 1
    scalar = which.astype(jnp.int32)[None]

    other, up_other = swapped(own), swapped(up)
    wide, narrow = ((rank, modes * rank), BF16), ((rank, modes * half), BF16)
    *parts, state, beside = call(
        prepare,
        [wide] * 6 + [narrow] * 2 + [((rank, rank + half), F32), ((rank, half), F32)],
        [SMEM] + [VMEM] * 4,
    )(scalar, own, other, up, up_other)

    run_chain = call(chain, [((rank, rank + half), F32)], [SMEM] + [VMEM] * 10)
    run_factor = call(
        factor,
        [((rank, rank), F32)] * 2,
        [SMEM] + [VMEM] * 3,
        [pltpu.VMEM((rank, 2 * rank), F32)],
    )
    u_now = x_now = up
    grams = []
    for tick in range(sections):
        (partial,) = run_chain(scalar, state, beside, *parts)
        tiles = partial.reshape(rows, rank // rows, rank + half)
        piece = lax.all_to_all(tiles, "row", 0, 0, tiled=True).sum(axis=0)
        if tick < last:
            piece = jnp.where(section == tick + 1, moved(piece, tick, tick + 1), piece)
        copies = jnp.broadcast_to(piece[None], tiles.shape)
        state = lax.all_to_all(copies, "row", 0, 0, tiled=True).reshape(partial.shape)
        beside = swapped(state[:, rank:])
        grams.append(state)
        if tick == last - 1:
            gram = grams[0]
            for k in range(1, last):
                gram = jnp.where(section == k, grams[k], gram)
            u_now, x_now = run_factor((section < last).astype(jnp.int32)[None], gram, u_now, x_now)
            u_before = lax.ppermute(u_now, "cores", [(k, k + 1) for k in range(last)])
            u_before = jnp.where(section == 0, up, u_before)

    mine = state[:, rank:]
    link = jnp.concatenate(
        [jnp.where(which == 0, mine, beside), jnp.where(which == 0, beside, mine)], axis=1
    )
    link = jnp.where(which == 0, link, link.T)
    u_now, x_now = run_factor((section == last).astype(jnp.int32)[None], state, u_now, x_now)
    (frames,) = call(
        functools.partial(frame, float(MODE * rank) ** 0.5), [(own.shape, F32)], [VMEM] * 3
    )(own, u_before, x_now)
    share = rank // sections

    def spread(x):
        tiles = x.reshape(sections, share, rank)
        result = tiles[last]
        for k in range(last):
            result = jnp.where(section == k, moved(tiles[k], last, k), result)
        return result

    return frames[None, None], spread(u_now)[None], spread(link)[None]


def solution(mesh):
    in_specs = (P("tensor", "cores", "row", None, None), P("tensor", None, None))
    out_specs = (
        P("tensor", "cores", "row", None, None),
        P("tensor", "cores", None),
        P("tensor", "cores", None),
    )
    return jax.shard_map(shards, mesh=mesh, in_specs=in_specs, out_specs=out_specs, check_vma=False)
```

time: 650 us -> 290 us (0.45); the launches traced: 641 us -> 289 us
  waiting for transfers between devices: 192 us -> 69.7 us
  starting transfers between devices: 118 us -> 42.6 us
  other arithmetic: 76.4 us -> 3.63 us
  Pallas kernels: 0 us -> 55.5 us
  local copies, waits for them, and re-layouts: 58.4 us -> 5.91 us
  blocking collectives: 151 us -> 111 us
  loops' own time: 16.5 us -> 0 us
  between operations: 14.9 us -> 1.04 us
  matrix products: 13.3 us -> 0 us
    all_gather x2 -> x0, waiting for transfers between devices: 164 us -> none  [picked(): lax.all_gather(x, axis)]
    ppermute x8 -> x16, starting transfers between devices: 112 us -> 33.5 us  [the longest x6 18 us: swapped(): return lax.ppermute(x, 'tensor', [(0, 1), (1, 0)])]
    another operation x10 -> x0, other arithmetic: 57.5 us -> none  [the longest x6 35.2 us: make_frame(): lower = jnp.linalg.cholesky(gram_matrix)]
    pallas_call x0 -> x8, Pallas kernels: none -> 55.5 us  [the longest x1 36.9 us: shards(): run_factor((section < last).astype(jnp.int32)[None], gram, u_now, x_now)]
    ppermute x8 -> x16, waiting for transfers between devices: 13.6 us -> 55.8 us  [the longest x9 46.2 us: moved(): return lax.ppermute(x, 'cores', [(source, target)])]
    all_to_all x7 -> x6, blocking collectives: 151 us -> 111 us  [the longest x3 58.7 us: shards(): piece = lax.all_to_all(tiles, 'row', 0, 0, tiled=True).sum(axis=0)]
    another operation x9 -> x0, loops' own time: 16.5 us -> none  [the longest x4 16.4 us: shards(): lax.cond(active, busy_frame, quiet_frame, (mixed_gram, gram_matrix, upper))]
    another operation x16 -> x0, local copies, waits for them, and re-layouts: 10.3 us -> none  [the longest x7 5.82 us: make_frame(): lax.linalg.triangular_solve(lower, flat.T, left_side=True, lower=True)]
  transfers between devices with their start and end apart: 11 -> 18, of which waited for: 7 -> 9; matrix products, arithmetic and copies ran while one was open for 3% -> 0% of each run, Pallas kernels for 0% -> 14%
where the time goes in v1:
time: 290 us; the launch traced here: 289 us
  blocking collectives  111 us (38%)
  waiting for transfers between devices  69.7 us (24%)
  Pallas kernels  55.5 us (19%)
  starting transfers between devices  42.6 us (15%)
  local copies, waits for them, and re-layouts  5.91 us (2%)
  other arithmetic  3.63 us (1%)
    all_to_all x3, blocking collectives, shards(): piece = lax.all_to_all(tiles, 'row', 0, 0, tiled=True).sum(axis=0)  58.7 us
    all_to_all x3, blocking collectives, shards(): lax.all_to_all(copies, 'row', 0, 0, tiled=True).reshape(partial.shape)  52.1 us
    ppermute x9, waiting for transfers between devices, moved(): return lax.ppermute(x, 'cores', [(source, target)])  46.2 us
    pallas_call x1, Pallas kernels, shards(): run_factor((section < last).astype(jnp.int32)[None], gram, u_now, x_now)  36.9 us
    ppermute x6, starting transfers between devices, swapped(): return lax.ppermute(x, 'tensor', [(0, 1), (1, 0)])  18 us
    all_to_all x1, waiting for transfers between devices, shards(): piece = lax.all_to_all(tiles, 'row', 0, 0, tiled=True).sum(axis=0)  13.9 us
    pallas_call x4, Pallas kernels, shards(): partial, = run_chain(scalar, state, beside, *parts)  13.8 us
    ppermute x9, starting transfers between devices, moved(): return lax.ppermute(x, 'cores', [(source, target)])  10.9 us
  transfers between devices with their start and end apart: 18, of which 9 were waited for; matrix products, arithmetic and copies ran while one was open for 0% of the time, Pallas kernels for 14%

profile of v1, /device:TPU:1, one launch (start us, length us, event | category | flops | bytes accessed | tf_op | source)
XLA Modules:
  0.0 289.2 jit_solution(10950508413992350213)
XLA Ops:
  0.6 3.3 %collective-permute-start = (f32[4,256,256]{2,1,0:T(8,128)}, f32[4,256,256]{2,1,0:T(8,128)S(1)}, u32[]{:S(2)}, u32[]{:S(2)}) collective-permute-start(f32[4,256,256]{2,1,0:T(8,128)} %bitcast.30), channel_id=1, source_target_pairs={{0,1},{1,0},{2,3},{3,2},{4,5},{5,4},{6,7},{7,6},{8,9},{9,8},{10,11... | collective-permute-start | bytes 3145736 | tf_op jit(solution)/shard_map/ppermute | solution.py:150
  4.0 0.1 collective-permute-start.1
  4.1 2.8 collective-permute-done.1.up_other
  6.8 0.0 collective-permute-done.other
  6.8 1.0 copy-done.17
  7.8 1.2 copy-done.12
  9.0 0.9 copy-done.14
  10.0 2.3 shard_map.49
  12.3 3.5 %shard_map.50 = f32[256,384]{1,0:T(8,128)S(1)} custom-call(s32[1]{0:T(128)} %bitcast.3.which, f32[256,384]{1,0:T(8,128)S(1)} %get-tuple-element.17.state, f32[256,128]{1,0:T(8,128)S(1)} %get-tuple-element.18.beside, bf16[256,1024]{1,0:T(8,128)(2,1)S(1)} %get-tuple-element.19.ch, bf16[256,1024]{1,0:T(8,128)(2,1)S(1)} %get-tuple-element.20.cl, ...), custom_call_target="tpu_custom_call" | custom-call | tf_op jit(solution)/shard_map/pallas_call | solution.py:184
  15.8 23.1 %all_to_all.40 = f32[32,8,384]{2,1,0:T(8,128)S(1)} all-to-all(f32[32,8,384]{2,1,0:T(8,128)S(1)} %bitcast.41), channel_id=1, replica_groups=mesh['cores'=4,'row'=32,'tensor'=2] {'row'}, dimensions={0} | all-to-all | bytes 786432 | tf_op jit(solution)/shard_map/all_to_all | solution.py:186
  39.0 3.1 %collective-permute-start.2 = (f32[8,384]{1,0:T(8,128)S(1)}, f32[8,384]{1,0:T(8,128)S(1)}, u32[]{:S(2)}, u32[]{:S(2)}) collective-permute-start(f32[8,384]{1,0:T(8,128)S(1)} %reduce_sum.36), channel_id=1, source_target_pairs={{0,64},{1,65},{2,66},{3,67},{4,68},{5,69},{6,70},{7,71},{8,72},{9,... | collective-permute-start | bytes 36872 | tf_op jit(solution)/shard_map/ppermute | solution.py:154
  42.1 0.8 collective-permute-done.2
  42.9 16.6 %all_to_all.41 = f32[32,8,384]{2,1,0:T(8,128)S(1)} all-to-all(f32[32,8,384]{2,1,0:T(8,128)S(1)} %broadcast_in_dim.49), channel_id=1, replica_groups=mesh['cores'=4,'row'=32,'tensor'=2] {'row'}, dimensions={0} | all-to-all | bytes 786432 | tf_op jit(solution)/shard_map/all_to_all | solution.py:190
  59.5 4.7 %collective-permute-start.3 = (f32[256,128]{1,0:T(8,128)S(1)}, f32[256,128]{1,0:T(8,128)S(1)}, u32[]{:S(2)}, u32[]{:S(2)}) collective-permute-start(f32[256,128]{1,0:T(8,128)S(1)} %slice.57), channel_id=1, source_target_pairs={{0,1},{1,0},{2,3},{3,2},{4,5},{5,4},{6,7},{7,6},{8,9},{9,8},{10,11... | collective-permute-start | bytes 393224 | tf_op jit(solution)/shard_map/ppermute | solution.py:150
  64.2 1.0 collective-permute-done.3.beside
  65.2 3.5 %shard_map.51 = f32[256,384]{1,0:T(8,128)S(1)} custom-call(s32[1]{0:T(128)} %bitcast.3.which, f32[256,384]{1,0:T(8,128)S(1)} %bitcast.25, f32[256,128]{1,0:T(8,128)S(1)} %collective-permute-done.3.beside, bf16[256,1024]{1,0:T(8,128)(2,1)S(1)} %get-tuple-element.19.ch, bf16[256,1024]{1,0:T(8,128)(2,1)S(1)} %get-tuple-element.20.cl, ...), custom_call_target="tpu_custom_call" | custom-call | tf_op jit(solution)/shard_map/pallas_call | solution.py:184
  68.7 17.8 %all_to_all.42 = f32[32,8,384]{2,1,0:T(8,128)} all-to-all(f32[32,8,384]{2,1,0:T(8,128)S(1)} %bitcast.42), channel_id=1, replica_groups=mesh['cores'=4,'row'=32,'tensor'=2] {'row'}, dimensions={0} | all-to-all | bytes 786432 | tf_op jit(solution)/shard_map/all_to_all | solution.py:186
  86.4 1.0 reduce_sum.37
  87.5 1.3 collective-permute-start.4
  88.7 0.0 collective-permute-done.4
  88.8 17.8 %all_to_all.43 = f32[32,8,384]{2,1,0:T(8,128)S(1)} all-to-all(f32[32,8,384]{2,1,0:T(8,128)S(1)} %broadcast_in_dim.50), channel_id=1, replica_groups=mesh['cores'=4,'row'=32,'tensor'=2] {'row'}, dimensions={0} | all-to-all | bytes 786432 | tf_op jit(solution)/shard_map/all_to_all | solution.py:190
  106.6 3.7 %collective-permute-start.5 = (f32[256,128]{1,0:T(8,128)S(1)}, f32[256,128]{1,0:T(8,128)S(1)}, u32[]{:S(2)}, u32[]{:S(2)}) collective-permute-start(f32[256,128]{1,0:T(8,128)S(1)} %slice.58), channel_id=1, source_target_pairs={{0,1},{1,0},{2,3},{3,2},{4,5},{5,4},{6,7},{7,6},{8,9},{9,8},{10,11... | collective-permute-start | bytes 393224 | tf_op jit(solution)/shard_map/ppermute | solution.py:150
  110.2 1.0 collective-permute-done.5.beside
  111.2 3.5 %shard_map.52 = f32[256,384]{1,0:T(8,128)S(1)} custom-call(s32[1]{0:T(128)} %bitcast.3.which, f32[256,384]{1,0:T(8,128)S(1)} %bitcast.27, f32[256,128]{1,0:T(8,128)S(1)} %collective-permute-done.5.beside, bf16[256,1024]{1,0:T(8,128)(2,1)S(1)} %get-tuple-element.19.ch, bf16[256,1024]{1,0:T(8,128)(2,1)S(1)} %get-tuple-element.20.cl, ...), custom_call_target="tpu_custom_call" | custom-call | tf_op jit(solution)/shard_map/pallas_call | solution.py:184
  114.7 17.8 %all_to_all.44 = f32[32,8,384]{2,1,0:T(8,128)} all-to-all(f32[32,8,384]{2,1,0:T(8,128)S(1)} %bitcast.43), channel_id=1, replica_groups=mesh['cores'=4,'row'=32,'tensor'=2] {'row'}, dimensions={0} | all-to-all | bytes 786432 | tf_op jit(solution)/shard_map/all_to_all | solution.py:186
  132.5 1.0 reduce_sum.38
  133.5 1.3 collective-permute-start.6
  134.8 0.0 collective-permute-done.6
  134.8 17.8 %all_to_all.45 = f32[32,8,384]{2,1,0:T(8,128)S(1)} all-to-all(f32[32,8,384]{2,1,0:T(8,128)S(1)} %broadcast_in_dim.51), channel_id=1, replica_groups=mesh['cores'=4,'row'=32,'tensor'=2] {'row'}, dimensions={0} | all-to-all | bytes 786432 | tf_op jit(solution)/shard_map/all_to_all | solution.py:190
  152.6 3.5 %collective-permute-start.8 = (f32[256,128]{1,0:T(8,128)S(1)}, f32[256,128]{1,0:T(8,128)S(1)}, u32[]{:S(2)}, u32[]{:S(2)}) collective-permute-start(f32[256,128]{1,0:T(8,128)S(1)} %slice.59), channel_id=1, source_target_pairs={{0,1},{1,0},{2,3},{3,2},{4,5},{5,4},{6,7},{7,6},{8,9},{9,8},{10,11... | collective-permute-start | bytes 393224 | tf_op jit(solution)/shard_map/ppermute | solution.py:150
  156.1 1.0 collective-permute-done.8.beside
  157.1 3.5 %shard_map.54 = f32[256,384]{1,0:T(8,128)S(1)} custom-call(s32[1]{0:T(128)} %bitcast.3.which, f32[256,384]{1,0:T(8,128)S(1)} %bitcast.29, f32[256,128]{1,0:T(8,128)S(1)} %collective-permute-done.8.beside, bf16[256,1024]{1,0:T(8,128)(2,1)S(1)} %get-tuple-element.19.ch, bf16[256,1024]{1,0:T(8,128)(2,1)S(1)} %get-tuple-element.20.cl, ...), custom_call_target="tpu_custom_call" | custom-call | tf_op jit(solution)/shard_map/pallas_call | solution.py:184
  160.6 0.8 copy-done.16
  161.3 4.0 %all-to-all-start.6 = ((f32[32,8,384]{2,1,0:T(8,128)}), f32[32,8,384]{2,1,0:T(8,128)S(1)}, u32[]{:S(2)}, u32[]{:S(2)}) async-start(f32[32,8,384]{2,1,0:T(8,128)} %bitcast.40), calls=%async_computation.6 | async-start | bytes 786432 | tf_op jit(solution)/shard_map/all_to_all | solution.py:186
  165.4 13.9 %all-to-all-done.6 = f32[32,8,384]{2,1,0:T(8,128)S(1)} async-done(((f32[32,8,384]{2,1,0:T(8,128)}), f32[32,8,384]{2,1,0:T(8,128)S(1)}, u32[]{:S(2)}, u32[]{:S(2)}) %all-to-all-start.6) | async-done | bytes 393248 | tf_op jit(solution)/shard_map/all_to_all | solution.py:186
  179.3 0.8 broadcast_in_dim.54
  180.1 5.1 %all-to-all-start.7 = ((f32[32,8,384]{2,1,0:T(8,128)}), f32[32,8,384]{2,1,0:T(8,128)S(1)}, u32[]{:S(2)}, u32[]{:S(2)}) async-start(f32[32,8,384]{2,1,0:T(8,128)} %broadcast_in_dim.54), calls=%async_computation.7 | async-start | bytes 786432 | tf_op jit(solution)/shard_map/all_to_all | solution.py:190
  185.2 0.0 copy-start.15
  185.2 0.1 select_select_fusion.gram
  185.3 0.9 copy-done.15
  186.2 36.9 %shard_map.53 = (f32[256,256]{1,0:T(8,128)S(1)}, f32[256,256]{1,0:T(8,128)S(1)}) custom-call(s32[1]{0:T(128)} %bitcast.2.active, f32[256,384]{1,0:T(8,128)S(1)} %select_select_fusion.gram, f32[256,256]{1,0:T(8,128)S(1)} %bitcast.35, f32[256,256]{1,0:T(8,128)S(1)} %bitcast.36), custom_call_target="tpu_custom_call" | custom-call | tf_op jit(solution)/shard_map/pallas_call | solution.py:197
  223.1 4.7 %collective-permute-start.7 = (f32[256,256]{1,0:T(8,128)S(1)}, f32[256,256]{1,0:T(8,128)S(1)}, u32[]{:S(2)}, u32[]{:S(2)}) collective-permute-start(f32[256,256]{1,0:T(8,128)S(1)} %get-tuple-element.27.u_before), channel_id=1, source_target_pairs={{0,64},{64,128},{128,192},{1,65},{65,129},{129,193},{2,66},{66,130... | collective-permute-start | bytes 786440 | tf_op jit(solution)/shard_map/ppermute | solution.py:198
  227.7 0.0 copy-start.13
  227.8 3.8 %collective-permute-done.7 = f32[256,256]{1,0:T(8,128)S(1)} collective-permute-done((f32[256,256]{1,0:T(8,128)S(1)}, f32[256,256]{1,0:T(8,128)S(1)}, u32[]{:S(2)}, u32[]{:S(2)}) %collective-permute-start.7) | collective-permute-done | bytes 262176 | tf_op jit(solution)/shard_map/ppermute | solution.py:198
  231.6 0.0 all-to-all-done.7
  231.7 2.7 collective-permute-start.12
  234.4 0.3 shard_map.55
  234.7 0.7 collective-permute-start.10
  235.4 1.3 collective-permute-start.11
  236.7 0.7 collective-permute-start.9
  237.4 2.2 shard_map.56
  239.5 0.0 collective-permute-done.12
  239.6 0.1 copy.5
  239.8 0.7 collective-permute-start.13
  240.5 0.7 collective-permute-start.14
  241.2 0.0 collective-permute-done.10
  241.2 1.3 collective-permute-start.15
  242.5 38.4 %collective-permute-done.11 = f32[64,256]{1,0:T(8,128)S(1)} collective-permute-done((f32[64,256]{1,0:T(8,128)S(1)}, f32[64,256]{1,0:T(8,128)S(1)}, u32[]{:S(2)}, u32[]{:S(2)}) %collective-permute-start.11) | collective-permute-done | bytes 65568 | tf_op jit(solution)/shard_map/ppermute | solution.py:154
  280.9 0.0 collective-permute-done.9
  280.9 0.6 select_bitcast_fusion
  281.5 0.0 collective-permute-done.13
  281.5 0.0 collective-permute-done.14
  281.5 7.0 %collective-permute-done.15 = f32[64,256]{1,0:T(8,128)S(1)} collective-permute-done((f32[64,256]{1,0:T(8,128)S(1)}, f32[64,256]{1,0:T(8,128)S(1)}, u32[]{:S(2)}, u32[]{:S(2)}) %collective-permute-start.15) | collective-permute-done | bytes 65568 | tf_op jit(solution)/shard_map/ppermute | solution.py:154
  288.5 0.6 fusion.2
  (47 shorter events, 0.4 us)
Async XLA Ops:
  0.6 6.2 %collective-permute-start = (f32[4,256,256]{2,1,0:T(8,128)}, f32[4,256,256]{2,1,0:T(8,128)S(1)}, u32[]{:S(2)}, u32[]{:S(2)}) collective-permute-start(f32[4,256,256]{2,1,0:T(8,128)} %bitcast.30), channel_id=1, source_target_pairs={{0,1},{1,0},{2,3},{3,2},{4,5},{5,4},{6,7},{7,6},{8,9},{9,8},{10,11... | collective-permute-start | bytes 3145736 | tf_op jit(solution)/shard_map/ppermute | solution.py:150
  4.0 2.9 collective-permute-start.1
  6.8 1.0 copy-start.17
  7.8 1.2 copy-start.12
  9.0 0.9 copy-start.14
  12.3 3.5 %copy-start.4 = (bf16[256,512]{1,0:T(8,128)(2,1)}, bf16[256,512]{1,0:T(8,128)(2,1)S(1)}, u32[]{:S(2)}) copy-start(bf16[256,512]{1,0:T(8,128)(2,1)S(1)} %get-tuple-element.25.rh) | copy-start | bytes 786436
  12.3 3.5 %copy-start.8 = (bf16[256,512]{1,0:T(8,128)(2,1)}, bf16[256,512]{1,0:T(8,128)(2,1)S(1)}, u32[]{:S(2)}) copy-start(bf16[256,512]{1,0:T(8,128)(2,1)S(1)} %get-tuple-element.26.rl) | copy-start | bytes 786436
  39.0 3.9 %collective-permute-start.2 = (f32[8,384]{1,0:T(8,128)S(1)}, f32[8,384]{1,0:T(8,128)S(1)}, u32[]{:S(2)}, u32[]{:S(2)}) collective-permute-start(f32[8,384]{1,0:T(8,128)S(1)} %reduce_sum.36), channel_id=1, source_target_pairs={{0,64},{1,65},{2,66},{3,67},{4,68},{5,69},{6,70},{7,71},{8,72},{9,... | collective-permute-start | bytes 36872 | tf_op jit(solution)/shard_map/ppermute | solution.py:154
  42.9 22.3 %copy-start.9 = (bf16[256,512]{1,0:T(8,128)(2,1)S(1)}, bf16[256,512]{1,0:T(8,128)(2,1)}, u32[]{:S(2)}) copy-start(bf16[256,512]{1,0:T(8,128)(2,1)} %copy-done.8) | copy-start | bytes 786436
  59.5 5.7 %copy-start.5 = (bf16[256,512]{1,0:T(8,128)(2,1)S(1)}, bf16[256,512]{1,0:T(8,128)(2,1)}, u32[]{:S(2)}) copy-start(bf16[256,512]{1,0:T(8,128)(2,1)} %copy-done.4) | copy-start | bytes 786436
  59.5 5.7 %collective-permute-start.3 = (f32[256,128]{1,0:T(8,128)S(1)}, f32[256,128]{1,0:T(8,128)S(1)}, u32[]{:S(2)}, u32[]{:S(2)}) collective-permute-start(f32[256,128]{1,0:T(8,128)S(1)} %slice.57), channel_id=1, source_target_pairs={{0,1},{1,0},{2,3},{3,2},{4,5},{5,4},{6,7},{7,6},{8,9},{9,8},{10,11... | collective-permute-start | bytes 393224 | tf_op jit(solution)/shard_map/ppermute | solution.py:150
  87.5 1.3 collective-permute-start.4
  88.8 22.5 %copy-start.10 = (bf16[256,512]{1,0:T(8,128)(2,1)S(1)}, bf16[256,512]{1,0:T(8,128)(2,1)}, u32[]{:S(2)}) copy-start(bf16[256,512]{1,0:T(8,128)(2,1)} %copy-done.8) | copy-start | bytes 786436
  106.6 8.1 %copy-start = (f32[32,8,384]{2,1,0:T(8,128)}, f32[32,8,384]{2,1,0:T(8,128)S(1)}, u32[]{:S(2)}) copy-start(f32[32,8,384]{2,1,0:T(8,128)S(1)} %all_to_all.43) | copy-start | bytes 1179652
  106.6 4.7 %copy-start.6 = (bf16[256,512]{1,0:T(8,128)(2,1)S(1)}, bf16[256,512]{1,0:T(8,128)(2,1)}, u32[]{:S(2)}) copy-start(bf16[256,512]{1,0:T(8,128)(2,1)} %copy-done.4) | copy-start | bytes 786436
  106.6 4.7 %collective-permute-start.5 = (f32[256,128]{1,0:T(8,128)S(1)}, f32[256,128]{1,0:T(8,128)S(1)}, u32[]{:S(2)}, u32[]{:S(2)}) collective-permute-start(f32[256,128]{1,0:T(8,128)S(1)} %slice.58), channel_id=1, source_target_pairs={{0,1},{1,0},{2,3},{3,2},{4,5},{5,4},{6,7},{7,6},{8,9},{9,8},{10,11... | collective-permute-start | bytes 393224 | tf_op jit(solution)/shard_map/ppermute | solution.py:150
  133.5 1.3 collective-permute-start.6
  134.8 22.3 %copy-start.11 = (bf16[256,512]{1,0:T(8,128)(2,1)S(1)}, bf16[256,512]{1,0:T(8,128)(2,1)}, u32[]{:S(2)}) copy-start(bf16[256,512]{1,0:T(8,128)(2,1)} %copy-done.8) | copy-start | bytes 786436
  152.6 8.0 %copy-start.2 = (f32[32,8,384]{2,1,0:T(8,128)}, f32[32,8,384]{2,1,0:T(8,128)S(1)}, u32[]{:S(2)}) copy-start(f32[32,8,384]{2,1,0:T(8,128)S(1)} %all_to_all.45) | copy-start | bytes 1179652
  152.6 4.5 %copy-start.7 = (bf16[256,512]{1,0:T(8,128)(2,1)S(1)}, bf16[256,512]{1,0:T(8,128)(2,1)}, u32[]{:S(2)}) copy-start(bf16[256,512]{1,0:T(8,128)(2,1)} %copy-done.4) | copy-start | bytes 786436
  152.6 4.5 %collective-permute-start.8 = (f32[256,128]{1,0:T(8,128)S(1)}, f32[256,128]{1,0:T(8,128)S(1)}, u32[]{:S(2)}, u32[]{:S(2)}) collective-permute-start(f32[256,128]{1,0:T(8,128)S(1)} %slice.59), channel_id=1, source_target_pairs={{0,1},{1,0},{2,3},{3,2},{4,5},{5,4},{6,7},{7,6},{8,9},{9,8},{10,11... | collective-permute-start | bytes 393224 | tf_op jit(solution)/shard_map/ppermute | solution.py:150
  160.6 0.8 copy-start.16
  161.3 17.9 %all-to-all-start.6 = ((f32[32,8,384]{2,1,0:T(8,128)}), f32[32,8,384]{2,1,0:T(8,128)S(1)}, u32[]{:S(2)}, u32[]{:S(2)}) async-start(f32[32,8,384]{2,1,0:T(8,128)} %bitcast.40), calls=%async_computation.6 | async-start | bytes 786432 | tf_op jit(solution)/shard_map/all_to_all | solution.py:186
  180.1 5.1 %copy-start.1 = (f32[32,8,384]{2,1,0:T(8,128)S(1)}, f32[32,8,384]{2,1,0:T(8,128)}, u32[]{:S(2)}) copy-start(f32[32,8,384]{2,1,0:T(8,128)} %copy-done) | copy-start | bytes 1179652
  180.1 5.1 %copy-start.3 = (f32[32,8,384]{2,1,0:T(8,128)S(1)}, f32[32,8,384]{2,1,0:T(8,128)}, u32[]{:S(2)}) copy-start(f32[32,8,384]{2,1,0:T(8,128)} %copy-done.2) | copy-start | bytes 1179652
  180.1 51.6 %all-to-all-start.7 = ((f32[32,8,384]{2,1,0:T(8,128)}), f32[32,8,384]{2,1,0:T(8,128)S(1)}, u32[]{:S(2)}, u32[]{:S(2)}) async-start(f32[32,8,384]{2,1,0:T(8,128)} %broadcast_in_dim.54), calls=%async_computation.7 | async-start | bytes 786432 | tf_op jit(solution)/shard_map/all_to_all | solution.py:190
  185.2 1.0 copy-start.15
  223.1 8.6 %collective-permute-start.7 = (f32[256,256]{1,0:T(8,128)S(1)}, f32[256,256]{1,0:T(8,128)S(1)}, u32[]{:S(2)}, u32[]{:S(2)}) collective-permute-start(f32[256,256]{1,0:T(8,128)S(1)} %get-tuple-element.27.u_before), channel_id=1, source_target_pairs={{0,64},{64,128},{128,192},{1,65},{65,129},{129,193},{2,66},{66,130... | collective-permute-start | bytes 786440 | tf_op jit(solution)/shard_map/ppermute | solution.py:198
  227.7 9.6 %copy-start.13 = (f32[1,1,4,256,256]{4,3,2,1,0:T(8,128)S(1)}, f32[1,1,4,256,256]{4,3,2,1,0:T(8,128)}, u32[]{:S(2)}) copy-start(f32[1,1,4,256,256]{4,3,2,1,0:T(8,128)} %param.2) | copy-start | bytes 3145732
  231.7 7.9 %collective-permute-start.12 = (f32[256,128]{1,0:T(8,128)S(1)}, f32[256,128]{1,0:T(8,128)S(1)}, u32[]{:S(2)}, u32[]{:S(2)}) collective-permute-start(f32[256,128]{1,0:T(8,128)S(1)} %slice.60), channel_id=1, source_target_pairs={{0,1},{1,0},{2,3},{3,2},{4,5},{5,4},{6,7},{7,6},{8,9},{9,8},{10,11... | collective-permute-start | bytes 393224 | tf_op jit(solution)/shard_map/ppermute | solution.py:150
  234.7 6.5 %collective-permute-start.10 = (f32[64,256]{1,0:T(8,128)S(1)}, f32[64,256]{1,0:T(8,128)S(1)}, u32[]{:S(2)}, u32[]{:S(2)}) collective-permute-start(f32[64,256]{1,0:T(8,128)S(1)} %get-tuple-element.37), channel_id=1, source_target_pairs={{192,64},{193,65},{194,66},{195,67},{196,68},{197,69},{198,70},{19... | collective-permute-start | bytes 196616 | tf_op jit(solution)/shard_map/ppermute | solution.py:154
  235.4 45.5 %collective-permute-start.11 = (f32[64,256]{1,0:T(8,128)S(1)}, f32[64,256]{1,0:T(8,128)S(1)}, u32[]{:S(2)}, u32[]{:S(2)}) collective-permute-start(f32[64,256]{1,0:T(8,128)S(1)} %get-tuple-element.36), channel_id=1, source_target_pairs={{192,0},{193,1},{194,2},{195,3},{196,4},{197,5},{198,6},{199,7},{2... | collective-permute-start | bytes 196616 | tf_op jit(solution)/shard_map/ppermute | solution.py:154
  236.7 44.2 %collective-permute-start.9 = (f32[64,256]{1,0:T(8,128)S(1)}, f32[64,256]{1,0:T(8,128)S(1)}, u32[]{:S(2)}, u32[]{:S(2)}) collective-permute-start(f32[64,256]{1,0:T(8,128)S(1)} %get-tuple-element.38), channel_id=1, source_target_pairs={{192,128},{193,129},{194,130},{195,131},{196,132},{197,133},{198,1... | collective-permute-start | bytes 196616 | tf_op jit(solution)/shard_map/ppermute | solution.py:154
  239.8 41.7 %collective-permute-start.13 = (f32[64,256]{1,0:T(8,128)S(1)}, f32[64,256]{1,0:T(8,128)S(1)}, u32[]{:S(2)}, u32[]{:S(2)}) collective-permute-start(f32[64,256]{1,0:T(8,128)S(1)} %get-tuple-element.35), channel_id=1, source_target_pairs={{192,128},{193,129},{194,130},{195,131},{196,132},{197,133},{198,1... | collective-permute-start | bytes 196616 | tf_op jit(solution)/shard_map/ppermute | solution.py:154
  240.5 41.0 %collective-permute-start.14 = (f32[64,256]{1,0:T(8,128)S(1)}, f32[64,256]{1,0:T(8,128)S(1)}, u32[]{:S(2)}, u32[]{:S(2)}) collective-permute-start(f32[64,256]{1,0:T(8,128)S(1)} %get-tuple-element.34), channel_id=1, source_target_pairs={{192,64},{193,65},{194,66},{195,67},{196,68},{197,69},{198,70},{19... | collective-permute-start | bytes 196616 | tf_op jit(solution)/shard_map/ppermute | solution.py:154
  241.2 47.4 %collective-permute-start.15 = (f32[64,256]{1,0:T(8,128)S(1)}, f32[64,256]{1,0:T(8,128)S(1)}, u32[]{:S(2)}, u32[]{:S(2)}) collective-permute-start(f32[64,256]{1,0:T(8,128)S(1)} %get-tuple-element.33), channel_id=1, source_target_pairs={{192,0},{193,1},{194,2},{195,3},{196,4},{197,5},{198,6},{199,7},{2... | collective-permute-start | bytes 196616 | tf_op jit(solution)/shard_map/ppermute | solution.py:154

commit v2 on v1

v2 whole, which is shorter than its diff:
```python
import functools

import jax
import jax.numpy as jnp
from jax import lax
from jax.experimental import pallas as pl
from jax.experimental.pallas import tpu as pltpu
from jax.sharding import PartitionSpec as P

MODE = 128
LANES = 128
BLOCK = 64
GROUP = 8
VMEM_LIMIT = 48 * 1024 * 1024
F32 = jnp.float32
BF16 = jnp.bfloat16

VMEM = pl.BlockSpec(memory_space=pltpu.VMEM)
SMEM = pl.BlockSpec(memory_space=pltpu.SMEM)


def call(body, outs, in_specs, scratch=()):
    return pl.pallas_call(
        body,
        out_shape=[jax.ShapeDtypeStruct(s, d) for s, d in outs],
        in_specs=in_specs,
        out_specs=[VMEM] * len(outs),
        scratch_shapes=list(scratch),
        compiler_params=pltpu.CompilerParams(vmem_limit_bytes=VMEM_LIMIT),
    )


def split(x):
    hi = x.astype(BF16)
    return hi, (x - hi.astype(F32)).astype(BF16)


def dot(a, b, dims=((1,), (0,))):
    return lax.dot_general(a, b, (dims, ((), ())), preferred_element_type=F32)


def dot3(a, b, dims=((1,), (0,))):
    (ah, al), (bh, bl) = a, b
    return dot(ah, bh, dims) + (dot(ah, bl, dims) + dot(al, bh, dims))


def full(a, b, dims=((1,), (0,))):
    return lax.dot_general(
        a, b, (dims, ((), ())), precision=lax.Precision.HIGHEST, preferred_element_type=F32
    )


def pack_gram(out, gram):
    half = gram.shape[0] // 2
    out[0:half, :] = gram[:half, :half]
    out[half : 2 * half, :] = gram[:half, half:]
    out[2 * half : 3 * half, :] = gram[half:, half:]


def gram_blocks(state):
    half = LANES
    return state[0:half, :], state[half : 2 * half, :], state[2 * half : 3 * half, :]


def whole_link(first, mine, theirs):
    return jnp.concatenate(
        [jnp.where(first, mine, theirs), jnp.where(first, theirs, mine)], axis=1
    )


def prepare_own(own, ch, cl, th, tl):
    modes, rank = own.shape[0], own.shape[1]
    for i in range(modes):
        at = pl.ds(i * rank, rank)
        mine = own[i]
        ch[:, at], cl[:, at] = split(mine)
        th[:, at], tl[:, at] = split(mine.T)


def prepare_link(which, own, other, th, tl, up, up_other, lh, ll, rh, rl, start, beside):
    modes, rank = own.shape[0], own.shape[1]
    half = rank // 2
    u, v = up[...], up_other[...]
    pack_gram(start, full(u, u, ((0,), (0,))))

    def sides(left, right, mine, theirs):
        link = full(left, right, ((0,), (0,)))
        start[3 * half :, :] = link[:, mine]
        beside[...] = link[:, theirs]

    low, high = slice(0, half), slice(half, rank)

    @pl.when(which[0] == 0)
    def _():
        lh[...] = th[...]
        ll[...] = tl[...]
        for i in range(modes):
            at = pl.ds(i * half, half)
            rh[:, at], rl[:, at] = split(other[i][:, low])
        sides(u, v, low, high)

    @pl.when(which[0] != 0)
    def _():
        for i in range(modes):
            at = pl.ds(i * half, half)
            rh[:, at], rl[:, at] = split(own[i][:, high])
            at = pl.ds(i * rank, rank)
            lh[:, at], ll[:, at] = split(other[i].T)
        sides(v, u, high, low)


def stacked(x, width):
    return jnp.concatenate(
        [x[:, i : i + width] for i in range(0, x.shape[1], width)], axis=0
    )


def chain_product(middle, right, left, width):
    mh, ml = split(dot3(middle, right))
    return dot3(left, (stacked(mh, width), stacked(ml, width)))


def chain(which, state, beside, ch, cl, th, tl, lh, ll, rh, rl, out):
    rank = ch.shape[0]
    half = rank // 2
    a, b, c = gram_blocks(state)
    gram = jnp.concatenate(
        [jnp.concatenate([a, b], axis=1), jnp.concatenate([b.T, c], axis=1)], axis=0
    )
    pack_gram(out, chain_product(split(gram), (ch[...], cl[...]), (th[...], tl[...]), rank))
    link = whole_link(which[0] == 0, state[3 * half :, :], beside[...])
    out[3 * half :, :] = chain_product(
        split(link), (rh[...], rl[...]), (lh[...], ll[...]), half
    )


def eliminate(m, offset, n):
    rows = lax.broadcasted_iota(jnp.int32, (n, LANES), 0)
    lanes = lax.broadcasted_iota(jnp.int32, (n, LANES), 1)
    e = jnp.where(rows == lanes, 1.0, 0.0).astype(F32)
    done = []
    for g in range(0, n, GROUP):
        left = n - g
        at = lax.broadcasted_iota(jnp.int32, (left, LANES), 0)
        first = offset + g
        columns = [
            jnp.broadcast_to(m[:, first + k : first + k + 1], (left, LANES))
            for k in range(GROUP)
        ]
        for k in range(GROUP):
            pivot = columns[k][k : k + 1, :]
            f = jnp.where(at > k, columns[k] * (1.0 / pivot), 0.0)
            for l in range(k + 1, GROUP):
                columns[l] = columns[l] - f * columns[l][k : k + 1, :]
            root = lax.rsqrt(pivot)
            root = root * (1.5 - 0.5 * pivot * root * root)
            done.append(e[k : k + 1, :] * root)
            m = m - f * m[k : k + 1, :]
            e = e - f * e[k : k + 1, :]
        m, e = m[GROUP:], e[GROUP:]
    return jnp.concatenate(done, axis=0)


def factorize(u_out, x_out, work):
    rank = work.shape[0]
    for r in range(0, rank, BLOCK):
        tile, offset = r // LANES * LANES, r % LANES
        x = eliminate(work[r : r + BLOCK, tile : tile + LANES], offset, BLOCK)
        line = dot3(split(x[:, :BLOCK]), split(work[r : r + BLOCK, :]))
        row = lax.broadcasted_iota(jnp.int32, (BLOCK, rank), 0) + r
        column = lax.broadcasted_iota(jnp.int32, (BLOCK, rank), 1)
        upper = jnp.where(column >= row, line[:, :rank], 0.0)
        u_out[r : r + BLOCK, :rank] = upper
        x_out[r : r + BLOCK, :] = line[:, rank:]
        if r + BLOCK < rank:
            below = slice(r + BLOCK, rank)
            work[below, :] = work[below, :] - dot3(split(upper.T[below, :]), split(line))


def unpack_gram(state, work):
    rank = work.shape[0]
    half = rank // 2
    a, b, c = gram_blocks(state)
    work[:half, :half] = a
    work[:half, half:rank] = b
    work[half:, :half] = jnp.zeros_like(b)
    work[half:, half:rank] = c
    rows = lax.broadcasted_iota(jnp.int32, (rank, rank), 0)
    columns = lax.broadcasted_iota(jnp.int32, (rank, rank), 1)
    work[:, rank:] = jnp.where(rows == columns, 1.0, 0.0).astype(F32)


def factor_own(section, *refs):
    *states, u_out, x_out, work = refs
    for k, state in enumerate(states):

        @pl.when(section[0] == k)
        def _(state=state):
            unpack_gram(state, work)

    @pl.when(section[0] < len(states))
    def _():
        factorize(u_out, x_out, work)


def factor_last(flags, state, beside, x_own, both, x_out, work):
    rank = work.shape[0]

    @pl.when(flags[0] == 0)
    def _():
        x_out[...] = x_own[...]

    @pl.when(flags[0] != 0)
    def _():
        first = flags[1] == 0
        link = whole_link(first, state[3 * rank // 2 :, :], beside[...])
        both[:, rank:] = jnp.where(first, link, link.T)
        unpack_gram(state, work)
        factorize(both, x_out, work)


def frame(scale, own, upper, inverse, out):
    u = split(upper[...])
    x = split(inverse[...] * scale)
    for i in range(own.shape[0]):
        mixed = split(dot3(u, split(own[i])))
        out[i] = dot3(mixed, x, ((1,), (1,)))


def swapped(x):
    return lax.ppermute(x, "tensor", [(0, 1), (1, 0)])


def scalars(*values):
    return jnp.stack([v.astype(jnp.int32) for v in values])


def shards(cores, incoming):
    own, up = cores[0, 0], incoming[0]
    modes, rank, _ = own.shape
    half = rank // 2
    section, which = lax.axis_index("cores"), lax.axis_index("tensor")
    sections, rows = lax.axis_size("cores"), lax.axis_size("row")
    last = sections - 1

    other, up_other = swapped(own), swapped(up)
    wide, narrow = ((rank, modes * rank), BF16), ((rank, modes * half), BF16)
    packed, side = ((3 * half + rank, half), F32), ((rank, half), F32)
    square = ((rank, rank), F32)
    scratch = [pltpu.VMEM((rank, 2 * rank), F32)]
    own_parts = call(prepare_own, [wide] * 4, [VMEM])(own)
    *link_parts, state, beside = call(
        prepare_link, [wide] * 2 + [narrow] * 2 + [packed, side], [SMEM] + [VMEM] * 6
    )(scalars(which), own, other, *own_parts[2:], up, up_other)
    run_chain = call(chain, [packed], [SMEM] + [VMEM] * 10)

    def exchange(x, pair):
        if pair is None:
            return lax.all_to_all(x, "row", 0, 0, tiled=True)
        rest = [k for k in range(sections) if k not in pair]
        groups = [[k * rows + r for k in p for r in range(rows)] for p in (pair, rest)]
        return lax.all_to_all(
            x, ("cores", "row"), 0, 0, tiled=True, axis_index_groups=groups
        )

    states = []
    for tick in range(sections):
        (partial,) = run_chain(scalars(which), state, beside, *own_parts, *link_parts)
        pair = (tick, tick + 1) if tick < last else None
        count = rows * (2 if pair else 1)
        arrived = exchange(partial.reshape(count, 1, -1), pair)
        piece = arrived[:rows].sum(axis=0)
        copies = jnp.broadcast_to(piece[None], arrived.shape)
        state = exchange(copies, pair).reshape(partial.shape)
        beside = swapped(state[3 * half :])
        states.append(state)
        if tick == last - 1:
            u_own, x_own = call(
                factor_own, [square] * 2, [SMEM] + [VMEM] * last, scratch
            )(scalars(section), *states)
            state, beside, u_own, x_own = lax.optimization_barrier(
                (state, beside, u_own, x_own)
            )
            u_before = lax.ppermute(u_own, "cores", [(k, k + 1) for k in range(last)])
            u_before = jnp.where(section == 0, up, u_before)

    both, x_own = call(
        factor_last, [((rank, 2 * rank), F32), square], [SMEM] + [VMEM] * 3, scratch
    )(scalars(section == last, which), state, beside, x_own)
    share = rank // sections
    tiles = both.reshape(sections, share, 2 * rank)
    sent = [lax.ppermute(tiles[k], "cores", [(last, k)]) for k in range(last)]
    (frames,) = call(
        functools.partial(frame, float(MODE * rank) ** 0.5), [(own.shape, F32)], [VMEM] * 3
    )(own, u_before, x_own)
    result = tiles[last]
    for k in range(last):
        result = jnp.where(section == k, sent[k], result)
    return frames[None, None], result[None, :, :rank], result[None, :, rank:]


def solution(mesh):
    in_specs = (P("tensor", "cores", "row", None, None), P("tensor", None, None))
    out_specs = (
        P("tensor", "cores", "row", None, None),
        P("tensor", "cores", None),
        P("tensor", "cores", None),
    )
    return jax.shard_map(shards, mesh=mesh, in_specs=in_specs, out_specs=out_specs, check_vma=False)
```

time: 290 us -> 214 us (0.74)
  waiting for transfers between devices: 69.7 us -> 8.28 us
  blocking collectives: 111 us -> 147 us
  Pallas kernels: 55.5 us -> 20.4 us
  starting transfers between devices: 42.6 us -> 24.1 us
  local copies, waits for them, and re-layouts: 5.91 us -> 12 us
  other arithmetic: 3.63 us -> 0.59 us
    ppermute x10 -> x4, waiting for transfers between devices: 50.1 us -> 5.26 us  [the longest x3 3.09 us: shards(): sent = [lax.ppermute(tiles[k], 'cores', [(last, k)]) for k in range(last)]]
    all_to_all x6 -> x8, blocking collectives: 111 us -> 147 us  [the longest x6 114 us: exchange(): lax.all_to_all(x, ('cores', 'row'), 0, 0, tiled=True, axis_index_groups=g...]
    pallas_call x7 -> x8, Pallas kernels: 53.3 us -> 18.2 us  [the longest x1 8.36 us: shards(): call(factor_own, [square] * 2, [SMEM] + [VMEM] * last, scratch)]
    all_to_all x2 -> x0, waiting for transfers between devices: 13.9 us -> none  [the longest x1 13.9 us: shards(): piece = lax.all_to_all(tiles, 'row', 0, 0, tiled=True).sum(axis=0)]
    ppermute x10 -> x4, starting transfers between devices: 15.5 us -> 4.8 us  [the longest x3 2.76 us: shards(): sent = [lax.ppermute(tiles[k], 'cores', [(last, k)]) for k in range(last)]]
    all_to_all x2 -> x0, starting transfers between devices: 9.11 us -> none  [the longest x1 5.1 us: shards(): lax.all_to_all(copies, 'row', 0, 0, tiled=True).reshape(partial.shape)]
    unnamed x36 -> x44, local copies, waits for them, and re-layouts: 4.84 us -> 9.99 us
  transfers between devices with their start and end apart: 18 -> 10, of which waited for: 9 -> 5; matrix products, arithmetic and copies ran while one was open for 0% -> 0% of each run, Pallas kernels for 14% -> 5%
where the time goes in v2:
time: 214 us; the launch traced here: 213 us
  blocking collectives  147 us (69%)
  starting transfers between devices  24.1 us (11%)
  Pallas kernels  20.4 us (10%)
  local copies, waits for them, and re-layouts  12 us (6%)
  waiting for transfers between devices  8.28 us (4%)
    all_to_all x6, blocking collectives, exchange(): lax.all_to_all(x, ('cores', 'row'), 0, 0, tiled=True, axis_index_groups=g...  114 us
    all_to_all x2, blocking collectives, exchange(): return lax.all_to_all(x, 'row', 0, 0, tiled=True)  32.8 us
    ppermute x6, starting transfers between devices, swapped(): return lax.ppermute(x, 'tensor', [(0, 1), (1, 0)])  19.3 us
    unnamed x44, local copies, waits for them, and re-layouts  9.99 us
    pallas_call x1, Pallas kernels, shards(): call(factor_own, [square] * 2, [SMEM] + [VMEM] * last, scratch)  8.36 us
    pallas_call x4, Pallas kernels, shards(): partial, = run_chain(scalars(which), state, beside, *own_parts, *link_parts)  6.73 us
  transfers between devices with their start and end apart: 10, of which 5 were waited for; matrix products, arithmetic and copies ran while one was open for 0% of the time, Pallas kernels for 5%

profile of v2, /device:TPU:1, one launch (start us, length us, event | category | flops | bytes accessed | tf_op | source)
XLA Modules:
  0.0 212.9 jit_solution(13863858562926976227)
XLA Ops:
  0.6 3.3 %collective-permute-start = (f32[4,256,256]{2,1,0:T(8,128)}, f32[4,256,256]{2,1,0:T(8,128)}, u32[]{:S(2)}, u32[]{:S(2)}) collective-permute-start(f32[4,256,256]{2,1,0:T(8,128)} %bitcast.19), channel_id=1, source_target_pairs={{0,1},{1,0},{2,3},{3,2},{4,5},{5,4},{6,7},{7,6},{8,9},{9,8},{10,11... | collective-permute-start | bytes 3145736 | tf_op jit(solution)/shard_map/ppermute | solution.py:231
  4.0 0.1 collective-permute-start.1
  4.1 1.2 copy-done
  5.3 0.4 shard_map.49
  5.7 1.0 collective-permute-done.1.up_other
  6.7 0.7 copy-done.18
  7.4 0.0 collective-permute-done.other
  7.4 0.0 copy-done.1
  7.4 0.9 copy-done.14
  8.4 0.9 copy-done.19
  9.3 2.2 %shard_map.50 = (bf16[256,1024]{1,0:T(8,128)(2,1)S(1)}, bf16[256,1024]{1,0:T(8,128)(2,1)S(1)}, bf16[256,512]{1,0:T(8,128)(2,1)S(1)}, bf16[256,512]{1,0:T(8,128)(...) custom-call(s32[1]{0:T(128)} %bitcast.2.which, f32[4,256,256]{2,1,0:T(8,128)S(1)} %bitcast.21, ...), custom_call_target="tpu_custom_call" | custom-call | tf_op jit(solution)/shard_map/pallas_call | solution.py:252
  11.5 0.0 copy-start.2
  11.5 0.0 copy-start.4
  11.5 1.7 shard_map.51
  13.2 22.8 %all_to_all.40 = f32[64,1,1280]{2,1,0:T(1,128)S(1)} all-to-all(f32[64,1,1280]{2,1,0:T(1,128)S(1)} %bitcast.35), channel_id=1, replica_groups={{0,2,4,6,8,10,12,14,16,18,20,22,24,26,28,30,32,34,36,38,40,42,44,46,48,..., dimensions={0} | all-to-all | bytes 655360 | tf_op jit(solution)/shard_map/all_to_all | solution.py:262
  36.0 0.1 slice_reduce_fusion.2
  36.0 0.2 broadcast_in_dim.14
  36.2 18.2 %all_to_all.41 = f32[64,1,1280]{2,1,0:T(1,128)S(1)} all-to-all(f32[64,1,1280]{2,1,0:T(1,128)S(1)} %broadcast_in_dim.14), channel_id=1, replica_groups={{0,2,4,6,8,10,12,14,16,18,20,22,24,26,28,30,32,34,36,38,40,42,44,46,48,..., dimensions={0} | all-to-all | bytes 655360 | tf_op jit(solution)/shard_map/all_to_all | solution.py:262
  54.4 4.0 %collective-permute-start.2 = (f32[256,128]{1,0:T(8,128)S(1)}, f32[256,128]{1,0:T(8,128)S(1)}, u32[]{:S(2)}, u32[]{:S(2)}) collective-permute-start(f32[256,128]{1,0:T(8,128)S(1)} %slice.57), channel_id=1, source_target_pairs={{0,1},{1,0},{2,3},{3,2},{4,5},{5,4},{6,7},{7,6},{8,9},{9,8},{10,11... | collective-permute-start | bytes 393224 | tf_op jit(solution)/shard_map/ppermute | solution.py:231
  58.4 1.0 collective-permute-done.2.beside
  59.4 1.7 shard_map.52
  61.1 18.8 %all_to_all.42 = f32[64,1,1280]{2,1,0:T(1,128)S(1)} all-to-all(f32[64,1,1280]{2,1,0:T(1,128)S(1)} %bitcast.36), channel_id=1, replica_groups={{64,66,68,70,72,74,76,78,80,82,84,86,88,90,92,94,96,98,100,102,104,106,..., dimensions={0} | all-to-all | bytes 655360 | tf_op jit(solution)/shard_map/all_to_all | solution.py:262
  79.9 0.1 slice_reduce_fusion.1
  80.0 0.2 broadcast_in_dim.15
  80.2 19.3 %all_to_all.43 = f32[64,1,1280]{2,1,0:T(1,128)S(1)} all-to-all(f32[64,1,1280]{2,1,0:T(1,128)S(1)} %broadcast_in_dim.15), channel_id=1, replica_groups={{64,66,68,70,72,74,76,78,80,82,84,86,88,90,92,94,96,98,100,102,104,106,..., dimensions={0} | all-to-all | bytes 655360 | tf_op jit(solution)/shard_map/all_to_all | solution.py:262
  99.5 4.2 %collective-permute-start.3 = (f32[256,128]{1,0:T(8,128)S(1)}, f32[256,128]{1,0:T(8,128)S(1)}, u32[]{:S(2)}, u32[]{:S(2)}) collective-permute-start(f32[256,128]{1,0:T(8,128)S(1)} %slice.59), channel_id=1, source_target_pairs={{0,1},{1,0},{2,3},{3,2},{4,5},{5,4},{6,7},{7,6},{8,9},{9,8},{10,11... | collective-permute-start | bytes 393224 | tf_op jit(solution)/shard_map/ppermute | solution.py:231
  103.7 1.0 collective-permute-done.3.beside
  104.7 1.7 shard_map.53
  106.4 16.5 %all_to_all.44 = f32[64,1,1280]{2,1,0:T(1,128)S(1)} all-to-all(f32[64,1,1280]{2,1,0:T(1,128)S(1)} %bitcast.37), channel_id=1, replica_groups={{128,130,132,134,136,138,140,142,144,146,148,150,152,154,156,158,160,16..., dimensions={0} | all-to-all | bytes 655360 | tf_op jit(solution)/shard_map/all_to_all | solution.py:262
  122.9 0.1 slice_reduce_fusion
  123.0 0.2 broadcast_in_dim.16
  123.2 18.1 %all_to_all.45 = f32[64,1,1280]{2,1,0:T(1,128)S(1)} all-to-all(f32[64,1,1280]{2,1,0:T(1,128)S(1)} %broadcast_in_dim.16), channel_id=1, replica_groups={{128,130,132,134,136,138,140,142,144,146,148,150,152,154,156,158,160,16..., dimensions={0} | all-to-all | bytes 655360 | tf_op jit(solution)/shard_map/all_to_all | solution.py:262
  141.3 0.7 slice.61
  142.0 0.7 copy-done.12
  142.7 3.9 %collective-permute-start.4 = (f32[256,128]{1,0:T(8,128)}, f32[256,128]{1,0:T(8,128)S(1)}, u32[]{:S(2)}, u32[]{:S(2)}) collective-permute-start(f32[256,128]{1,0:T(8,128)} %slice.61), channel_id=1, source_target_pairs={{0,1},{1,0},{2,3},{3,2},{4,5},{5,4},{6,7},{7,6},{8,9},{9,8},{10,11... | collective-permute-start | bytes 393224 | tf_op jit(solution)/shard_map/ppermute | solution.py:231
  146.6 1.0 copy-done.9
  147.7 1.0 copy-done.11
  148.6 1.0 copy-done.13
  149.6 8.4 %shard_map.54 = (f32[256,256]{1,0:T(8,128)S(1)}, f32[256,256]{1,0:T(8,128)S(1)}) custom-call(s32[1]{0:T(128)} %bitcast.9.section, f32[640,128]{1,0:T(8,128)S(1)} %bitcast.25, f32[640,128]{1,0:T(8,128)S(1)} %bitcast.28, f32[640,128]{1,0:T(8,128)S(1)} %bitcast.30), custom_call_target="tpu_custom_call" | custom-call | tf_op jit(solution)/shard_map/pallas_call | solution.py:278
  158.0 0.7 copy-done.16
  158.7 0.7 copy-done.20
  159.4 0.0 collective-permute-done.4.beside
  159.4 1.0 copy-done.5
  160.4 1.7 shard_map.55
  162.1 17.1 %all_to_all.46 = f32[32,1,2560]{2,1,0:T(1,128)S(1)} all-to-all(f32[32,1,2560]{2,1,0:T(1,128)S(1)} %bitcast.34), channel_id=1, replica_groups=mesh['cores'=4,'row'=32,'tensor'=2] {'row'}, dimensions={0} | all-to-all | bytes 655360 | tf_op jit(solution)/shard_map/all_to_all | solution.py:259
  179.3 0.2 reduce_sum.39
  179.4 0.2 broadcast_in_dim.17
  179.6 0.0 copy-start.21
  179.6 15.7 %all_to_all.47 = f32[32,1,2560]{2,1,0:T(1,128)S(1)} all-to-all(f32[32,1,2560]{2,1,0:T(1,128)S(1)} %broadcast_in_dim.17), channel_id=1, replica_groups=mesh['cores'=4,'row'=32,'tensor'=2] {'row'}, dimensions={0} | all-to-all | bytes 655360 | tf_op jit(solution)/shard_map/all_to_all | solution.py:259
  195.4 3.8 %collective-permute-start.6 = (f32[256,128]{1,0:T(8,128)S(1)}, f32[256,128]{1,0:T(8,128)S(1)}, u32[]{:S(2)}, u32[]{:S(2)}) collective-permute-start(f32[256,128]{1,0:T(8,128)S(1)} %slice.62), channel_id=1, source_target_pairs={{0,1},{1,0},{2,3},{3,2},{4,5},{5,4},{6,7},{7,6},{8,9},{9,8},{10,11... | collective-permute-start | bytes 393224 | tf_op jit(solution)/shard_map/ppermute | solution.py:231
  199.1 2.0 collective-permute-start.5
  201.2 0.1 pad_add_fusion.flags
  201.3 0.0 collective-permute-done.6.beside
  201.3 0.6 shard_map.56
  201.8 0.0 copy-start.15
  201.9 0.8 collective-permute-start.7
  202.7 0.7 collective-permute-start.8
  203.4 1.3 collective-permute-start.9
  204.7 2.2 %collective-permute-done.5 = f32[256,256]{1,0:T(8,128)S(1)} collective-permute-done((f32[256,256]{1,0:T(8,128)S(1)}, f32[256,256]{1,0:T(8,128)S(1)}, u32[]{:S(2)}, u32[]{:S(2)}) %collective-permute-start.5) | collective-permute-done | bytes 262176 | tf_op jit(solution)/shard_map/ppermute | solution.py:284
  206.9 2.2 %shard_map.57 = f32[4,256,256]{2,1,0:T(8,128)} custom-call(f32[4,256,256]{2,1,0:T(8,128)S(1)} %bitcast.22, f32[256,256]{1,0:T(8,128)S(1)} %broadcast_select_fusion.upper, f32[256,256]{1,0:T(8,128)S(1)} %get-tuple-element.37.inverse), custom_call_target="tpu_custom_call" | custom-call | tf_op jit(solution)/shard_map/pallas_call | solution.py:293
  209.1 0.0 collective-permute-done.7
  209.1 0.0 collective-permute-done.8
  209.1 3.1 %collective-permute-done.9 = f32[64,512]{1,0:T(8,128)S(1)} collective-permute-done((f32[64,512]{1,0:T(8,128)S(1)}, f32[64,512]{1,0:T(8,128)S(1)}, u32[]{:S(2)}, u32[]{:S(2)}) %collective-permute-start.9) | collective-permute-done | bytes 131104 | tf_op jit(solution)/shard_map/ppermute | solution.py:292
  212.2 0.7 slice_bitcast_fusion
  (34 shorter events, 0.2 us)
Async XLA Ops:
  0.6 6.8 %collective-permute-start = (f32[4,256,256]{2,1,0:T(8,128)}, f32[4,256,256]{2,1,0:T(8,128)}, u32[]{:S(2)}, u32[]{:S(2)}) collective-permute-start(f32[4,256,256]{2,1,0:T(8,128)} %bitcast.19), channel_id=1, source_target_pairs={{0,1},{1,0},{2,3},{3,2},{4,5},{5,4},{6,7},{7,6},{8,9},{9,8},{10,11... | collective-permute-start | bytes 3145736 | tf_op jit(solution)/shard_map/ppermute | solution.py:231
  4.0 2.8 %collective-permute-start.1 = (f32[256,256]{1,0:T(8,128)}, f32[256,256]{1,0:T(8,128)S(1)}, u32[]{:S(2)}, u32[]{:S(2)}) collective-permute-start(f32[256,256]{1,0:T(8,128)} %bitcast.38), channel_id=1, source_target_pairs={{0,1},{1,0},{2,3},{3,2},{4,5},{5,4},{6,7},{7,6},{8,9},{9,8},{10,11... | collective-permute-start | bytes 786440 | tf_op jit(solution)/shard_map/ppermute | solution.py:231
  4.1 1.2 copy-start
  5.3 2.1 %copy-start.1 = (f32[1,1,4,256,256]{4,3,2,1,0:T(8,128)S(1)}, f32[1,1,4,256,256]{4,3,2,1,0:T(8,128)}, u32[]{:S(2)}) copy-start(f32[1,1,4,256,256]{4,3,2,1,0:T(8,128)} %param.2) | copy-start | bytes 3145732
  6.7 0.7 copy-start.18
  7.4 1.0 copy-start.14
  8.4 0.9 copy-start.19
  11.5 93.2 %copy-start.2 = (bf16[256,1024]{1,0:T(8,128)(2,1)}, bf16[256,1024]{1,0:T(8,128)(2,1)S(1)}, u32[]{:S(2)}) copy-start(bf16[256,1024]{1,0:T(8,128)(2,1)S(1)} %get-tuple-element.27.lh) | copy-start | bytes 1572868
  11.5 93.2 %copy-start.4 = (bf16[256,1024]{1,0:T(8,128)(2,1)}, bf16[256,1024]{1,0:T(8,128)(2,1)S(1)}, u32[]{:S(2)}) copy-start(bf16[256,1024]{1,0:T(8,128)(2,1)S(1)} %get-tuple-element.28.ll) | copy-start | bytes 1572868
  11.5 93.2 %copy-start.6 = (bf16[256,512]{1,0:T(8,128)(2,1)}, bf16[256,512]{1,0:T(8,128)(2,1)S(1)}, u32[]{:S(2)}) copy-start(bf16[256,512]{1,0:T(8,128)(2,1)S(1)} %get-tuple-element.30.rl) | copy-start | bytes 786436
  54.4 6.7 %copy-start.8 = (f32[64,1,1280]{2,1,0:T(1,128)}, f32[64,1,1280]{2,1,0:T(1,128)S(1)}, u32[]{:S(2)}) copy-start(f32[64,1,1280]{2,1,0:T(1,128)S(1)} %all_to_all.41) | copy-start | bytes 983044
  54.4 5.0 %collective-permute-start.2 = (f32[256,128]{1,0:T(8,128)S(1)}, f32[256,128]{1,0:T(8,128)S(1)}, u32[]{:S(2)}, u32[]{:S(2)}) collective-permute-start(f32[256,128]{1,0:T(8,128)S(1)} %slice.57), channel_id=1, source_target_pairs={{0,1},{1,0},{2,3},{3,2},{4,5},{5,4},{6,7},{7,6},{8,9},{9,8},{10,11... | collective-permute-start | bytes 393224 | tf_op jit(solution)/shard_map/ppermute | solution.py:231
  99.5 6.9 %copy-start.10 = (f32[64,1,1280]{2,1,0:T(1,128)}, f32[64,1,1280]{2,1,0:T(1,128)S(1)}, u32[]{:S(2)}) copy-start(f32[64,1,1280]{2,1,0:T(1,128)S(1)} %all_to_all.43) | copy-start | bytes 983044
  99.5 5.2 %collective-permute-start.3 = (f32[256,128]{1,0:T(8,128)S(1)}, f32[256,128]{1,0:T(8,128)S(1)}, u32[]{:S(2)}, u32[]{:S(2)}) collective-permute-start(f32[256,128]{1,0:T(8,128)S(1)} %slice.59), channel_id=1, source_target_pairs={{0,1},{1,0},{2,3},{3,2},{4,5},{5,4},{6,7},{7,6},{8,9},{9,8},{10,11... | collective-permute-start | bytes 393224 | tf_op jit(solution)/shard_map/ppermute | solution.py:231
  142.0 0.7 copy-start.12
  142.7 16.7 %collective-permute-start.4 = (f32[256,128]{1,0:T(8,128)}, f32[256,128]{1,0:T(8,128)S(1)}, u32[]{:S(2)}, u32[]{:S(2)}) collective-permute-start(f32[256,128]{1,0:T(8,128)} %slice.61), channel_id=1, source_target_pairs={{0,1},{1,0},{2,3},{3,2},{4,5},{5,4},{6,7},{7,6},{8,9},{9,8},{10,11... | collective-permute-start | bytes 393224 | tf_op jit(solution)/shard_map/ppermute | solution.py:231
  146.6 12.8 %copy-start.3 = (bf16[256,1024]{1,0:T(8,128)(2,1)S(1)}, bf16[256,1024]{1,0:T(8,128)(2,1)}, u32[]{:S(2)}) copy-start(bf16[256,1024]{1,0:T(8,128)(2,1)} %copy-done.2) | copy-start | bytes 1572868
  146.6 1.0 copy-start.9
  147.6 1.0 copy-start.11
  148.6 1.0 copy-start.13
  149.6 9.8 %copy-start.7 = (bf16[256,512]{1,0:T(8,128)(2,1)S(1)}, bf16[256,512]{1,0:T(8,128)(2,1)}, u32[]{:S(2)}) copy-start(bf16[256,512]{1,0:T(8,128)(2,1)} %copy-done.6) | copy-start | bytes 786436
  158.0 0.7 copy-start.16
  158.7 0.7 copy-start.20
  159.4 1.0 copy-start.5
  179.6 19.5 %copy-start.21 = (f32[256,256]{1,0:T(8,128)S(1)}, f32[256,256]{1,0:T(8,128)}, u32[]{:S(2)}) copy-start(f32[256,256]{1,0:T(8,128)} %copy-done.20) | copy-start | bytes 786436
  195.3 5.9 %copy-start.17 = (f32[256,256]{1,0:T(8,128)S(1)}, f32[256,256]{1,0:T(8,128)}, u32[]{:S(2)}) copy-start(f32[256,256]{1,0:T(8,128)} %copy-done.16) | copy-start | bytes 786436
  195.4 5.9 %collective-permute-start.6 = (f32[256,128]{1,0:T(8,128)S(1)}, f32[256,128]{1,0:T(8,128)S(1)}, u32[]{:S(2)}, u32[]{:S(2)}) collective-permute-start(f32[256,128]{1,0:T(8,128)S(1)} %slice.62), channel_id=1, source_target_pairs={{0,1},{1,0},{2,3},{3,2},{4,5},{5,4},{6,7},{7,6},{8,9},{9,8},{10,11... | collective-permute-start | bytes 393224 | tf_op jit(solution)/shard_map/ppermute | solution.py:231
  199.1 7.7 %collective-permute-start.5 = (f32[256,256]{1,0:T(8,128)S(1)}, f32[256,256]{1,0:T(8,128)S(1)}, u32[]{:S(2)}, u32[]{:S(2)}) collective-permute-start(f32[256,256]{1,0:T(8,128)S(1)} %copy-done.21), channel_id=1, source_target_pairs={{0,64},{64,128},{128,192},{1,65},{65,129},{129,193},{2,66},{66,130... | collective-permute-start | bytes 786440 | tf_op jit(solution)/shard_map/ppermute | solution.py:284
  201.8 5.0 %copy-start.15 = (f32[1,256,256]{2,1,0:T(8,128)S(1)}, f32[1,256,256]{2,1,0:T(8,128)}, u32[]{:S(2)}) copy-start(f32[1,256,256]{2,1,0:T(8,128)} %param.3) | copy-start | bytes 786436
  201.9 7.2 %collective-permute-start.7 = (f32[64,512]{1,0:T(8,128)S(1)}, f32[64,512]{1,0:T(8,128)S(1)}, u32[]{:S(2)}, u32[]{:S(2)}) collective-permute-start(f32[64,512]{1,0:T(8,128)S(1)} %get-tuple-element.41), channel_id=1, source_target_pairs={{192,128},{193,129},{194,130},{195,131},{196,132},{197,133},{198,1... | collective-permute-start | bytes 393224 | tf_op jit(solution)/shard_map/ppermute | solution.py:292
  202.7 6.4 %collective-permute-start.8 = (f32[64,512]{1,0:T(8,128)S(1)}, f32[64,512]{1,0:T(8,128)S(1)}, u32[]{:S(2)}, u32[]{:S(2)}) collective-permute-start(f32[64,512]{1,0:T(8,128)S(1)} %get-tuple-element.40), channel_id=1, source_target_pairs={{192,64},{193,65},{194,66},{195,67},{196,68},{197,69},{198,70},{19... | collective-permute-start | bytes 393224 | tf_op jit(solution)/shard_map/ppermute | solution.py:292
  203.4 8.8 %collective-permute-start.9 = (f32[64,512]{1,0:T(8,128)S(1)}, f32[64,512]{1,0:T(8,128)S(1)}, u32[]{:S(2)}, u32[]{:S(2)}) collective-permute-start(f32[64,512]{1,0:T(8,128)S(1)} %get-tuple-element.39), channel_id=1, source_target_pairs={{192,0},{193,1},{194,2},{195,3},{196,4},{197,5},{198,6},{199,7},{2... | collective-permute-start | bytes 393224 | tf_op jit(solution)/shard_map/ppermute | solution.py:292

commit v3 on v2

--- a/solution.py
+++ b/solution.py
@@ -11,20 +11,21 @@
 LANES = 128
 BLOCK = 64
 GROUP = 8
-VMEM_LIMIT = 48 * 1024 * 1024
+VMEM_LIMIT = 16 * 1024 * 1024
 F32 = jnp.float32
 BF16 = jnp.bfloat16
 
 VMEM = pl.BlockSpec(memory_space=pltpu.VMEM)
 SMEM = pl.BlockSpec(memory_space=pltpu.SMEM)
-
-
-def call(body, outs, in_specs, scratch=()):
+HBM = pl.BlockSpec(memory_space=pltpu.HBM)
+
+
+def call(body, outs, in_specs, scratch=(), out_spec=VMEM):
     return pl.pallas_call(
         body,
         out_shape=[jax.ShapeDtypeStruct(s, d) for s, d in outs],
         in_specs=in_specs,
-        out_specs=[VMEM] * len(outs),
+        out_specs=[out_spec] * len(outs),
         scratch_shapes=list(scratch),
         compiler_params=pltpu.CompilerParams(vmem_limit_bytes=VMEM_LIMIT),
     )
@@ -120,14 +121,25 @@
     return dot3(left, (stacked(mh, width), stacked(ml, width)))
 
 
-def chain(which, state, beside, ch, cl, th, tl, lh, ll, rh, rl, out):
+def chain_gram(state, ch, cl, th, tl, out):
     rank = ch.shape[0]
-    half = rank // 2
     a, b, c = gram_blocks(state)
     gram = jnp.concatenate(
         [jnp.concatenate([a, b], axis=1), jnp.concatenate([b.T, c], axis=1)], axis=0
     )
     pack_gram(out, chain_product(split(gram), (ch[...], cl[...]), (th[...], tl[...]), rank))
+
+
+def chain_gram_keep(tick, section, kept, state, ch, cl, th, tl, out, keep):
+    mine = section[0] == tick - 1
+    keep[...] = jnp.where(mine, state[: keep.shape[0], :], kept[...])
+    chain_gram(state, ch, cl, th, tl, out)
+
+
+def chain_link(which, gram, state, beside, lh, ll, rh, rl, out):
+    rank = lh.shape[0]
+    half = rank // 2
+    out[: 3 * half, :] = gram[...]
     link = whole_link(which[0] == 0, state[3 * half :, :], beside[...])
     out[3 * half :, :] = chain_product(
         split(link), (rh[...], rl[...]), (lh[...], ll[...]), half
@@ -190,33 +202,39 @@
     work[:, rank:] = jnp.where(rows == columns, 1.0, 0.0).astype(F32)
 
 
-def factor_own(section, *refs):
-    *states, u_out, x_out, work = refs
-    for k, state in enumerate(states):
-
-        @pl.when(section[0] == k)
-        def _(state=state):
-            unpack_gram(state, work)
-
-    @pl.when(section[0] < len(states))
-    def _():
-        factorize(u_out, x_out, work)
-
-
-def factor_last(flags, state, beside, x_own, both, x_out, work):
+def factor_own(section, kept, state, u_out, x_out, work, gram, u, x):
+    busy = section[0] < section[1]
+
+    @pl.when(busy)
+    def _():
+        pltpu.sync_copy(kept, gram)
+
+    @pl.when(section[0] == section[1] - 1)
+    def _():
+        pltpu.sync_copy(state.at[pl.ds(0, gram.shape[0])], gram)
+
+    @pl.when(busy)
+    def _():
+        unpack_gram(gram, work)
+        factorize(u, x, work)
+        pltpu.sync_copy(u, u_out)
+        pltpu.sync_copy(x, x_out)
+
+
+def factor_last(place, state, beside, x_own, tail, correlation, x_out, work, square):
     rank = work.shape[0]
-
-    @pl.when(flags[0] == 0)
+    rows = pl.ds(pl.multiple_of(place[0] * tail.shape[0], tail.shape[0]), tail.shape[0])
+    first = place[1] == 0
+    link = whole_link(first, state[3 * rank // 2 :, :], beside[...])
+    square[...] = jnp.where(first, link, link.T)
+    correlation[...] = square[rows, :]
+    unpack_gram(state, work)
+    factorize(square, x_out, work)
+    tail[...] = square[rows, :]
+
+    @pl.when(place[2] == 0)
     def _():
         x_out[...] = x_own[...]
-
-    @pl.when(flags[0] != 0)
-    def _():
-        first = flags[1] == 0
-        link = whole_link(first, state[3 * rank // 2 :, :], beside[...])
-        both[:, rank:] = jnp.where(first, link, link.T)
-        unpack_gram(state, work)
-        factorize(both, x_out, work)
 
 
 def frame(scale, own, upper, inverse, out):
@@ -232,7 +250,7 @@
 
 
 def scalars(*values):
-    return jnp.stack([v.astype(jnp.int32) for v in values])
+    return jnp.stack([jnp.asarray(v, jnp.int32) for v in values])
 
 
 def shards(cores, incoming):
@@ -252,7 +270,9 @@
     *link_parts, state, beside = call(
         prepare_link, [wide] * 2 + [narrow] * 2 + [packed, side], [SMEM] + [VMEM] * 6
     )(scalars(which), own, other, *own_parts[2:], up, up_other)
-    run_chain = call(chain, [packed], [SMEM] + [VMEM] * 10)
+    gram_shape = ((3 * half, half), F32)
+    run_gram = call(chain_gram, [gram_shape], [VMEM] * 5)
+    run_link = call(chain_link, [packed], [SMEM] + [VMEM] * 7)
 
     def exchange(x, pair):
         if pair is None:
@@ -263,40 +283,52 @@
             x, ("cores", "row"), 0, 0, tiled=True, axis_index_groups=groups
         )
 
-    states = []
+    kept = None
     for tick in range(sections):
-        (partial,) = run_chain(scalars(which), state, beside, *own_parts, *link_parts)
+        if 0 < tick < last:
+            gram, kept = call(
+                functools.partial(chain_gram_keep, tick),
+                [gram_shape] * 2,
+                [SMEM] + [VMEM] * 6,
+            )(scalars(section), kept, state, *own_parts)
+        else:
+            (gram,) = run_gram(state, *own_parts)
+            kept = gram if tick == 0 else kept
+        (partial,) = run_link(scalars(which), gram, state, beside, *link_parts)
         pair = (tick, tick + 1) if tick < last else None
         count = rows * (2 if pair else 1)
         arrived = exchange(partial.reshape(count, 1, -1), pair)
         piece = arrived[:rows].sum(axis=0)
+        if tick == last:
+            sent = [lax.ppermute(piece, "cores", [(last, k)]) for k in range(last)]
+            for k in range(last):
+                piece = jnp.where(section == k, sent[k], piece)
         copies = jnp.broadcast_to(piece[None], arrived.shape)
         state = exchange(copies, pair).reshape(partial.shape)
         beside = swapped(state[3 * half :])
-        states.append(state)
         if tick == last - 1:
             u_own, x_own = call(
-                factor_own, [square] * 2, [SMEM] + [VMEM] * last, scratch
-            )(scalars(section), *states)
-            state, beside, u_own, x_own = lax.optimization_barrier(
-                (state, beside, u_own, x_own)
-            )
+                factor_own,
+                [square] * 2,
+                [SMEM] + [HBM] * 2,
+                scratch + [pltpu.VMEM(*gram_shape)] + [pltpu.VMEM(*square)] * 2,
+                HBM,
+            )(scalars(section, last), kept, state)
+            state, u_own, x_own = lax.optimization_barrier((state, u_own, x_own))
             u_before = lax.ppermute(u_own, "cores", [(k, k + 1) for k in range(last)])
             u_before = jnp.where(section == 0, up, u_before)
 
-    both, x_own = call(
-        factor_last, [((rank, 2 * rank), F32), square], [SMEM] + [VMEM] * 3, scratch
-    )(scalars(section == last, which), state, beside, x_own)
-    share = rank // sections
-    tiles = both.reshape(sections, share, 2 * rank)
-    sent = [lax.ppermute(tiles[k], "cores", [(last, k)]) for k in range(last)]
+    share = ((rank // sections, rank), F32)
+    tail, correlation, x_own = call(
+        factor_last,
+        [share, share, square],
+        [SMEM] + [VMEM] * 3,
+        scratch + [pltpu.VMEM((rank, rank), F32)],
+    )(scalars(section, which, section == last), state, beside, x_own)
     (frames,) = call(
         functools.partial(frame, float(MODE * rank) ** 0.5), [(own.shape, F32)], [VMEM] * 3
     )(own, u_before, x_own)
-    result = tiles[last]
-    for k in range(last):
-        result = jnp.where(section == k, sent[k], result)
-    return frames[None, None], result[None, :, :rank], result[None, :, rank:]
+    return frames[None, None], tail[None], correlation[None]
 
 
 def solution(mesh):

time: 214 us -> 221 us (1.033)
  blocking collectives: 147 us -> 131 us
  Pallas kernels: 20.4 us -> 33.8 us
  waiting for transfers between devices: 8.28 us -> 16.1 us
  starting transfers between devices: 24.1 us -> 29.2 us
  local copies, waits for them, and re-layouts: 12 us -> 8.63 us
    all_to_all x2 -> x1, blocking collectives: 32.8 us -> 17.1 us  [exchange(): return lax.all_to_all(x, 'row', 0, 0, tiled=True)]
    pallas_call x6 -> x10, Pallas kernels: 15.7 us -> 29.1 us  [the longest x1 9.49 us: shards(): call(factor_last, [share, share, square], [SMEM] + [VMEM] * 3, scratch +...]
    all_to_all x0 -> x1, waiting for transfers between devices: none -> 9.28 us  [exchange(): return lax.all_to_all(x, 'row', 0, 0, tiled=True)]
    all_to_all x0 -> x1, starting transfers between devices: none -> 4.45 us  [exchange(): return lax.all_to_all(x, 'row', 0, 0, tiled=True)]
    unnamed x44 -> x42, local copies, waits for them, and re-layouts: 9.99 us -> 6.52 us
  transfers between devices with their start and end apart: 10 -> 11, of which waited for: 5 -> 4; matrix products, arithmetic and copies ran while one was open for 0% -> 0% of each run, Pallas kernels for 5% -> 7%
where the time goes in v3:
time: 221 us; the launch traced here: 220 us
  blocking collectives  131 us (59%)
  Pallas kernels  33.8 us (15%)
  starting transfers between devices  29.2 us (13%)
  waiting for transfers between devices  16.1 us (7%)
  local copies, waits for them, and re-layouts  8.63 us (4%)
    all_to_all x6, blocking collectives, exchange(): lax.all_to_all(x, ('cores', 'row'), 0, 0, tiled=True, axis_index_groups=g...  113 us
    ppermute x6, starting transfers between devices, swapped(): return lax.ppermute(x, 'tensor', [(0, 1), (1, 0)])  20.7 us
    all_to_all x1, blocking collectives, exchange(): return lax.all_to_all(x, 'row', 0, 0, tiled=True)  17.1 us
    pallas_call x1, Pallas kernels, shards(): call(factor_last, [share, share, square], [SMEM] + [VMEM] * 3, scratch +...  9.49 us
    all_to_all x1, waiting for transfers between devices, exchange(): return lax.all_to_all(x, 'row', 0, 0, tiled=True)  9.28 us
    pallas_call x1, Pallas kernels, shards(): call(factor_own, [square] * 2, [SMEM] + [HBM] * 2, scratch + [pltpu.VMEM(...  9.14 us
    unnamed x42, local copies, waits for them, and re-layouts  6.52 us
    ppermute x3, waiting for transfers between devices, shards(): sent = [lax.ppermute(piece, 'cores', [(last, k)]) for k in range(last)]  4.79 us
  transfers between devices with their start and end apart: 11, of which 4 were waited for; matrix products, arithmetic and copies ran while one was open for 0% of the time, Pallas kernels for 7%

profile of v3, /device:TPU:1, one launch (start us, length us, event | category | flops | bytes accessed | tf_op | source)
XLA Modules:
  0.0 220.0 jit_solution(1725966685394666837)
XLA Ops:
  0.6 3.3 %collective-permute-start = (f32[4,256,256]{2,1,0:T(8,128)}, f32[4,256,256]{2,1,0:T(8,128)}, u32[]{:S(2)}, u32[]{:S(2)}) collective-permute-start(f32[4,256,256]{2,1,0:T(8,128)} %bitcast.17), channel_id=1, source_target_pairs={{0,1},{1,0},{2,3},{3,2},{4,5},{5,4},{6,7},{7,6},{8,9},{9,8},{10,11... | collective-permute-start | bytes 3145736 | tf_op jit(solution)/shard_map/ppermute | solution.py:249
  4.0 0.1 collective-permute-start.1
  4.1 1.2 copy-done
  5.3 0.4 shard_map.49
  5.7 1.0 collective-permute-done.1.up_other
  6.7 0.7 copy-done.17
  7.4 0.0 collective-permute-done.other
  7.4 0.9 copy-done.13
  8.4 0.9 copy-done.18
  9.3 2.2 shard_map.50
  11.5 0.0 copy-start.2
  11.5 1.7 shard_map.51.gram.kept
  13.2 0.0 copy-start.11
  13.2 0.0 copy-done.2
  13.3 0.9 shard_map.52
  14.2 22.8 %all_to_all.40 = f32[64,1,1280]{2,1,0:T(1,128)S(1)} all-to-all(f32[64,1,1280]{2,1,0:T(1,128)S(1)} %bitcast.36), channel_id=1, replica_groups={{0,2,4,6,8,10,12,14,16,18,20,22,24,26,28,30,32,34,36,38,40,42,44,46,48,..., dimensions={0} | all-to-all | bytes 655360 | tf_op jit(solution)/shard_map/all_to_all | solution.py:282
  36.9 0.1 slice_reduce_fusion.2
  37.0 0.2 broadcast_in_dim.16
  37.2 18.2 %all_to_all.41 = f32[64,1,1280]{2,1,0:T(1,128)S(1)} all-to-all(f32[64,1,1280]{2,1,0:T(1,128)S(1)} %broadcast_in_dim.16), channel_id=1, replica_groups={{0,2,4,6,8,10,12,14,16,18,20,22,24,26,28,30,32,34,36,38,40,42,44,46,48,..., dimensions={0} | all-to-all | bytes 655360 | tf_op jit(solution)/shard_map/all_to_all | solution.py:282
  55.4 0.7 slice.29
  56.0 0.7 copy-done.8
  56.8 3.9 %collective-permute-start.2 = (f32[256,128]{1,0:T(8,128)}, f32[256,128]{1,0:T(8,128)S(1)}, u32[]{:S(2)}, u32[]{:S(2)}) collective-permute-start(f32[256,128]{1,0:T(8,128)} %slice.29), channel_id=1, source_target_pairs={{0,1},{1,0},{2,3},{3,2},{4,5},{5,4},{6,7},{7,6},{8,9},{9,8},{10,11... | collective-permute-start | bytes 393224 | tf_op jit(solution)/shard_map/ppermute | solution.py:249
  60.7 1.0 copy-done.9
  61.7 0.9 copy-done.12
  62.6 1.7 shard_map.53
  64.3 0.0 collective-permute-done.2.beside
  64.4 0.9 shard_map.54
  65.3 19.4 %all_to_all.42 = f32[64,1,1280]{2,1,0:T(1,128)S(1)} all-to-all(f32[64,1,1280]{2,1,0:T(1,128)S(1)} %bitcast.34), channel_id=1, replica_groups={{64,66,68,70,72,74,76,78,80,82,84,86,88,90,92,94,96,98,100,102,104,106,..., dimensions={0} | all-to-all | bytes 655360 | tf_op jit(solution)/shard_map/all_to_all | solution.py:282
  84.7 0.1 slice_reduce_fusion.1
  84.8 0.2 broadcast_in_dim.17
  84.9 18.7 %all_to_all.43 = f32[64,1,1280]{2,1,0:T(1,128)S(1)} all-to-all(f32[64,1,1280]{2,1,0:T(1,128)S(1)} %broadcast_in_dim.17), channel_id=1, replica_groups={{64,66,68,70,72,74,76,78,80,82,84,86,88,90,92,94,96,98,100,102,104,106,..., dimensions={0} | all-to-all | bytes 655360 | tf_op jit(solution)/shard_map/all_to_all | solution.py:282
  103.7 4.4 %collective-permute-start.3 = (f32[256,128]{1,0:T(8,128)S(1)}, f32[256,128]{1,0:T(8,128)S(1)}, u32[]{:S(2)}, u32[]{:S(2)}) collective-permute-start(f32[256,128]{1,0:T(8,128)S(1)} %slice.31), channel_id=1, source_target_pairs={{0,1},{1,0},{2,3},{3,2},{4,5},{5,4},{6,7},{7,6},{8,9},{9,8},{10,11... | collective-permute-start | bytes 393224 | tf_op jit(solution)/shard_map/ppermute | solution.py:249
  108.1 1.7 shard_map.55
  109.8 0.0 collective-permute-done.3.beside
  109.8 0.9 shard_map.56
  110.7 17.0 %all_to_all.44 = f32[64,1,1280]{2,1,0:T(1,128)S(1)} all-to-all(f32[64,1,1280]{2,1,0:T(1,128)S(1)} %bitcast.35), channel_id=1, replica_groups={{128,130,132,134,136,138,140,142,144,146,148,150,152,154,156,158,160,16..., dimensions={0} | all-to-all | bytes 655360 | tf_op jit(solution)/shard_map/all_to_all | solution.py:282
  127.7 0.1 slice_reduce_fusion
  127.8 0.2 broadcast_in_dim.18
  128.0 17.5 %all_to_all.45 = f32[64,1,1280]{2,1,0:T(1,128)S(1)} all-to-all(f32[64,1,1280]{2,1,0:T(1,128)S(1)} %broadcast_in_dim.18), channel_id=1, replica_groups={{128,130,132,134,136,138,140,142,144,146,148,150,152,154,156,158,160,16..., dimensions={0} | all-to-all | bytes 655360 | tf_op jit(solution)/shard_map/all_to_all | solution.py:282
  145.5 4.2 %collective-permute-start.5 = (f32[256,128]{1,0:T(8,128)S(1)}, f32[256,128]{1,0:T(8,128)S(1)}, u32[]{:S(2)}, u32[]{:S(2)}) collective-permute-start(f32[256,128]{1,0:T(8,128)S(1)} %slice.33), channel_id=1, source_target_pairs={{0,1},{1,0},{2,3},{3,2},{4,5},{5,4},{6,7},{7,6},{8,9},{9,8},{10,11... | collective-permute-start | bytes 393224 | tf_op jit(solution)/shard_map/ppermute | solution.py:249
  149.7 0.1 pad_add_fusion.section
  149.8 9.1 %shard_map.57 = (f32[256,256]{1,0:T(8,128)S(1)}, f32[256,256]{1,0:T(8,128)S(1)}) custom-call(s32[2]{0:T(128)S(1)} %pad_add_fusion.section, f32[384,128]{1,0:T(8,128)S(1)} %get-tuple-element.38.kept, f32[640,128]{1,0:T(8,128)S(1)} %bitcast.22), custom_call_target="tpu_custom_call" | custom-call | tf_op jit(solution)/shard_map/pallas_call | solution.py:310
  159.0 1.7 shard_map.58.gram
  160.7 0.0 collective-permute-done.5.beside
  160.7 0.9 shard_map.59
  161.6 17.1 %all_to_all.46 = f32[32,1,2560]{2,1,0:T(1,128)S(1)} all-to-all(f32[32,1,2560]{2,1,0:T(1,128)S(1)} %bitcast.33), channel_id=1, replica_groups=mesh['cores'=4,'row'=32,'tensor'=2] {'row'}, dimensions={0} | all-to-all | bytes 655360 | tf_op jit(solution)/shard_map/all_to_all | solution.py:279
  178.7 0.2 reduce_sum.41
  178.9 0.7 collective-permute-start.6
  179.6 0.7 collective-permute-start.7
  180.3 1.3 collective-permute-start.8
  181.6 0.0 collective-permute-done.6
  181.6 0.0 collective-permute-done.7
  181.6 4.8 %collective-permute-done.8 = f32[1,2560]{1,0:T(1,128)S(1)} collective-permute-done((f32[1,2560]{1,0:T(1,128)S(1)}, f32[1,2560]{1,0:T(1,128)S(1)}, u32[]{:S(2)}, u32[]{:S(2)}) %collective-permute-start.8) | collective-permute-done | bytes 10272 | tf_op jit(solution)/shard_map/ppermute | solution.py:303
  186.4 0.9 broadcast_in_dim.39
  187.3 4.5 %all-to-all-start.7 = ((f32[32,1,2560]{2,1,0:T(1,128)}), f32[32,1,2560]{2,1,0:T(1,128)S(1)}, u32[]{:S(2)}, u32[]{:S(2)}) async-start(f32[32,1,2560]{2,1,0:T(1,128)} %broadcast_in_dim.39), calls=%async_computation.7 | async-start | bytes 655360 | tf_op jit(solution)/shard_map/all_to_all | solution.py:279
  191.8 0.0 copy-start.14
  191.8 1.4 collective-permute-start.4
  193.3 0.1 pad_add_fusion.1.place
  193.3 9.3 %all-to-all-done.7 = f32[32,1,2560]{2,1,0:T(1,128)S(1)} async-done(((f32[32,1,2560]{2,1,0:T(1,128)}), f32[32,1,2560]{2,1,0:T(1,128)S(1)}, u32[]{:S(2)}, u32[]{:S(2)}) %all-to-all-start.7) | async-done | bytes 327712 | tf_op jit(solution)/shard_map/all_to_all | solution.py:279
  202.6 4.7 %collective-permute-start.9 = (f32[256,128]{1,0:T(8,128)S(1)}, f32[256,128]{1,0:T(8,128)S(1)}, u32[]{:S(2)}, u32[]{:S(2)}) collective-permute-start(f32[256,128]{1,0:T(8,128)S(1)} %slice.34), channel_id=1, source_target_pairs={{0,1},{1,0},{2,3},{3,2},{4,5},{5,4},{6,7},{7,6},{8,9},{9,8},{10,11... | collective-permute-start | bytes 393224 | tf_op jit(solution)/shard_map/ppermute | solution.py:249
  207.3 0.0 collective-permute-done.4
  207.4 0.9 collective-permute-done.9.beside
  208.3 9.5 %shard_map.60 = (f32[64,256]{1,0:T(8,128)}, f32[64,256]{1,0:T(8,128)}, f32[256,256]{1,0:T(8,128)S(1)}) custom-call(s32[3]{0:T(128)S(1)} %pad_add_fusion.1.place, f32[640,128]{1,0:T(8,128)S(1)} %bitcast.32, f32[256,128]{1,0:T(8,128)S(1)} %collective-permute-done.9.beside, f32[256,256]{1,0:T(8,128)S(1)} %copy-done.16), custom_call_target="tpu_custom_call" | custom-call | tf_op jit(solution)/shard_map/pallas_call | solution.py:322
  217.8 2.2 shard_map.61
  (37 shorter events, 0.2 us)
Async XLA Ops:
  0.6 6.8 %collective-permute-start = (f32[4,256,256]{2,1,0:T(8,128)}, f32[4,256,256]{2,1,0:T(8,128)}, u32[]{:S(2)}, u32[]{:S(2)}) collective-permute-start(f32[4,256,256]{2,1,0:T(8,128)} %bitcast.17), channel_id=1, source_target_pairs={{0,1},{1,0},{2,3},{3,2},{4,5},{5,4},{6,7},{7,6},{8,9},{9,8},{10,11... | collective-permute-start | bytes 3145736 | tf_op jit(solution)/shard_map/ppermute | solution.py:249
  4.0 2.8 %collective-permute-start.1 = (f32[256,256]{1,0:T(8,128)}, f32[256,256]{1,0:T(8,128)S(1)}, u32[]{:S(2)}, u32[]{:S(2)}) collective-permute-start(f32[256,256]{1,0:T(8,128)} %bitcast.37), channel_id=1, source_target_pairs={{0,1},{1,0},{2,3},{3,2},{4,5},{5,4},{6,7},{7,6},{8,9},{9,8},{10,11... | collective-permute-start | bytes 786440 | tf_op jit(solution)/shard_map/ppermute | solution.py:249
  4.1 1.2 copy-start
  5.3 2.1 copy-start.1
  6.7 0.7 copy-start.17
  7.4 1.0 copy-start.13
  8.4 0.9 copy-start.18
  11.5 1.7 copy-start.2
  11.5 1.7 copy-start.4
  11.5 1.7 copy-start.6
  13.2 1.0 copy-start.11
  56.0 0.7 copy-start.8
  56.8 7.6 %collective-permute-start.2 = (f32[256,128]{1,0:T(8,128)}, f32[256,128]{1,0:T(8,128)S(1)}, u32[]{:S(2)}, u32[]{:S(2)}) collective-permute-start(f32[256,128]{1,0:T(8,128)} %slice.29), channel_id=1, source_target_pairs={{0,1},{1,0},{2,3},{3,2},{4,5},{5,4},{6,7},{7,6},{8,9},{9,8},{10,11... | collective-permute-start | bytes 393224 | tf_op jit(solution)/shard_map/ppermute | solution.py:249
  60.7 1.0 copy-start.9
  61.7 0.9 copy-start.12
  62.6 1.7 copy-start.3
  62.6 1.7 copy-start.5
  62.6 1.8 copy-start.7
  62.6 1.8 copy-start.10
  103.7 6.1 %collective-permute-start.3 = (f32[256,128]{1,0:T(8,128)S(1)}, f32[256,128]{1,0:T(8,128)S(1)}, u32[]{:S(2)}, u32[]{:S(2)}) collective-permute-start(f32[256,128]{1,0:T(8,128)S(1)} %slice.31), channel_id=1, source_target_pairs={{0,1},{1,0},{2,3},{3,2},{4,5},{5,4},{6,7},{7,6},{8,9},{9,8},{10,11... | collective-permute-start | bytes 393224 | tf_op jit(solution)/shard_map/ppermute | solution.py:249
  145.5 15.2 %collective-permute-start.5 = (f32[256,128]{1,0:T(8,128)S(1)}, f32[256,128]{1,0:T(8,128)S(1)}, u32[]{:S(2)}, u32[]{:S(2)}) collective-permute-start(f32[256,128]{1,0:T(8,128)S(1)} %slice.33), channel_id=1, source_target_pairs={{0,1},{1,0},{2,3},{3,2},{4,5},{5,4},{6,7},{7,6},{8,9},{9,8},{10,11... | collective-permute-start | bytes 393224 | tf_op jit(solution)/shard_map/ppermute | solution.py:249
  158.9 1.7 copy-start.15
  159.0 1.7 copy-start.19
  178.9 2.7 %collective-permute-start.6 = (f32[1,2560]{1,0:T(1,128)S(1)}, f32[1,2560]{1,0:T(1,128)S(1)}, u32[]{:S(2)}, u32[]{:S(2)}) collective-permute-start(f32[1,2560]{1,0:T(1,128)S(1)} %reduce_sum.42), channel_id=1, source_target_pairs={{192,128},{193,129},{194,130},{195,131},{196,132},{197,133},{198,1... | collective-permute-start | bytes 30728 | tf_op jit(solution)/shard_map/ppermute | solution.py:303
  179.6 2.0 collective-permute-start.7
  180.3 6.1 %collective-permute-start.8 = (f32[1,2560]{1,0:T(1,128)S(1)}, f32[1,2560]{1,0:T(1,128)S(1)}, u32[]{:S(2)}, u32[]{:S(2)}) collective-permute-start(f32[1,2560]{1,0:T(1,128)S(1)} %reduce_sum.42), channel_id=1, source_target_pairs={{192,0},{193,1},{194,2},{195,3},{196,4},{197,5},{198,6},{199,7},{2... | collective-permute-start | bytes 30728 | tf_op jit(solution)/shard_map/ppermute | solution.py:303
  187.3 4.5 %copy-start.20 = (f32[256,256]{1,0:T(8,128)S(1)}, f32[256,256]{1,0:T(8,128)}, u32[]{:S(2)}) copy-start(f32[256,256]{1,0:T(8,128)} %copy-done.19) | copy-start | bytes 786436
  187.3 15.3 %all-to-all-start.7 = ((f32[32,1,2560]{2,1,0:T(1,128)}), f32[32,1,2560]{2,1,0:T(1,128)S(1)}, u32[]{:S(2)}, u32[]{:S(2)}) async-start(f32[32,1,2560]{2,1,0:T(1,128)} %broadcast_in_dim.39), calls=%async_computation.7 | async-start | bytes 655360 | tf_op jit(solution)/shard_map/all_to_all | solution.py:279
  191.8 15.6 %copy-start.14 = (f32[1,256,256]{2,1,0:T(8,128)S(1)}, f32[1,256,256]{2,1,0:T(8,128)}, u32[]{:S(2)}) copy-start(f32[1,256,256]{2,1,0:T(8,128)} %param.3) | copy-start | bytes 786436
  191.8 15.5 %collective-permute-start.4 = (f32[256,256]{1,0:T(8,128)S(1)}, f32[256,256]{1,0:T(8,128)S(1)}, u32[]{:S(2)}, u32[]{:S(2)}) collective-permute-start(f32[256,256]{1,0:T(8,128)S(1)} %copy-done.20), channel_id=1, source_target_pairs={{0,64},{64,128},{128,192},{1,65},{65,129},{129,193},{2,66},{66,130... | collective-permute-start | bytes 786440 | tf_op jit(solution)/shard_map/ppermute | solution.py:318
  202.6 5.7 %copy-start.16 = (f32[256,256]{1,0:T(8,128)S(1)}, f32[256,256]{1,0:T(8,128)}, u32[]{:S(2)}) copy-start(f32[256,256]{1,0:T(8,128)} %copy-done.15) | copy-start | bytes 786436
  202.6 5.7 %collective-permute-start.9 = (f32[256,128]{1,0:T(8,128)S(1)}, f32[256,128]{1,0:T(8,128)S(1)}, u32[]{:S(2)}, u32[]{:S(2)}) collective-permute-start(f32[256,128]{1,0:T(8,128)S(1)} %slice.34), channel_id=1, source_target_pairs={{0,1},{1,0},{2,3},{3,2},{4,5},{5,4},{6,7},{7,6},{8,9},{9,8},{10,11... | collective-permute-start | bytes 393224 | tf_op jit(solution)/shard_map/ppermute | solution.py:249

commit v4 on v3

--- a/solution.py
+++ b/solution.py
@@ -121,29 +121,37 @@
     return dot3(left, (stacked(mh, width), stacked(ml, width)))
 
 
-def chain_gram(state, ch, cl, th, tl, out):
+def chain_gram(tick, place, state, ch, cl, th, tl, out):
     rank = ch.shape[0]
-    a, b, c = gram_blocks(state)
-    gram = jnp.concatenate(
-        [jnp.concatenate([a, b], axis=1), jnp.concatenate([b.T, c], axis=1)], axis=0
-    )
-    pack_gram(out, chain_product(split(gram), (ch[...], cl[...]), (th[...], tl[...]), rank))
-
-
-def chain_gram_keep(tick, section, kept, state, ch, cl, th, tl, out, keep):
-    mine = section[0] == tick - 1
+
+    @pl.when(place[0] == tick)
+    def _():
+        a, b, c = gram_blocks(state)
+        gram = jnp.concatenate(
+            [jnp.concatenate([a, b], axis=1), jnp.concatenate([b.T, c], axis=1)], axis=0
+        )
+        pack_gram(
+            out, chain_product(split(gram), (ch[...], cl[...]), (th[...], tl[...]), rank)
+        )
+
+
+def chain_gram_keep(tick, place, kept, state, ch, cl, th, tl, out, keep):
+    mine = place[0] == tick - 1
     keep[...] = jnp.where(mine, state[: keep.shape[0], :], kept[...])
-    chain_gram(state, ch, cl, th, tl, out)
-
-
-def chain_link(which, gram, state, beside, lh, ll, rh, rl, out):
+    chain_gram(tick, place, state, ch, cl, th, tl, out)
+
+
+def chain_link(tick, place, gram, state, beside, lh, ll, rh, rl, out):
     rank = lh.shape[0]
     half = rank // 2
-    out[: 3 * half, :] = gram[...]
-    link = whole_link(which[0] == 0, state[3 * half :, :], beside[...])
-    out[3 * half :, :] = chain_product(
-        split(link), (rh[...], rl[...]), (lh[...], ll[...]), half
-    )
+
+    @pl.when(place[0] == tick)
+    def _():
+        out[: 3 * half, :] = gram[...]
+        link = whole_link(place[1] == 0, state[3 * half :, :], beside[...])
+        out[3 * half :, :] = chain_product(
+            split(link), (rh[...], rl[...]), (lh[...], ll[...]), half
+        )
 
 
 def eliminate(m, offset, n):
@@ -221,20 +229,20 @@
         pltpu.sync_copy(x, x_out)
 
 
-def factor_last(place, state, beside, x_own, tail, correlation, x_out, work, square):
+def factor_last(flags, state, beside, x_own, both, x_out, work):
     rank = work.shape[0]
-    rows = pl.ds(pl.multiple_of(place[0] * tail.shape[0], tail.shape[0]), tail.shape[0])
-    first = place[1] == 0
-    link = whole_link(first, state[3 * rank // 2 :, :], beside[...])
-    square[...] = jnp.where(first, link, link.T)
-    correlation[...] = square[rows, :]
-    unpack_gram(state, work)
-    factorize(square, x_out, work)
-    tail[...] = square[rows, :]
-
-    @pl.when(place[2] == 0)
+
+    @pl.when(flags[0] == 0)
     def _():
         x_out[...] = x_own[...]
+
+    @pl.when(flags[0] != 0)
+    def _():
+        first = flags[1] == 0
+        link = whole_link(first, state[3 * rank // 2 :, :], beside[...])
+        both[:, rank:] = jnp.where(first, link, link.T)
+        unpack_gram(state, work)
+        factorize(both, x_out, work)
 
 
 def frame(scale, own, upper, inverse, out):
@@ -271,17 +279,26 @@
         prepare_link, [wide] * 2 + [narrow] * 2 + [packed, side], [SMEM] + [VMEM] * 6
     )(scalars(which), own, other, *own_parts[2:], up, up_other)
     gram_shape = ((3 * half, half), F32)
-    run_gram = call(chain_gram, [gram_shape], [VMEM] * 5)
-    run_link = call(chain_link, [packed], [SMEM] + [VMEM] * 7)
+    near = max(1, rows // 4)
+    far = rows // near
+    place = scalars(section, which)
 
     def exchange(x, pair):
+        blocks = [[g * near + j for j in range(near)] for g in range(far)]
         if pair is None:
-            return lax.all_to_all(x, "row", 0, 0, tiled=True)
+            return lax.all_to_all(x, "row", 0, 0, tiled=True, axis_index_groups=blocks)
         rest = [k for k in range(sections) if k not in pair]
-        groups = [[k * rows + r for k in p for r in range(rows)] for p in (pair, rest)]
+        groups = [[k * rows + r for k in p for r in b] for p in (pair, rest) for b in blocks]
         return lax.all_to_all(
             x, ("cores", "row"), 0, 0, tiled=True, axis_index_groups=groups
         )
+
+    def over_far(x):
+        terms = [x]
+        for step in range(1, far):
+            pairs = [(r, (r + step * near) % rows) for r in range(rows)]
+            terms.append(lax.ppermute(x, "row", pairs))
+        return sum(terms[2::2], terms[0]) + sum(terms[3::2], terms[1])
 
     kept = None
     for tick in range(sections):
@@ -290,19 +307,19 @@
                 functools.partial(chain_gram_keep, tick),
                 [gram_shape] * 2,
                 [SMEM] + [VMEM] * 6,
-            )(scalars(section), kept, state, *own_parts)
+            )(place, kept, state, *own_parts)
         else:
-            (gram,) = run_gram(state, *own_parts)
+            (gram,) = call(
+                functools.partial(chain_gram, tick), [gram_shape], [SMEM] + [VMEM] * 5
+            )(place, state, *own_parts)
             kept = gram if tick == 0 else kept
-        (partial,) = run_link(scalars(which), gram, state, beside, *link_parts)
+        (partial,) = call(
+            functools.partial(chain_link, tick), [packed], [SMEM] + [VMEM] * 7
+        )(place, gram, state, beside, *link_parts)
         pair = (tick, tick + 1) if tick < last else None
-        count = rows * (2 if pair else 1)
-        arrived = exchange(partial.reshape(count, 1, -1), pair)
-        piece = arrived[:rows].sum(axis=0)
-        if tick == last:
-            sent = [lax.ppermute(piece, "cores", [(last, k)]) for k in range(last)]
-            for k in range(last):
-                piece = jnp.where(section == k, sent[k], piece)
+        count = near * (2 if pair else 1)
+        arrived = exchange(partial.reshape(count, -1, half), pair)
+        piece = over_far(arrived[:near].sum(axis=0))
         copies = jnp.broadcast_to(piece[None], arrived.shape)
         state = exchange(copies, pair).reshape(partial.shape)
         beside = swapped(state[3 * half :])
@@ -318,17 +335,19 @@
             u_before = lax.ppermute(u_own, "cores", [(k, k + 1) for k in range(last)])
             u_before = jnp.where(section == 0, up, u_before)
 
-    share = ((rank // sections, rank), F32)
-    tail, correlation, x_own = call(
-        factor_last,
-        [share, share, square],
-        [SMEM] + [VMEM] * 3,
-        scratch + [pltpu.VMEM((rank, rank), F32)],
-    )(scalars(section, which, section == last), state, beside, x_own)
+    both, x_own = call(
+        factor_last, [((rank, 2 * rank), F32), square], [SMEM] + [VMEM] * 3, scratch
+    )(scalars(section == last, which), state, beside, x_own)
+    share = rank // sections
+    tiles = both.reshape(sections, share, 2 * rank)
+    sent = [lax.ppermute(tiles[k], "cores", [(last, k)]) for k in range(last)]
     (frames,) = call(
         functools.partial(frame, float(MODE * rank) ** 0.5), [(own.shape, F32)], [VMEM] * 3
     )(own, u_before, x_own)
-    return frames[None, None], tail[None], correlation[None]
+    result = tiles[last]
+    for k in range(last):
+        result = jnp.where(section == k, sent[k], result)
+    return frames[None, None], result[None, :, :rank], result[None, :, rank:]
 
 
 def solution(mesh):

time: 221 us -> 185 us (0.84)
  blocking collectives: 131 us -> 89.6 us
  starting transfers between devices: 29.2 us -> 50.4 us
  Pallas kernels: 33.8 us -> 21.7 us
  local copies, waits for them, and re-layouts: 8.63 us -> 3.71 us
    all_to_all x6, blocking collectives: 113 us -> 67.9 us  [exchange(): lax.all_to_all(x, ('cores', 'row'), 0, 0, tiled=True, axis_index_groups=g...]
    ppermute x3 -> x15, starting transfers between devices: 2.62 us -> 30 us  [the longest x12 27.3 us: over_far(): terms.append(lax.ppermute(x, 'row', pairs))]
    ppermute x3 -> x15, waiting for transfers between devices: 4.79 us -> 14.7 us  [the longest x12 9.7 us: over_far(): terms.append(lax.ppermute(x, 'row', pairs))]
    pallas_call x7, Pallas kernels: 16.6 us -> 6.69 us  [the longest x4 3.34 us: shards(): call(functools.partial(chain_link, tick), [packed], [SMEM] + [VMEM] * 7)]
    all_to_all x1 -> x0, waiting for transfers between devices: 9.28 us -> none  [exchange(): return lax.all_to_all(x, 'row', 0, 0, tiled=True)]
    all_to_all x1 -> x2, blocking collectives: 17.1 us -> 21.7 us  [exchange(): return lax.all_to_all(x, 'row', 0, 0, tiled=True, axis_index_groups=blocks)]
    all_to_all x1 -> x0, starting transfers between devices: 4.45 us -> none  [exchange(): return lax.all_to_all(x, 'row', 0, 0, tiled=True)]
    unnamed x42 -> x12, local copies, waits for them, and re-layouts: 6.52 us -> 2.89 us
  transfers between devices with their start and end apart: 11 -> 22, of which waited for: 4 -> 13; matrix products, arithmetic and copies ran while one was open for 0% -> 0% of each run, Pallas kernels for 7% -> 8%
where the time goes in v4:
time: 185 us
  blocking collectives  89.6 us (48%)
  starting transfers between devices  50.4 us (27%)
  Pallas kernels  21.7 us (12%)
  waiting for transfers between devices  18 us (10%)
  local copies, waits for them, and re-layouts  3.71 us (2%)
    all_to_all x6, blocking collectives, exchange(): lax.all_to_all(x, ('cores', 'row'), 0, 0, tiled=True, axis_index_groups=g...  67.9 us
    ppermute x12, starting transfers between devices, over_far(): terms.append(lax.ppermute(x, 'row', pairs))  27.3 us
    all_to_all x2, blocking collectives, exchange(): return lax.all_to_all(x, 'row', 0, 0, tiled=True, axis_index_groups=blocks)  21.7 us
    ppermute x6, starting transfers between devices, swapped(): return lax.ppermute(x, 'tensor', [(0, 1), (1, 0)])  18.2 us
    ppermute x12, waiting for transfers between devices, over_far(): terms.append(lax.ppermute(x, 'row', pairs))  9.7 us
    pallas_call x1, Pallas kernels, shards(): call(factor_own, [square] * 2, [SMEM] + [HBM] * 2, scratch + [pltpu.VMEM(...  9.14 us
    ppermute x3, waiting for transfers between devices, shards(): sent = [lax.ppermute(tiles[k], 'cores', [(last, k)]) for k in range(last)]  4.99 us
  transfers between devices with their start and end apart: 22, of which 13 were waited for; matrix products, arithmetic and copies ran while one was open for 0% of the time, Pallas kernels for 8%

profile of v4, /device:TPU:1, one launch (start us, length us, event | category | flops | bytes accessed | tf_op | source)
XLA Modules:
  0.0 184.7 jit_solution(14728791107046223605)
XLA Ops:
  0.6 3.3 %collective-permute-start = (f32[4,256,256]{2,1,0:T(8,128)}, f32[4,256,256]{2,1,0:T(8,128)}, u32[]{:S(2)}, u32[]{:S(2)}) collective-permute-start(f32[4,256,256]{2,1,0:T(8,128)} %bitcast.19), channel_id=1, source_target_pairs={{0,1},{1,0},{2,3},{3,2},{4,5},{5,4},{6,7},{7,6},{8,9},{9,8},{10,11... | collective-permute-start | bytes 3145736 | tf_op jit(solution)/shard_map/ppermute | solution.py:257
  4.0 0.1 collective-permute-start.1
  4.1 1.2 copy-done
  5.3 0.4 shard_map.49
  5.7 0.1 pad_add_fusion.2.place
  5.8 1.0 collective-permute-done.1.up_other
  6.7 0.2 collective-permute-done.other
  7.0 0.9 copy-done.2
  7.9 2.2 %shard_map.50 = (bf16[256,1024]{1,0:T(8,128)(2,1)S(1)}, bf16[256,1024]{1,0:T(8,128)(2,1)S(1)}, bf16[256,512]{1,0:T(8,128)(2,1)S(1)}, bf16[256,512]{1,0:T(8,128)(...) custom-call(s32[1]{0:T(128)} %bitcast.3.which, f32[4,256,256]{2,1,0:T(8,128)S(1)} %bitcast.21, ...), custom_call_target="tpu_custom_call" | custom-call | tf_op jit(solution)/shard_map/pallas_call | solution.py:278
  10.1 2.2 %shard_map.51.gram.kept = f32[384,128]{1,0:T(8,128)S(1)} custom-call(s32[2]{0:T(128)S(1)} %pad_add_fusion.2.place, f32[640,128]{1,0:T(8,128)S(1)} %get-tuple-element.26.state, bf16[256,1024]{1,0:T(8,128)(2,1)S(1)} %get-tuple-element.27.ch, bf16[256,1024]{1,0:T(8,128)(2,1)S(1)} %get-tuple-element.28.cl, bf16[256,1024]{1,0:T(8,128)(2,1)S(1)} %get-tuple-element.24.th, ...), custom_call_target="tpu_custom_call" | custom-call | tf_op jit(solution)/shard_map/pallas_call | solution.py:312
  12.3 1.5 shard_map.52
  13.8 12.0 %all_to_all.40 = f32[16,40,128]{2,1,0:T(8,128)S(1)} all-to-all(f32[16,40,128]{2,1,0:T(8,128)S(1)} %bitcast.38), channel_id=1, replica_groups={{0,2,4,6,8,10,12,14,64,66,68,70,72,74,76,78},{16,18,20,22,24,26,28,30,8..., dimensions={0} | all-to-all | bytes 655360 | tf_op jit(solution)/shard_map/all_to_all | solution.py:292
  25.8 6.1 %collective-permute-start.2 = (f32[40,128]{1,0:T(8,128)S(1)}, f32[40,128]{1,0:T(8,128)S(1)}, u32[]{:S(2)}, u32[]{:S(2)}) collective-permute-start(f32[40,128]{1,0:T(8,128)S(1)} %slice_reduce_fusion.2), channel_id=1, source_target_pairs={{0,32},{2,34},{4,36},{6,38},{8,40},{10,42},{12,44},{14,46},{16,48}... | collective-permute-start | bytes 61448 | tf_op jit(solution)/shard_map/ppermute | solution.py:300
  31.9 1.2 collective-permute-start.3
  33.1 2.4 %collective-permute-start.4 = (f32[40,128]{1,0:T(8,128)S(1)}, f32[40,128]{1,0:T(8,128)S(1)}, u32[]{:S(2)}, u32[]{:S(2)}) collective-permute-start(f32[40,128]{1,0:T(8,128)S(1)} %slice_reduce_fusion.2), channel_id=1, source_target_pairs={{0,48},{2,50},{4,52},{6,54},{8,56},{10,58},{12,60},{14,62},{16,0},... | collective-permute-start | bytes 61448 | tf_op jit(solution)/shard_map/ppermute | solution.py:300
  35.5 1.3 collective-permute-done.3
  36.8 10.2 %all_to_all.41 = f32[16,40,128]{2,1,0:T(8,128)S(1)} all-to-all(f32[16,40,128]{2,1,0:T(8,128)S(1)} %broadcast_in_dim.14), channel_id=1, replica_groups={{0,2,4,6,8,10,12,14,64,66,68,70,72,74,76,78},{16,18,20,22,24,26,28,30,8..., dimensions={0} | all-to-all | bytes 655360 | tf_op jit(solution)/shard_map/all_to_all | solution.py:292
  47.0 4.6 %collective-permute-start.5 = (f32[256,128]{1,0:T(8,128)S(1)}, f32[256,128]{1,0:T(8,128)S(1)}, u32[]{:S(2)}, u32[]{:S(2)}) collective-permute-start(f32[256,128]{1,0:T(8,128)S(1)} %slice.57), channel_id=1, source_target_pairs={{0,1},{1,0},{2,3},{3,2},{4,5},{5,4},{6,7},{7,6},{8,9},{9,8},{10,11... | collective-permute-start | bytes 393224 | tf_op jit(solution)/shard_map/ppermute | solution.py:257
  51.6 0.6 shard_map.53
  52.2 0.4 collective-permute-done.5.beside
  52.6 0.5 shard_map.54
  53.1 12.4 %all_to_all.42 = f32[16,40,128]{2,1,0:T(8,128)S(1)} all-to-all(f32[16,40,128]{2,1,0:T(8,128)S(1)} %bitcast.36), channel_id=1, replica_groups={{64,66,68,70,72,74,76,78,128,130,132,134,136,138,140,142},{80,82,84,86,..., dimensions={0} | all-to-all | bytes 655360 | tf_op jit(solution)/shard_map/all_to_all | solution.py:292
  65.5 1.9 %collective-permute-start.6 = (f32[40,128]{1,0:T(8,128)S(1)}, f32[40,128]{1,0:T(8,128)S(1)}, u32[]{:S(2)}, u32[]{:S(2)}) collective-permute-start(f32[40,128]{1,0:T(8,128)S(1)} %slice_reduce_fusion.1), channel_id=1, source_target_pairs={{0,32},{2,34},{4,36},{6,38},{8,40},{10,42},{12,44},{14,46},{16,48}... | collective-permute-start | bytes 61448 | tf_op jit(solution)/shard_map/ppermute | solution.py:300
  67.4 3.9 %collective-permute-start.7 = (f32[40,128]{1,0:T(8,128)S(1)}, f32[40,128]{1,0:T(8,128)S(1)}, u32[]{:S(2)}, u32[]{:S(2)}) collective-permute-start(f32[40,128]{1,0:T(8,128)S(1)} %slice_reduce_fusion.1), channel_id=1, source_target_pairs={{0,16},{2,18},{4,20},{6,22},{8,24},{10,26},{12,28},{14,30},{16,32}... | collective-permute-start | bytes 61448 | tf_op jit(solution)/shard_map/ppermute | solution.py:300
  71.2 1.0 collective-permute-done.6
  72.2 0.1 collective-permute-done.7
  72.3 2.4 %collective-permute-done.8 = f32[40,128]{1,0:T(8,128)S(1)} collective-permute-done((f32[40,128]{1,0:T(8,128)S(1)}, f32[40,128]{1,0:T(8,128)S(1)}, u32[]{:S(2)}, u32[]{:S(2)}) %collective-permute-start.8) | collective-permute-done | bytes 20512 | tf_op jit(solution)/shard_map/ppermute | solution.py:300
  74.8 11.6 %all_to_all.43 = f32[16,40,128]{2,1,0:T(8,128)S(1)} all-to-all(f32[16,40,128]{2,1,0:T(8,128)S(1)} %broadcast_in_dim.15), channel_id=1, replica_groups={{64,66,68,70,72,74,76,78,128,130,132,134,136,138,140,142},{80,82,84,86,..., dimensions={0} | all-to-all | bytes 655360 | tf_op jit(solution)/shard_map/all_to_all | solution.py:292
  86.4 4.4 %collective-permute-start.9 = (f32[256,128]{1,0:T(8,128)S(1)}, f32[256,128]{1,0:T(8,128)S(1)}, u32[]{:S(2)}, u32[]{:S(2)}) collective-permute-start(f32[256,128]{1,0:T(8,128)S(1)} %slice.59), channel_id=1, source_target_pairs={{0,1},{1,0},{2,3},{3,2},{4,5},{5,4},{6,7},{7,6},{8,9},{9,8},{10,11... | collective-permute-start | bytes 393224 | tf_op jit(solution)/shard_map/ppermute | solution.py:257
  90.8 0.6 shard_map.55
  91.4 0.4 collective-permute-done.9.beside
  91.8 0.5 shard_map.56
  92.4 11.1 %all_to_all.44 = f32[16,40,128]{2,1,0:T(8,128)S(1)} all-to-all(f32[16,40,128]{2,1,0:T(8,128)S(1)} %bitcast.37), channel_id=1, replica_groups={{128,130,132,134,136,138,140,142,192,194,196,198,200,202,204,206},{144,..., dimensions={0} | all-to-all | bytes 655360 | tf_op jit(solution)/shard_map/all_to_all | solution.py:292
  103.5 0.8 collective-permute-start.10
  104.3 2.3 %collective-permute-start.11 = (f32[40,128]{1,0:T(8,128)S(1)}, f32[40,128]{1,0:T(8,128)S(1)}, u32[]{:S(2)}, u32[]{:S(2)}) collective-permute-start(f32[40,128]{1,0:T(8,128)S(1)} %slice_reduce_fusion), channel_id=1, source_target_pairs={{0,16},{2,18},{4,20},{6,22},{8,24},{10,26},{12,28},{14,30},{16,32}... | collective-permute-start | bytes 61448 | tf_op jit(solution)/shard_map/ppermute | solution.py:300
  106.6 1.5 collective-permute-start.12
  108.2 2.0 %collective-permute-done.10 = f32[40,128]{1,0:T(8,128)S(1)} collective-permute-done((f32[40,128]{1,0:T(8,128)S(1)}, f32[40,128]{1,0:T(8,128)S(1)}, u32[]{:S(2)}, u32[]{:S(2)}) %collective-permute-start.10) | collective-permute-done | bytes 20512 | tf_op jit(solution)/shard_map/ppermute | solution.py:300
  110.2 0.3 collective-permute-done.12
  110.5 10.6 %all_to_all.45 = f32[16,40,128]{2,1,0:T(8,128)S(1)} all-to-all(f32[16,40,128]{2,1,0:T(8,128)S(1)} %broadcast_in_dim.16), channel_id=1, replica_groups={{128,130,132,134,136,138,140,142,192,194,196,198,200,202,204,206},{144,..., dimensions={0} | all-to-all | bytes 655360 | tf_op jit(solution)/shard_map/all_to_all | solution.py:292
  121.1 3.7 %collective-permute-start.14 = (f32[256,128]{1,0:T(8,128)S(1)}, f32[256,128]{1,0:T(8,128)S(1)}, u32[]{:S(2)}, u32[]{:S(2)}) collective-permute-start(f32[256,128]{1,0:T(8,128)S(1)} %slice.61), channel_id=1, source_target_pairs={{0,1},{1,0},{2,3},{3,2},{4,5},{5,4},{6,7},{7,6},{8,9},{9,8},{10,11... | collective-permute-start | bytes 393224 | tf_op jit(solution)/shard_map/ppermute | solution.py:257
  124.8 0.1 pad_add_fusion.section
  124.9 9.1 %shard_map.57 = (f32[256,256]{1,0:T(8,128)S(1)}, f32[256,256]{1,0:T(8,128)S(1)}) custom-call(s32[2]{0:T(128)S(1)} %pad_add_fusion.section, f32[384,128]{1,0:T(8,128)S(1)} %get-tuple-element.37.kept, f32[640,128]{1,0:T(8,128)S(1)} %bitcast.24), custom_call_target="tpu_custom_call" | custom-call | tf_op jit(solution)/shard_map/pallas_call | solution.py:327
  134.0 0.0 copy-start.4
  134.1 0.7 copy-done.4
  134.8 0.5 shard_map.58.gram
  135.3 0.8 shard_map.59
  136.1 10.2 %all_to_all.46 = f32[8,80,128]{2,1,0:T(8,128)S(1)} all-to-all(f32[8,80,128]{2,1,0:T(8,128)S(1)} %bitcast.35), channel_id=1, replica_groups={{0,2,4,6,8,10,12,14},{16,18,20,22,24,26,28,30},{32,34,36,38,40,42,44,46..., dimensions={0} | all-to-all | bytes 655360 | tf_op jit(solution)/shard_map/all_to_all | solution.py:289
  146.3 3.7 %collective-permute-start.15 = (f32[80,128]{1,0:T(8,128)S(1)}, f32[80,128]{1,0:T(8,128)S(1)}, u32[]{:S(2)}, u32[]{:S(2)}) collective-permute-start(f32[80,128]{1,0:T(8,128)S(1)} %reduce_sum.39), channel_id=1, source_target_pairs={{0,32},{2,34},{4,36},{6,38},{8,40},{10,42},{12,44},{14,46},{16,48}... | collective-permute-start | bytes 122888 | tf_op jit(solution)/shard_map/ppermute | solution.py:300
  150.0 0.9 collective-permute-start.16
  150.9 2.6 %collective-permute-start.17 = (f32[80,128]{1,0:T(8,128)S(1)}, f32[80,128]{1,0:T(8,128)S(1)}, u32[]{:S(2)}, u32[]{:S(2)}) collective-permute-start(f32[80,128]{1,0:T(8,128)S(1)} %reduce_sum.39), channel_id=1, source_target_pairs={{0,48},{2,50},{4,52},{6,54},{8,56},{10,58},{12,60},{14,62},{16,0},... | collective-permute-start | bytes 122888 | tf_op jit(solution)/shard_map/ppermute | solution.py:300
  153.6 2.6 %collective-permute-done.16 = f32[80,128]{1,0:T(8,128)S(1)} collective-permute-done((f32[80,128]{1,0:T(8,128)S(1)}, f32[80,128]{1,0:T(8,128)S(1)}, u32[]{:S(2)}, u32[]{:S(2)}) %collective-permute-start.16) | collective-permute-done | bytes 40992 | tf_op jit(solution)/shard_map/ppermute | solution.py:300
  156.2 11.5 %all_to_all.47 = f32[8,80,128]{2,1,0:T(8,128)S(1)} all-to-all(f32[8,80,128]{2,1,0:T(8,128)S(1)} %broadcast_in_dim.17), channel_id=1, replica_groups={{0,2,4,6,8,10,12,14},{16,18,20,22,24,26,28,30},{32,34,36,38,40,42,44,46..., dimensions={0} | all-to-all | bytes 655360 | tf_op jit(solution)/shard_map/all_to_all | solution.py:289
  167.8 2.0 %collective-permute-start.18 = (f32[256,128]{1,0:T(8,128)S(1)}, f32[256,128]{1,0:T(8,128)S(1)}, u32[]{:S(2)}, u32[]{:S(2)}) collective-permute-start(f32[256,128]{1,0:T(8,128)S(1)} %slice.62), channel_id=1, source_target_pairs={{0,1},{1,0},{2,3},{3,2},{4,5},{5,4},{6,7},{7,6},{8,9},{9,8},{10,11... | collective-permute-start | bytes 393224 | tf_op jit(solution)/shard_map/ppermute | solution.py:257
  169.8 2.2 %collective-permute-start.13 = (f32[256,256]{1,0:T(8,128)S(1)}, f32[256,256]{1,0:T(8,128)S(1)}, u32[]{:S(2)}, u32[]{:S(2)}) collective-permute-start(f32[256,256]{1,0:T(8,128)S(1)} %copy-done.5), channel_id=1, source_target_pairs={{0,64},{64,128},{128,192},{1,65},{65,129},{129,193},{2,66},{66,130... | collective-permute-start | bytes 786440 | tf_op jit(solution)/shard_map/ppermute | solution.py:335
  172.0 0.1 pad_add_fusion.1.flags
  172.1 0.6 shard_map.60
  172.6 0.0 copy-start.3
  172.7 0.8 collective-permute-start.19
  173.5 0.7 collective-permute-start.20
  174.2 1.3 collective-permute-start.21
  175.5 1.3 collective-permute-done.13
  176.8 2.2 %shard_map.61 = f32[4,256,256]{2,1,0:T(8,128)} custom-call(f32[4,256,256]{2,1,0:T(8,128)S(1)} %bitcast.22, f32[256,256]{1,0:T(8,128)S(1)} %broadcast_select_fusion.upper, f32[256,256]{1,0:T(8,128)S(1)} %get-tuple-element.43.inverse), custom_call_target="tpu_custom_call" | custom-call | tf_op jit(solution)/shard_map/pallas_call | solution.py:344
  179.0 5.0 %collective-permute-done.21 = f32[64,512]{1,0:T(8,128)S(1)} collective-permute-done((f32[64,512]{1,0:T(8,128)S(1)}, f32[64,512]{1,0:T(8,128)S(1)}, u32[]{:S(2)}, u32[]{:S(2)}) %collective-permute-start.21) | collective-permute-done | bytes 131104 | tf_op jit(solution)/shard_map/ppermute | solution.py:343
  184.0 0.7 slice_bitcast_fusion
  (36 shorter events, 0.4 us)
Async XLA Ops:
  0.6 6.3 %collective-permute-start = (f32[4,256,256]{2,1,0:T(8,128)}, f32[4,256,256]{2,1,0:T(8,128)}, u32[]{:S(2)}, u32[]{:S(2)}) collective-permute-start(f32[4,256,256]{2,1,0:T(8,128)} %bitcast.19), channel_id=1, source_target_pairs={{0,1},{1,0},{2,3},{3,2},{4,5},{5,4},{6,7},{7,6},{8,9},{9,8},{10,11... | collective-permute-start | bytes 3145736 | tf_op jit(solution)/shard_map/ppermute | solution.py:257
  4.0 2.8 %collective-permute-start.1 = (f32[256,256]{1,0:T(8,128)}, f32[256,256]{1,0:T(8,128)S(1)}, u32[]{:S(2)}, u32[]{:S(2)}) collective-permute-start(f32[256,256]{1,0:T(8,128)} %bitcast.39), channel_id=1, source_target_pairs={{0,1},{1,0},{2,3},{3,2},{4,5},{5,4},{6,7},{7,6},{8,9},{9,8},{10,11... | collective-permute-start | bytes 786440 | tf_op jit(solution)/shard_map/ppermute | solution.py:257
  4.1 1.2 copy-start
  5.3 1.7 copy-start.1
  7.0 1.0 copy-start.2
  25.8 9.7 %collective-permute-start.2 = (f32[40,128]{1,0:T(8,128)S(1)}, f32[40,128]{1,0:T(8,128)S(1)}, u32[]{:S(2)}, u32[]{:S(2)}) collective-permute-start(f32[40,128]{1,0:T(8,128)S(1)} %slice_reduce_fusion.2), channel_id=1, source_target_pairs={{0,32},{2,34},{4,36},{6,38},{8,40},{10,42},{12,44},{14,46},{16,48}... | collective-permute-start | bytes 61448 | tf_op jit(solution)/shard_map/ppermute | solution.py:300
  31.9 4.8 %collective-permute-start.3 = (f32[40,128]{1,0:T(8,128)S(1)}, f32[40,128]{1,0:T(8,128)S(1)}, u32[]{:S(2)}, u32[]{:S(2)}) collective-permute-start(f32[40,128]{1,0:T(8,128)S(1)} %slice_reduce_fusion.2), channel_id=1, source_target_pairs={{0,16},{2,18},{4,20},{6,22},{8,24},{10,26},{12,28},{14,30},{16,32}... | collective-permute-start | bytes 61448 | tf_op jit(solution)/shard_map/ppermute | solution.py:300
  33.1 3.6 %collective-permute-start.4 = (f32[40,128]{1,0:T(8,128)S(1)}, f32[40,128]{1,0:T(8,128)S(1)}, u32[]{:S(2)}, u32[]{:S(2)}) collective-permute-start(f32[40,128]{1,0:T(8,128)S(1)} %slice_reduce_fusion.2), channel_id=1, source_target_pairs={{0,48},{2,50},{4,52},{6,54},{8,56},{10,58},{12,60},{14,62},{16,0},... | collective-permute-start | bytes 61448 | tf_op jit(solution)/shard_map/ppermute | solution.py:300
  47.0 5.6 %collective-permute-start.5 = (f32[256,128]{1,0:T(8,128)S(1)}, f32[256,128]{1,0:T(8,128)S(1)}, u32[]{:S(2)}, u32[]{:S(2)}) collective-permute-start(f32[256,128]{1,0:T(8,128)S(1)} %slice.57), channel_id=1, source_target_pairs={{0,1},{1,0},{2,3},{3,2},{4,5},{5,4},{6,7},{7,6},{8,9},{9,8},{10,11... | collective-permute-start | bytes 393224 | tf_op jit(solution)/shard_map/ppermute | solution.py:257
  65.5 6.7 %collective-permute-start.6 = (f32[40,128]{1,0:T(8,128)S(1)}, f32[40,128]{1,0:T(8,128)S(1)}, u32[]{:S(2)}, u32[]{:S(2)}) collective-permute-start(f32[40,128]{1,0:T(8,128)S(1)} %slice_reduce_fusion.1), channel_id=1, source_target_pairs={{0,32},{2,34},{4,36},{6,38},{8,40},{10,42},{12,44},{14,46},{16,48}... | collective-permute-start | bytes 61448 | tf_op jit(solution)/shard_map/ppermute | solution.py:300
  67.4 5.0 %collective-permute-start.7 = (f32[40,128]{1,0:T(8,128)S(1)}, f32[40,128]{1,0:T(8,128)S(1)}, u32[]{:S(2)}, u32[]{:S(2)}) collective-permute-start(f32[40,128]{1,0:T(8,128)S(1)} %slice_reduce_fusion.1), channel_id=1, source_target_pairs={{0,16},{2,18},{4,20},{6,22},{8,24},{10,26},{12,28},{14,30},{16,32}... | collective-permute-start | bytes 61448 | tf_op jit(solution)/shard_map/ppermute | solution.py:300
  71.2 3.5 %collective-permute-start.8 = (f32[40,128]{1,0:T(8,128)S(1)}, f32[40,128]{1,0:T(8,128)S(1)}, u32[]{:S(2)}, u32[]{:S(2)}) collective-permute-start(f32[40,128]{1,0:T(8,128)S(1)} %slice_reduce_fusion.1), channel_id=1, source_target_pairs={{0,48},{2,50},{4,52},{6,54},{8,56},{10,58},{12,60},{14,62},{16,0},... | collective-permute-start | bytes 61448 | tf_op jit(solution)/shard_map/ppermute | solution.py:300
  86.4 5.4 %collective-permute-start.9 = (f32[256,128]{1,0:T(8,128)S(1)}, f32[256,128]{1,0:T(8,128)S(1)}, u32[]{:S(2)}, u32[]{:S(2)}) collective-permute-start(f32[256,128]{1,0:T(8,128)S(1)} %slice.59), channel_id=1, source_target_pairs={{0,1},{1,0},{2,3},{3,2},{4,5},{5,4},{6,7},{7,6},{8,9},{9,8},{10,11... | collective-permute-start | bytes 393224 | tf_op jit(solution)/shard_map/ppermute | solution.py:257
  103.5 6.6 %collective-permute-start.10 = (f32[40,128]{1,0:T(8,128)S(1)}, f32[40,128]{1,0:T(8,128)S(1)}, u32[]{:S(2)}, u32[]{:S(2)}) collective-permute-start(f32[40,128]{1,0:T(8,128)S(1)} %slice_reduce_fusion), channel_id=1, source_target_pairs={{0,32},{2,34},{4,36},{6,38},{8,40},{10,42},{12,44},{14,46},{16,48}... | collective-permute-start | bytes 61448 | tf_op jit(solution)/shard_map/ppermute | solution.py:300
  104.3 5.9 %collective-permute-start.11 = (f32[40,128]{1,0:T(8,128)S(1)}, f32[40,128]{1,0:T(8,128)S(1)}, u32[]{:S(2)}, u32[]{:S(2)}) collective-permute-start(f32[40,128]{1,0:T(8,128)S(1)} %slice_reduce_fusion), channel_id=1, source_target_pairs={{0,16},{2,18},{4,20},{6,22},{8,24},{10,26},{12,28},{14,30},{16,32}... | collective-permute-start | bytes 61448 | tf_op jit(solution)/shard_map/ppermute | solution.py:300
  106.6 3.8 %collective-permute-start.12 = (f32[40,128]{1,0:T(8,128)S(1)}, f32[40,128]{1,0:T(8,128)S(1)}, u32[]{:S(2)}, u32[]{:S(2)}) collective-permute-start(f32[40,128]{1,0:T(8,128)S(1)} %slice_reduce_fusion), channel_id=1, source_target_pairs={{0,48},{2,50},{4,52},{6,54},{8,56},{10,58},{12,60},{14,62},{16,0},... | collective-permute-start | bytes 61448 | tf_op jit(solution)/shard_map/ppermute | solution.py:300
  121.1 14.2 %collective-permute-start.14 = (f32[256,128]{1,0:T(8,128)S(1)}, f32[256,128]{1,0:T(8,128)S(1)}, u32[]{:S(2)}, u32[]{:S(2)}) collective-permute-start(f32[256,128]{1,0:T(8,128)S(1)} %slice.61), channel_id=1, source_target_pairs={{0,1},{1,0},{2,3},{3,2},{4,5},{5,4},{6,7},{7,6},{8,9},{9,8},{10,11... | collective-permute-start | bytes 393224 | tf_op jit(solution)/shard_map/ppermute | solution.py:257
  134.0 0.7 copy-start.4
  146.3 7.3 %collective-permute-start.15 = (f32[80,128]{1,0:T(8,128)S(1)}, f32[80,128]{1,0:T(8,128)S(1)}, u32[]{:S(2)}, u32[]{:S(2)}) collective-permute-start(f32[80,128]{1,0:T(8,128)S(1)} %reduce_sum.39), channel_id=1, source_target_pairs={{0,32},{2,34},{4,36},{6,38},{8,40},{10,42},{12,44},{14,46},{16,48}... | collective-permute-start | bytes 122888 | tf_op jit(solution)/shard_map/ppermute | solution.py:300
  150.0 6.2 %collective-permute-start.16 = (f32[80,128]{1,0:T(8,128)S(1)}, f32[80,128]{1,0:T(8,128)S(1)}, u32[]{:S(2)}, u32[]{:S(2)}) collective-permute-start(f32[80,128]{1,0:T(8,128)S(1)} %reduce_sum.39), channel_id=1, source_target_pairs={{0,16},{2,18},{4,20},{6,22},{8,24},{10,26},{12,28},{14,30},{16,32}... | collective-permute-start | bytes 122888 | tf_op jit(solution)/shard_map/ppermute | solution.py:300
  150.9 5.3 %collective-permute-start.17 = (f32[80,128]{1,0:T(8,128)S(1)}, f32[80,128]{1,0:T(8,128)S(1)}, u32[]{:S(2)}, u32[]{:S(2)}) collective-permute-start(f32[80,128]{1,0:T(8,128)S(1)} %reduce_sum.39), channel_id=1, source_target_pairs={{0,48},{2,50},{4,52},{6,54},{8,56},{10,58},{12,60},{14,62},{16,0},... | collective-permute-start | bytes 122888 | tf_op jit(solution)/shard_map/ppermute | solution.py:300
  167.7 2.1 %copy-start.5 = (f32[256,256]{1,0:T(8,128)S(1)}, f32[256,256]{1,0:T(8,128)}, u32[]{:S(2)}) copy-start(f32[256,256]{1,0:T(8,128)} %copy-done.4) | copy-start | bytes 786436
  167.8 4.3 %collective-permute-start.18 = (f32[256,128]{1,0:T(8,128)S(1)}, f32[256,128]{1,0:T(8,128)S(1)}, u32[]{:S(2)}, u32[]{:S(2)}) collective-permute-start(f32[256,128]{1,0:T(8,128)S(1)} %slice.62), channel_id=1, source_target_pairs={{0,1},{1,0},{2,3},{3,2},{4,5},{5,4},{6,7},{7,6},{8,9},{9,8},{10,11... | collective-permute-start | bytes 393224 | tf_op jit(solution)/shard_map/ppermute | solution.py:257
  169.8 6.9 %collective-permute-start.13 = (f32[256,256]{1,0:T(8,128)S(1)}, f32[256,256]{1,0:T(8,128)S(1)}, u32[]{:S(2)}, u32[]{:S(2)}) collective-permute-start(f32[256,256]{1,0:T(8,128)S(1)} %copy-done.5), channel_id=1, source_target_pairs={{0,64},{64,128},{128,192},{1,65},{65,129},{129,193},{2,66},{66,130... | collective-permute-start | bytes 786440 | tf_op jit(solution)/shard_map/ppermute | solution.py:335
  172.6 4.1 %copy-start.3 = (f32[1,256,256]{2,1,0:T(8,128)S(1)}, f32[1,256,256]{2,1,0:T(8,128)}, u32[]{:S(2)}) copy-start(f32[1,256,256]{2,1,0:T(8,128)} %param.3) | copy-start | bytes 786436
  172.7 6.3 %collective-permute-start.19 = (f32[64,512]{1,0:T(8,128)S(1)}, f32[64,512]{1,0:T(8,128)S(1)}, u32[]{:S(2)}, u32[]{:S(2)}) collective-permute-start(f32[64,512]{1,0:T(8,128)S(1)} %get-tuple-element.47), channel_id=1, source_target_pairs={{192,128},{193,129},{194,130},{195,131},{196,132},{197,133},{198,1... | collective-permute-start | bytes 393224 | tf_op jit(solution)/shard_map/ppermute | solution.py:343
  173.5 5.5 %collective-permute-start.20 = (f32[64,512]{1,0:T(8,128)S(1)}, f32[64,512]{1,0:T(8,128)S(1)}, u32[]{:S(2)}, u32[]{:S(2)}) collective-permute-start(f32[64,512]{1,0:T(8,128)S(1)} %get-tuple-element.46), channel_id=1, source_target_pairs={{192,64},{193,65},{194,66},{195,67},{196,68},{197,69},{198,70},{19... | collective-permute-start | bytes 393224 | tf_op jit(solution)/shard_map/ppermute | solution.py:343
  174.2 9.8 %collective-permute-start.21 = (f32[64,512]{1,0:T(8,128)S(1)}, f32[64,512]{1,0:T(8,128)S(1)}, u32[]{:S(2)}, u32[]{:S(2)}) collective-permute-start(f32[64,512]{1,0:T(8,128)S(1)} %get-tuple-element.45), channel_id=1, source_target_pairs={{192,0},{193,1},{194,2},{195,3},{196,4},{197,5},{198,6},{199,7},{2... | collective-permute-start | bytes 393224 | tf_op jit(solution)/shard_map/ppermute | solution.py:343

commit v5 on v4

--- a/solution.py
+++ b/solution.py
@@ -10,7 +10,7 @@
 MODE = 128
 LANES = 128
 BLOCK = 64
-GROUP = 8
+GROUP = 16
 VMEM_LIMIT = 16 * 1024 * 1024
 F32 = jnp.float32
 BF16 = jnp.bfloat16
@@ -45,12 +45,6 @@
     return dot(ah, bh, dims) + (dot(ah, bl, dims) + dot(al, bh, dims))
 
 
-def full(a, b, dims=((1,), (0,))):
-    return lax.dot_general(
-        a, b, (dims, ((), ())), precision=lax.Precision.HIGHEST, preferred_element_type=F32
-    )
-
-
 def pack_gram(out, gram):
     half = gram.shape[0] // 2
     out[0:half, :] = gram[:half, :half]
@@ -69,8 +63,10 @@
     )
 
 
-def prepare_own(own, ch, cl, th, tl):
+def prepare_own(own, up, ch, cl, th, tl, start):
     modes, rank = own.shape[0], own.shape[1]
+    u = split(up[...].T)
+    pack_gram(start, dot3(u, u, ((1,), (1,))))
     for i in range(modes):
         at = pl.ds(i * rank, rank)
         mine = own[i]
@@ -81,12 +77,10 @@
 def prepare_link(which, own, other, th, tl, up, up_other, lh, ll, rh, rl, start, beside):
     modes, rank = own.shape[0], own.shape[1]
     half = rank // 2
-    u, v = up[...], up_other[...]
-    pack_gram(start, full(u, u, ((0,), (0,))))
 
     def sides(left, right, mine, theirs):
-        link = full(left, right, ((0,), (0,)))
-        start[3 * half :, :] = link[:, mine]
+        link = dot3(split(left.T), split(right))
+        start[...] = link[:, mine]
         beside[...] = link[:, theirs]
 
     low, high = slice(0, half), slice(half, rank)
@@ -98,7 +92,7 @@
         for i in range(modes):
             at = pl.ds(i * half, half)
             rh[:, at], rl[:, at] = split(other[i][:, low])
-        sides(u, v, low, high)
+        sides(up[...], up_other[...], low, high)
 
     @pl.when(which[0] != 0)
     def _():
@@ -107,7 +101,7 @@
             rh[:, at], rl[:, at] = split(own[i][:, high])
             at = pl.ds(i * rank, rank)
             lh[:, at], ll[:, at] = split(other[i].T)
-        sides(v, u, high, low)
+        sides(up_other[...], up[...], high, low)
 
 
 def stacked(x, width):
@@ -121,37 +115,41 @@
     return dot3(left, (stacked(mh, width), stacked(ml, width)))
 
 
-def chain_gram(tick, place, state, ch, cl, th, tl, out):
+def chain_gram(state, ch, cl, th, tl, out):
     rank = ch.shape[0]
-
-    @pl.when(place[0] == tick)
-    def _():
-        a, b, c = gram_blocks(state)
-        gram = jnp.concatenate(
-            [jnp.concatenate([a, b], axis=1), jnp.concatenate([b.T, c], axis=1)], axis=0
-        )
-        pack_gram(
-            out, chain_product(split(gram), (ch[...], cl[...]), (th[...], tl[...]), rank)
-        )
+    a, b, c = gram_blocks(state)
+    gram = jnp.concatenate(
+        [jnp.concatenate([a, b], axis=1), jnp.concatenate([b.T, c], axis=1)], axis=0
+    )
+    pack_gram(out, chain_product(split(gram), (ch[...], cl[...]), (th[...], tl[...]), rank))
 
 
 def chain_gram_keep(tick, place, kept, state, ch, cl, th, tl, out, keep):
     mine = place[0] == tick - 1
     keep[...] = jnp.where(mine, state[: keep.shape[0], :], kept[...])
-    chain_gram(tick, place, state, ch, cl, th, tl, out)
-
-
-def chain_link(tick, place, gram, state, beside, lh, ll, rh, rl, out):
+    chain_gram(state, ch, cl, th, tl, out)
+
+
+def chain_gram_last(tick, place, *refs):
+    @pl.when(place[0] == tick)
+    def _():
+        chain_gram(*refs)
+
+
+def chain_link(place, gram, state, beside, lh, ll, rh, rl, out):
     rank = lh.shape[0]
     half = rank // 2
-
+    out[: 3 * half, :] = gram[...]
+    link = whole_link(place[1] == 0, state[state.shape[0] - rank :, :], beside[...])
+    out[3 * half :, :] = chain_product(
+        split(link), (rh[...], rl[...]), (lh[...], ll[...]), half
+    )
+
+
+def chain_link_last(tick, place, *refs):
     @pl.when(place[0] == tick)
     def _():
-        out[: 3 * half, :] = gram[...]
-        link = whole_link(place[1] == 0, state[3 * half :, :], beside[...])
-        out[3 * half :, :] = chain_product(
-            split(link), (rh[...], rl[...]), (lh[...], ll[...]), half
-        )
+        chain_link(place, *refs)
 
 
 def eliminate(m, offset, n):
@@ -274,11 +272,11 @@
     packed, side = ((3 * half + rank, half), F32), ((rank, half), F32)
     square = ((rank, rank), F32)
     scratch = [pltpu.VMEM((rank, 2 * rank), F32)]
-    own_parts = call(prepare_own, [wide] * 4, [VMEM])(own)
-    *link_parts, state, beside = call(
-        prepare_link, [wide] * 2 + [narrow] * 2 + [packed, side], [SMEM] + [VMEM] * 6
+    gram_shape = ((3 * half, half), F32)
+    *own_parts, state = call(prepare_own, [wide] * 4 + [gram_shape], [VMEM] * 2)(own, up)
+    *link_parts, link, beside = call(
+        prepare_link, [wide] * 2 + [narrow] * 2 + [side] * 2, [SMEM] + [VMEM] * 6
     )(scalars(which), own, other, *own_parts[2:], up, up_other)
-    gram_shape = ((3 * half, half), F32)
     near = max(1, rows // 4)
     far = rows // near
     place = scalars(section, which)
@@ -294,15 +292,17 @@
         )
 
     def over_far(x):
-        terms = [x]
-        for step in range(1, far):
-            pairs = [(r, (r + step * near) % rows) for r in range(rows)]
-            terms.append(lax.ppermute(x, "row", pairs))
-        return sum(terms[2::2], terms[0]) + sum(terms[3::2], terms[1])
+        for step in (1, far - 1) if far > 2 else (1,):
+            pairs = [(r, (r // near ^ step) * near + r % near) for r in range(rows)]
+            x = x + lax.ppermute(x, "row", pairs)
+        return x
 
     kept = None
     for tick in range(sections):
-        if 0 < tick < last:
+        if tick == 0:
+            (gram,) = call(chain_gram, [gram_shape], [VMEM] * 5)(state, *own_parts)
+            kept = gram
+        elif tick < last:
             gram, kept = call(
                 functools.partial(chain_gram_keep, tick),
                 [gram_shape] * 2,
@@ -310,19 +310,21 @@
             )(place, kept, state, *own_parts)
         else:
             (gram,) = call(
-                functools.partial(chain_gram, tick), [gram_shape], [SMEM] + [VMEM] * 5
+                functools.partial(chain_gram_last, tick), [gram_shape], [SMEM] + [VMEM] * 5
             )(place, state, *own_parts)
-            kept = gram if tick == 0 else kept
-        (partial,) = call(
-            functools.partial(chain_link, tick), [packed], [SMEM] + [VMEM] * 7
-        )(place, gram, state, beside, *link_parts)
+        body = functools.partial(chain_link_last, tick) if tick == last else chain_link
+        (partial,) = call(body, [packed], [SMEM] + [VMEM] * 7)(
+            place, gram, link, beside, *link_parts
+        )
         pair = (tick, tick + 1) if tick < last else None
         count = near * (2 if pair else 1)
         arrived = exchange(partial.reshape(count, -1, half), pair)
         piece = over_far(arrived[:near].sum(axis=0))
+        if tick == last:
+            piece, u_before = lax.optimization_barrier((piece, u_before))
         copies = jnp.broadcast_to(piece[None], arrived.shape)
         state = exchange(copies, pair).reshape(partial.shape)
-        beside = swapped(state[3 * half :])
+        link, beside = state, swapped(state[3 * half :])
         if tick == last - 1:
             u_own, x_own = call(
                 factor_own,
@@ -332,6 +334,7 @@
                 HBM,
             )(scalars(section, last), kept, state)
             state, u_own, x_own = lax.optimization_barrier((state, u_own, x_own))
+            link = state
             u_before = lax.ppermute(u_own, "cores", [(k, k + 1) for k in range(last)])
             u_before = jnp.where(section == 0, up, u_before)
 

time: 185 us -> 190 us (1.027)
  blocking collectives: 89.6 us -> 80 us
  waiting for transfers between devices: 18 us -> 23 us
  starting transfers between devices: 50.4 us -> 55 us
  Pallas kernels: 21.7 us -> 25.7 us
    all_to_all x2 -> x1, blocking collectives: 21.7 us -> 10.3 us  [exchange(): return lax.all_to_all(x, 'row', 0, 0, tiled=True, axis_index_groups=blocks)]
    all_to_all x0 -> x1, waiting for transfers between devices: none -> 5.03 us  [exchange(): return lax.all_to_all(x, 'row', 0, 0, tiled=True, axis_index_groups=blocks)]
    ppermute x6, starting transfers between devices: 18.2 us -> 22.4 us  [swapped(): return lax.ppermute(x, 'tensor', [(0, 1), (1, 0)])]
    all_to_all x0 -> x1, starting transfers between devices: none -> 3.56 us  [exchange(): return lax.all_to_all(x, 'row', 0, 0, tiled=True, axis_index_groups=blocks)]
    pallas_call x2, Pallas kernels: 1.12 us -> 4.48 us  [shards(): call(functools.partial(chain_gram_keep, tick), [gram_shape] * 2, [SMEM] +...]
    ppermute x12 -> x8, starting transfers between devices: 27.3 us -> 24.2 us  [over_far(): x = x + lax.ppermute(x, 'row', pairs)]
    ppermute x12 -> x8, waiting for transfers between devices: 9.7 us -> 12.1 us  [over_far(): x = x + lax.ppermute(x, 'row', pairs)]
    unnamed x12 -> x20, local copies, waits for them, and re-layouts: 2.89 us -> 4.01 us
  transfers between devices with their start and end apart: 22 -> 19, of which waited for: 13 -> 11; matrix products, arithmetic and copies ran while one was open for 0% -> 0% of each run, Pallas kernels for 8% -> 9%
where the time goes in v5:
time: 190 us
  blocking collectives  80 us (42%)
  starting transfers between devices  55 us (29%)
  Pallas kernels  25.7 us (14%)
  waiting for transfers between devices  23 us (12%)
  local copies, waits for them, and re-layouts  4.84 us (3%)
    all_to_all x6, blocking collectives, exchange(): lax.all_to_all(x, ('cores', 'row'), 0, 0, tiled=True, axis_index_groups=g...  69.7 us
    ppermute x8, starting transfers between devices, over_far(): x = x + lax.ppermute(x, 'row', pairs)  24.2 us
    ppermute x6, starting transfers between devices, swapped(): return lax.ppermute(x, 'tensor', [(0, 1), (1, 0)])  22.4 us
    ppermute x8, waiting for transfers between devices, over_far(): x = x + lax.ppermute(x, 'row', pairs)  12.1 us
    all_to_all x1, blocking collectives, exchange(): return lax.all_to_all(x, 'row', 0, 0, tiled=True, axis_index_groups=blocks)  10.3 us
    pallas_call x1, Pallas kernels, shards(): call(factor_own, [square] * 2, [SMEM] + [HBM] * 2, scratch + [pltpu.VMEM(...  8.25 us
    pallas_call x4, Pallas kernels, shards(): call(body, [packed], [SMEM] + [VMEM] * 7)  5.68 us
    all_to_all x1, waiting for transfers between devices, exchange(): return lax.all_to_all(x, 'row', 0, 0, tiled=True, axis_index_groups=blocks)  5.03 us
  transfers between devices with their start and end apart: 19, of which 11 were waited for; matrix products, arithmetic and copies ran while one was open for 0% of the time, Pallas kernels for 9%

profile of v5, /device:TPU:1, one launch (start us, length us, event | category | flops | bytes accessed | tf_op | source)
XLA Modules:
  0.0 189.7 jit_solution(3691449301155107448)
XLA Ops:
  0.6 3.3 %collective-permute-start = (f32[4,256,256]{2,1,0:T(8,128)}, f32[4,256,256]{2,1,0:T(8,128)}, u32[]{:S(2)}, u32[]{:S(2)}) collective-permute-start(f32[4,256,256]{2,1,0:T(8,128)} %bitcast.19), channel_id=1, source_target_pairs={{0,1},{1,0},{2,3},{3,2},{4,5},{5,4},{6,7},{7,6},{8,9},{9,8},{10,11... | collective-permute-start | bytes 3145736 | tf_op jit(solution)/shard_map/ppermute | solution.py:255
  4.0 0.1 collective-permute-start.1
  4.1 1.2 copy-done
  5.3 0.9 copy-done.2
  6.2 0.5 shard_map.49
  6.7 0.0 copy-start.6
  6.7 0.7 copy-done.6
  7.4 0.9 copy-done.7
  8.3 1.7 shard_map.50.gram.kept
  10.0 0.1 pad_add_fusion.2.place
  10.1 0.0 collective-permute-done.1.up_other
  10.1 0.0 collective-permute-done.other
  10.1 1.8 shard_map.51
  11.9 1.5 shard_map.52
  13.4 13.0 %all_to_all.40 = f32[16,40,128]{2,1,0:T(8,128)S(1)} all-to-all(f32[16,40,128]{2,1,0:T(8,128)S(1)} %bitcast.38), channel_id=1, replica_groups={{0,2,4,6,8,10,12,14,64,66,68,70,72,74,76,78},{16,18,20,22,24,26,28,30,8..., dimensions={0} | all-to-all | bytes 655360 | tf_op jit(solution)/shard_map/all_to_all | solution.py:290
  26.4 3.1 %collective-permute-start.2 = (f32[40,128]{1,0:T(8,128)S(1)}, f32[40,128]{1,0:T(8,128)S(1)}, u32[]{:S(2)}, u32[]{:S(2)}) collective-permute-start(f32[40,128]{1,0:T(8,128)S(1)} %slice_reduce_fusion.2), channel_id=1, source_target_pairs={{0,16},{2,18},{4,20},{6,22},{8,24},{10,26},{12,28},{14,30},{16,0},... | collective-permute-start | bytes 61448 | tf_op jit(solution)/shard_map/ppermute | solution.py:297
  29.5 1.2 collective-permute-done.2
  30.7 4.5 %collective-permute-start.3 = (f32[40,128]{1,0:T(8,128)S(1)}, f32[40,128]{1,0:T(8,128)S(1)}, u32[]{:S(2)}, u32[]{:S(2)}) collective-permute-start(f32[40,128]{1,0:T(8,128)S(1)} %add.24), channel_id=1, source_target_pairs={{0,48},{2,50},{4,52},{6,54},{8,56},{10,58},{12,60},{14,62},{16,32}... | collective-permute-start | bytes 61448 | tf_op jit(solution)/shard_map/ppermute | solution.py:297
  35.2 1.2 collective-permute-done.3
  36.4 10.2 %all_to_all.41 = f32[16,40,128]{2,1,0:T(8,128)S(1)} all-to-all(f32[16,40,128]{2,1,0:T(8,128)S(1)} %broadcast_in_dim.14), channel_id=1, replica_groups={{0,2,4,6,8,10,12,14,64,66,68,70,72,74,76,78},{16,18,20,22,24,26,28,30,8..., dimensions={0} | all-to-all | bytes 655360 | tf_op jit(solution)/shard_map/all_to_all | solution.py:290
  46.6 4.9 %collective-permute-start.4 = (f32[256,128]{1,0:T(8,128)S(1)}, f32[256,128]{1,0:T(8,128)S(1)}, u32[]{:S(2)}, u32[]{:S(2)}) collective-permute-start(f32[256,128]{1,0:T(8,128)S(1)} %slice.57), channel_id=1, source_target_pairs={{0,1},{1,0},{2,3},{3,2},{4,5},{5,4},{6,7},{7,6},{8,9},{9,8},{10,11... | collective-permute-start | bytes 393224 | tf_op jit(solution)/shard_map/ppermute | solution.py:255
  51.5 2.2 %shard_map.53 = (f32[384,128]{1,0:T(8,128)S(1)}, f32[384,128]{1,0:T(8,128)S(1)}) custom-call(s32[2]{0:T(128)S(1)} %pad_add_fusion.2.place, f32[384,128]{1,0:T(8,128)S(1)} %shard_map.50.gram.kept, f32[640,128]{1,0:T(8,128)S(1)} %bitcast.31, bf16[256,1024]{1,0:T(8,128)(2,1)S(1)} %get-tuple-element.28.ch.refs_1_, ...), custom_call_target="tpu_custom_call" | custom-call | tf_op jit(solution)/shard_map/pallas_call | solution.py:306
  53.7 0.0 collective-permute-done.4.beside
  53.8 1.5 shard_map.54
  55.2 13.3 %all_to_all.42 = f32[16,40,128]{2,1,0:T(8,128)S(1)} all-to-all(f32[16,40,128]{2,1,0:T(8,128)S(1)} %bitcast.39), channel_id=1, replica_groups={{64,66,68,70,72,74,76,78,128,130,132,134,136,138,140,142},{80,82,84,86,..., dimensions={0} | all-to-all | bytes 655360 | tf_op jit(solution)/shard_map/all_to_all | solution.py:290
  68.6 1.8 collective-permute-start.5
  70.4 1.8 collective-permute-done.5
  72.2 3.9 %collective-permute-start.6 = (f32[40,128]{1,0:T(8,128)S(1)}, f32[40,128]{1,0:T(8,128)S(1)}, u32[]{:S(2)}, u32[]{:S(2)}) collective-permute-start(f32[40,128]{1,0:T(8,128)S(1)} %add.26), channel_id=1, source_target_pairs={{0,48},{2,50},{4,52},{6,54},{8,56},{10,58},{12,60},{14,62},{16,32}... | collective-permute-start | bytes 61448 | tf_op jit(solution)/shard_map/ppermute | solution.py:297
  76.1 1.2 collective-permute-done.6
  77.3 11.4 %all_to_all.43 = f32[16,40,128]{2,1,0:T(8,128)S(1)} all-to-all(f32[16,40,128]{2,1,0:T(8,128)S(1)} %broadcast_in_dim.15), channel_id=1, replica_groups={{64,66,68,70,72,74,76,78,128,130,132,134,136,138,140,142},{80,82,84,86,..., dimensions={0} | all-to-all | bytes 655360 | tf_op jit(solution)/shard_map/all_to_all | solution.py:290
  88.7 5.0 %collective-permute-start.7 = (f32[256,128]{1,0:T(8,128)S(1)}, f32[256,128]{1,0:T(8,128)S(1)}, u32[]{:S(2)}, u32[]{:S(2)}) collective-permute-start(f32[256,128]{1,0:T(8,128)S(1)} %slice.59), channel_id=1, source_target_pairs={{0,1},{1,0},{2,3},{3,2},{4,5},{5,4},{6,7},{7,6},{8,9},{9,8},{10,11... | collective-permute-start | bytes 393224 | tf_op jit(solution)/shard_map/ppermute | solution.py:255
  93.7 2.2 %shard_map.55 = (f32[384,128]{1,0:T(8,128)S(1)}, f32[384,128]{1,0:T(8,128)S(1)}) custom-call(s32[2]{0:T(128)S(1)} %pad_add_fusion.2.place, f32[384,128]{1,0:T(8,128)S(1)} %get-tuple-element.38.kept, f32[640,128]{1,0:T(8,128)S(1)} %bitcast.28, bf16[256,1024]{1,0:T(8,128)(2,1)S(1)} %get-tuple-element.28.ch.refs_1_, ...), custom_call_target="tpu_custom_call" | custom-call | tf_op jit(solution)/shard_map/pallas_call | solution.py:306
  95.9 1.5 shard_map.56
  97.4 11.5 %all_to_all.44 = f32[16,40,128]{2,1,0:T(8,128)S(1)} all-to-all(f32[16,40,128]{2,1,0:T(8,128)S(1)} %bitcast.40), channel_id=1, replica_groups={{128,130,132,134,136,138,140,142,192,194,196,198,200,202,204,206},{144,..., dimensions={0} | all-to-all | bytes 655360 | tf_op jit(solution)/shard_map/all_to_all | solution.py:290
  109.0 1.6 collective-permute-start.8
  110.6 2.0 %collective-permute-done.8 = f32[40,128]{1,0:T(8,128)S(1)} collective-permute-done((f32[40,128]{1,0:T(8,128)S(1)}, f32[40,128]{1,0:T(8,128)S(1)}, u32[]{:S(2)}, u32[]{:S(2)}) %collective-permute-start.8) | collective-permute-done | bytes 20512 | tf_op jit(solution)/shard_map/ppermute | solution.py:297
  112.6 3.7 %collective-permute-start.9 = (f32[40,128]{1,0:T(8,128)S(1)}, f32[40,128]{1,0:T(8,128)S(1)}, u32[]{:S(2)}, u32[]{:S(2)}) collective-permute-start(f32[40,128]{1,0:T(8,128)S(1)} %add.28), channel_id=1, source_target_pairs={{0,48},{2,50},{4,52},{6,54},{8,56},{10,58},{12,60},{14,62},{16,32}... | collective-permute-start | bytes 61448 | tf_op jit(solution)/shard_map/ppermute | solution.py:297
  116.3 1.2 collective-permute-done.9
  117.5 10.2 %all_to_all.45 = f32[16,40,128]{2,1,0:T(8,128)S(1)} all-to-all(f32[16,40,128]{2,1,0:T(8,128)S(1)} %broadcast_in_dim.16), channel_id=1, replica_groups={{128,130,132,134,136,138,140,142,192,194,196,198,200,202,204,206},{144,..., dimensions={0} | all-to-all | bytes 655360 | tf_op jit(solution)/shard_map/all_to_all | solution.py:290
  127.7 4.5 %collective-permute-start.10 = (f32[256,128]{1,0:T(8,128)S(1)}, f32[256,128]{1,0:T(8,128)S(1)}, u32[]{:S(2)}, u32[]{:S(2)}) collective-permute-start(f32[256,128]{1,0:T(8,128)S(1)} %slice.61), channel_id=1, source_target_pairs={{0,1},{1,0},{2,3},{3,2},{4,5},{5,4},{6,7},{7,6},{8,9},{9,8},{10,11... | collective-permute-start | bytes 393224 | tf_op jit(solution)/shard_map/ppermute | solution.py:255
  132.2 0.1 pad_add_fusion.section
  132.3 8.2 %shard_map.57 = (f32[256,256]{1,0:T(8,128)S(1)}, f32[256,256]{1,0:T(8,128)S(1)}) custom-call(s32[2]{0:T(128)S(1)} %pad_add_fusion.section, f32[384,128]{1,0:T(8,128)S(1)} %get-tuple-element.41.kept, f32[640,128]{1,0:T(8,128)S(1)} %bitcast.24), custom_call_target="tpu_custom_call" | custom-call | tf_op jit(solution)/shard_map/pallas_call | solution.py:329
  140.5 0.6 shard_map.58.refs_0_
  141.1 0.1 copy-done.4
  141.2 0.1 copy-done.8
  141.3 1.3 shard_map.59
  142.6 3.6 %all-to-all-start.6 = ((f32[8,80,128]{2,1,0:T(8,128)}), f32[8,80,128]{2,1,0:T(8,128)S(1)}, u32[]{:S(2)}, u32[]{:S(2)}) async-start(f32[8,80,128]{2,1,0:T(8,128)} %bitcast.10), calls=%async_computation.6 | async-start | bytes 655360 | tf_op jit(solution)/shard_map/all_to_all | solution.py:287
  146.2 2.2 %collective-permute-start.13 = (f32[256,256]{1,0:T(8,128)S(1)}, f32[256,256]{1,0:T(8,128)S(1)}, u32[]{:S(2)}, u32[]{:S(2)}) collective-permute-start(f32[256,256]{1,0:T(8,128)S(1)} %copy-done.9), channel_id=1, source_target_pairs={{0,64},{64,128},{128,192},{1,65},{65,129},{129,193},{2,66},{66,130... | collective-permute-start | bytes 786440 | tf_op jit(solution)/shard_map/ppermute | solution.py:338
  148.4 5.0 %all-to-all-done.6 = f32[8,80,128]{2,1,0:T(8,128)S(1)} async-done(((f32[8,80,128]{2,1,0:T(8,128)}), f32[8,80,128]{2,1,0:T(8,128)S(1)}, u32[]{:S(2)}, u32[]{:S(2)}) %all-to-all-start.6) | async-done | bytes 327712 | tf_op jit(solution)/shard_map/all_to_all | solution.py:287
  153.4 1.9 collective-permute-start.11
  155.3 2.2 %collective-permute-done.11 = f32[80,128]{1,0:T(8,128)S(1)} collective-permute-done((f32[80,128]{1,0:T(8,128)S(1)}, f32[80,128]{1,0:T(8,128)S(1)}, u32[]{:S(2)}, u32[]{:S(2)}) %collective-permute-start.11) | collective-permute-done | bytes 40992 | tf_op jit(solution)/shard_map/ppermute | solution.py:297
  157.5 3.8 %collective-permute-start.12 = (f32[80,128]{1,0:T(8,128)S(1)}, f32[80,128]{1,0:T(8,128)S(1)}, u32[]{:S(2)}, u32[]{:S(2)}) collective-permute-start(f32[80,128]{1,0:T(8,128)S(1)} %add.30), channel_id=1, source_target_pairs={{0,48},{2,50},{4,52},{6,54},{8,56},{10,58},{12,60},{14,62},{16,32}... | collective-permute-start | bytes 122888 | tf_op jit(solution)/shard_map/ppermute | solution.py:297
  161.3 1.4 collective-permute-done.12
  162.7 10.3 %all_to_all.46 = f32[8,80,128]{2,1,0:T(8,128)S(1)} all-to-all(f32[8,80,128]{2,1,0:T(8,128)S(1)} %broadcast_in_dim.17), channel_id=1, replica_groups={{0,2,4,6,8,10,12,14},{16,18,20,22,24,26,28,30},{32,34,36,38,40,42,44,46..., dimensions={0} | all-to-all | bytes 655360 | tf_op jit(solution)/shard_map/all_to_all | solution.py:287
  173.0 4.6 %collective-permute-start.14 = (f32[256,128]{1,0:T(8,128)S(1)}, f32[256,128]{1,0:T(8,128)S(1)}, u32[]{:S(2)}, u32[]{:S(2)}) collective-permute-start(f32[256,128]{1,0:T(8,128)S(1)} %slice.62), channel_id=1, source_target_pairs={{0,1},{1,0},{2,3},{3,2},{4,5},{5,4},{6,7},{7,6},{8,9},{9,8},{10,11... | collective-permute-start | bytes 393224 | tf_op jit(solution)/shard_map/ppermute | solution.py:255
  177.6 0.1 pad_add_fusion.1.flags
  177.7 0.9 collective-permute-done.14.beside
  178.6 0.6 shard_map.60
  179.2 0.7 collective-permute-start.15
  179.9 0.7 collective-permute-start.16
  180.5 1.3 collective-permute-start.17
  181.8 2.2 %shard_map.61 = f32[4,256,256]{2,1,0:T(8,128)} custom-call(f32[4,256,256]{2,1,0:T(8,128)S(1)} %bitcast.22, f32[256,256]{1,0:T(8,128)S(1)} %broadcast_select_fusion.upper, f32[256,256]{1,0:T(8,128)S(1)} %get-tuple-element.49.inverse), custom_call_target="tpu_custom_call" | custom-call | tf_op jit(solution)/shard_map/pallas_call | solution.py:347
  184.1 4.9 %collective-permute-done.17 = f32[64,512]{1,0:T(8,128)S(1)} collective-permute-done((f32[64,512]{1,0:T(8,128)S(1)}, f32[64,512]{1,0:T(8,128)S(1)}, u32[]{:S(2)}, u32[]{:S(2)}) %collective-permute-start.17) | collective-permute-done | bytes 131104 | tf_op jit(solution)/shard_map/ppermute | solution.py:346
  189.0 0.7 slice_bitcast_fusion
  (41 shorter events, 0.4 us)
Async XLA Ops:
  0.6 9.5 %collective-permute-start = (f32[4,256,256]{2,1,0:T(8,128)}, f32[4,256,256]{2,1,0:T(8,128)}, u32[]{:S(2)}, u32[]{:S(2)}) collective-permute-start(f32[4,256,256]{2,1,0:T(8,128)} %bitcast.19), channel_id=1, source_target_pairs={{0,1},{1,0},{2,3},{3,2},{4,5},{5,4},{6,7},{7,6},{8,9},{9,8},{10,11... | collective-permute-start | bytes 3145736 | tf_op jit(solution)/shard_map/ppermute | solution.py:255
  4.0 6.1 %collective-permute-start.1 = (f32[256,256]{1,0:T(8,128)}, f32[256,256]{1,0:T(8,128)}, u32[]{:S(2)}, u32[]{:S(2)}) collective-permute-start(f32[256,256]{1,0:T(8,128)} %bitcast.33), channel_id=1, source_target_pairs={{0,1},{1,0},{2,3},{3,2},{4,5},{5,4},{6,7},{7,6},{8,9},{9,8},{10,11... | collective-permute-start | bytes 786440 | tf_op jit(solution)/shard_map/ppermute | solution.py:255
  4.1 1.2 copy-start
  5.3 0.9 copy-start.2
  6.7 0.7 copy-start.6
  7.4 0.9 copy-start.7
  8.3 1.8 copy-start.1
  8.3 1.8 copy-start.3
  26.4 4.2 %collective-permute-start.2 = (f32[40,128]{1,0:T(8,128)S(1)}, f32[40,128]{1,0:T(8,128)S(1)}, u32[]{:S(2)}, u32[]{:S(2)}) collective-permute-start(f32[40,128]{1,0:T(8,128)S(1)} %slice_reduce_fusion.2), channel_id=1, source_target_pairs={{0,16},{2,18},{4,20},{6,22},{8,24},{10,26},{12,28},{14,30},{16,0},... | collective-permute-start | bytes 61448 | tf_op jit(solution)/shard_map/ppermute | solution.py:297
  30.7 5.7 %collective-permute-start.3 = (f32[40,128]{1,0:T(8,128)S(1)}, f32[40,128]{1,0:T(8,128)S(1)}, u32[]{:S(2)}, u32[]{:S(2)}) collective-permute-start(f32[40,128]{1,0:T(8,128)S(1)} %add.24), channel_id=1, source_target_pairs={{0,48},{2,50},{4,52},{6,54},{8,56},{10,58},{12,60},{14,62},{16,32}... | collective-permute-start | bytes 61448 | tf_op jit(solution)/shard_map/ppermute | solution.py:297
  46.6 7.2 %collective-permute-start.4 = (f32[256,128]{1,0:T(8,128)S(1)}, f32[256,128]{1,0:T(8,128)S(1)}, u32[]{:S(2)}, u32[]{:S(2)}) collective-permute-start(f32[256,128]{1,0:T(8,128)S(1)} %slice.57), channel_id=1, source_target_pairs={{0,1},{1,0},{2,3},{3,2},{4,5},{5,4},{6,7},{7,6},{8,9},{9,8},{10,11... | collective-permute-start | bytes 393224 | tf_op jit(solution)/shard_map/ppermute | solution.py:255
  68.6 3.6 %collective-permute-start.5 = (f32[40,128]{1,0:T(8,128)S(1)}, f32[40,128]{1,0:T(8,128)S(1)}, u32[]{:S(2)}, u32[]{:S(2)}) collective-permute-start(f32[40,128]{1,0:T(8,128)S(1)} %slice_reduce_fusion.1), channel_id=1, source_target_pairs={{0,16},{2,18},{4,20},{6,22},{8,24},{10,26},{12,28},{14,30},{16,0},... | collective-permute-start | bytes 61448 | tf_op jit(solution)/shard_map/ppermute | solution.py:297
  72.2 5.0 %collective-permute-start.6 = (f32[40,128]{1,0:T(8,128)S(1)}, f32[40,128]{1,0:T(8,128)S(1)}, u32[]{:S(2)}, u32[]{:S(2)}) collective-permute-start(f32[40,128]{1,0:T(8,128)S(1)} %add.26), channel_id=1, source_target_pairs={{0,48},{2,50},{4,52},{6,54},{8,56},{10,58},{12,60},{14,62},{16,32}... | collective-permute-start | bytes 61448 | tf_op jit(solution)/shard_map/ppermute | solution.py:297
  88.7 7.2 %collective-permute-start.7 = (f32[256,128]{1,0:T(8,128)S(1)}, f32[256,128]{1,0:T(8,128)S(1)}, u32[]{:S(2)}, u32[]{:S(2)}) collective-permute-start(f32[256,128]{1,0:T(8,128)S(1)} %slice.59), channel_id=1, source_target_pairs={{0,1},{1,0},{2,3},{3,2},{4,5},{5,4},{6,7},{7,6},{8,9},{9,8},{10,11... | collective-permute-start | bytes 393224 | tf_op jit(solution)/shard_map/ppermute | solution.py:255
  109.0 3.6 %collective-permute-start.8 = (f32[40,128]{1,0:T(8,128)S(1)}, f32[40,128]{1,0:T(8,128)S(1)}, u32[]{:S(2)}, u32[]{:S(2)}) collective-permute-start(f32[40,128]{1,0:T(8,128)S(1)} %slice_reduce_fusion), channel_id=1, source_target_pairs={{0,16},{2,18},{4,20},{6,22},{8,24},{10,26},{12,28},{14,30},{16,0},... | collective-permute-start | bytes 61448 | tf_op jit(solution)/shard_map/ppermute | solution.py:297
  112.6 4.9 %collective-permute-start.9 = (f32[40,128]{1,0:T(8,128)S(1)}, f32[40,128]{1,0:T(8,128)S(1)}, u32[]{:S(2)}, u32[]{:S(2)}) collective-permute-start(f32[40,128]{1,0:T(8,128)S(1)} %add.28), channel_id=1, source_target_pairs={{0,48},{2,50},{4,52},{6,54},{8,56},{10,58},{12,60},{14,62},{16,32}... | collective-permute-start | bytes 61448 | tf_op jit(solution)/shard_map/ppermute | solution.py:297
  127.7 13.6 %collective-permute-start.10 = (f32[256,128]{1,0:T(8,128)S(1)}, f32[256,128]{1,0:T(8,128)S(1)}, u32[]{:S(2)}, u32[]{:S(2)}) collective-permute-start(f32[256,128]{1,0:T(8,128)S(1)} %slice.61), channel_id=1, source_target_pairs={{0,1},{1,0},{2,3},{3,2},{4,5},{5,4},{6,7},{7,6},{8,9},{9,8},{10,11... | collective-permute-start | bytes 393224 | tf_op jit(solution)/shard_map/ppermute | solution.py:255
  140.5 0.7 copy-start.4
  140.5 0.8 copy-start.8
  142.6 3.6 %copy-start.9 = (f32[256,256]{1,0:T(8,128)S(1)}, f32[256,256]{1,0:T(8,128)}, u32[]{:S(2)}) copy-start(f32[256,256]{1,0:T(8,128)} %copy-done.8) | copy-start | bytes 786436
  142.6 10.8 %all-to-all-start.6 = ((f32[8,80,128]{2,1,0:T(8,128)}), f32[8,80,128]{2,1,0:T(8,128)S(1)}, u32[]{:S(2)}, u32[]{:S(2)}) async-start(f32[8,80,128]{2,1,0:T(8,128)} %bitcast.10), calls=%async_computation.6 | async-start | bytes 655360 | tf_op jit(solution)/shard_map/all_to_all | solution.py:287
  146.2 15.1 %collective-permute-start.13 = (f32[256,256]{1,0:T(8,128)S(1)}, f32[256,256]{1,0:T(8,128)S(1)}, u32[]{:S(2)}, u32[]{:S(2)}) collective-permute-start(f32[256,256]{1,0:T(8,128)S(1)} %copy-done.9), channel_id=1, source_target_pairs={{0,64},{64,128},{128,192},{1,65},{65,129},{129,193},{2,66},{66,130... | collective-permute-start | bytes 786440 | tf_op jit(solution)/shard_map/ppermute | solution.py:338
  153.4 4.1 %collective-permute-start.11 = (f32[80,128]{1,0:T(8,128)S(1)}, f32[80,128]{1,0:T(8,128)S(1)}, u32[]{:S(2)}, u32[]{:S(2)}) collective-permute-start(f32[80,128]{1,0:T(8,128)S(1)} %reduce_sum.39), channel_id=1, source_target_pairs={{0,16},{2,18},{4,20},{6,22},{8,24},{10,26},{12,28},{14,30},{16,0},... | collective-permute-start | bytes 122888 | tf_op jit(solution)/shard_map/ppermute | solution.py:297
  157.5 5.2 %collective-permute-start.12 = (f32[80,128]{1,0:T(8,128)S(1)}, f32[80,128]{1,0:T(8,128)S(1)}, u32[]{:S(2)}, u32[]{:S(2)}) collective-permute-start(f32[80,128]{1,0:T(8,128)S(1)} %add.30), channel_id=1, source_target_pairs={{0,48},{2,50},{4,52},{6,54},{8,56},{10,58},{12,60},{14,62},{16,32}... | collective-permute-start | bytes 122888 | tf_op jit(solution)/shard_map/ppermute | solution.py:297
  173.0 5.6 %copy-start.5 = (f32[256,256]{1,0:T(8,128)S(1)}, f32[256,256]{1,0:T(8,128)}, u32[]{:S(2)}) copy-start(f32[256,256]{1,0:T(8,128)} %copy-done.4) | copy-start | bytes 786436
  173.0 5.6 %collective-permute-start.14 = (f32[256,128]{1,0:T(8,128)S(1)}, f32[256,128]{1,0:T(8,128)S(1)}, u32[]{:S(2)}, u32[]{:S(2)}) collective-permute-start(f32[256,128]{1,0:T(8,128)S(1)} %slice.62), channel_id=1, source_target_pairs={{0,1},{1,0},{2,3},{3,2},{4,5},{5,4},{6,7},{7,6},{8,9},{9,8},{10,11... | collective-permute-start | bytes 393224 | tf_op jit(solution)/shard_map/ppermute | solution.py:255
  179.2 4.9 %collective-permute-start.15 = (f32[64,512]{1,0:T(8,128)S(1)}, f32[64,512]{1,0:T(8,128)S(1)}, u32[]{:S(2)}, u32[]{:S(2)}) collective-permute-start(f32[64,512]{1,0:T(8,128)S(1)} %get-tuple-element.53), channel_id=1, source_target_pairs={{192,128},{193,129},{194,130},{195,131},{196,132},{197,133},{198,1... | collective-permute-start | bytes 393224 | tf_op jit(solution)/shard_map/ppermute | solution.py:346
  179.9 4.2 %collective-permute-start.16 = (f32[64,512]{1,0:T(8,128)S(1)}, f32[64,512]{1,0:T(8,128)S(1)}, u32[]{:S(2)}, u32[]{:S(2)}) collective-permute-start(f32[64,512]{1,0:T(8,128)S(1)} %get-tuple-element.52), channel_id=1, source_target_pairs={{192,64},{193,65},{194,66},{195,67},{196,68},{197,69},{198,70},{19... | collective-permute-start | bytes 393224 | tf_op jit(solution)/shard_map/ppermute | solution.py:346
  180.5 8.5 %collective-permute-start.17 = (f32[64,512]{1,0:T(8,128)S(1)}, f32[64,512]{1,0:T(8,128)S(1)}, u32[]{:S(2)}, u32[]{:S(2)}) collective-permute-start(f32[64,512]{1,0:T(8,128)S(1)} %get-tuple-element.51), channel_id=1, source_target_pairs={{192,0},{193,1},{194,2},{195,3},{196,4},{197,5},{198,6},{199,7},{2... | collective-permute-start | bytes 393224 | tf_op jit(solution)/shard_map/ppermute | solution.py:346

commit v6 on v4

--- a/solution.py
+++ b/solution.py
@@ -141,14 +141,14 @@
     chain_gram(tick, place, state, ch, cl, th, tl, out)
 
 
-def chain_link(tick, place, gram, state, beside, lh, ll, rh, rl, out):
+def chain_link(tick, place, which, gram, state, beside, lh, ll, rh, rl, out):
     rank = lh.shape[0]
     half = rank // 2
 
     @pl.when(place[0] == tick)
     def _():
         out[: 3 * half, :] = gram[...]
-        link = whole_link(place[1] == 0, state[3 * half :, :], beside[...])
+        link = whole_link(which[0] == 0, state[3 * half :, :], beside[...])
         out[3 * half :, :] = chain_product(
             split(link), (rh[...], rl[...]), (lh[...], ll[...]), half
         )
@@ -281,7 +281,7 @@
     gram_shape = ((3 * half, half), F32)
     near = max(1, rows // 4)
     far = rows // near
-    place = scalars(section, which)
+    place = scalars(section)
 
     def exchange(x, pair):
         blocks = [[g * near + j for j in range(near)] for g in range(far)]
@@ -314,8 +314,8 @@
             )(place, state, *own_parts)
             kept = gram if tick == 0 else kept
         (partial,) = call(
-            functools.partial(chain_link, tick), [packed], [SMEM] + [VMEM] * 7
-        )(place, gram, state, beside, *link_parts)
+            functools.partial(chain_link, tick), [packed], [SMEM] * 2 + [VMEM] * 7
+        )(place, scalars(which), gram, state, beside, *link_parts)
         pair = (tick, tick + 1) if tick < last else None
         count = near * (2 if pair else 1)
         arrived = exchange(partial.reshape(count, -1, half), pair)

time: 185 us -> 181 us (0.978)
  Pallas kernels: 21.7 us -> 17.1 us
    pallas_call x4, Pallas kernels: 3.34 us -> 0.94 us  [shards(): call(functools.partial(chain_link, tick), [packed], [SMEM] * 2 + [VMEM] * 7)]
  transfers between devices with their start and end apart: 22 -> 22, of which waited for: 13 -> 13; matrix products, arithmetic and copies ran while one was open for 0% -> 0% of each run, Pallas kernels for 8% -> 7%
where the time goes in v6:
time: 181 us; the launch traced here: 180 us
  blocking collectives  90 us (50%)
  starting transfers between devices  50.4 us (28%)
  waiting for transfers between devices  17.7 us (10%)
  Pallas kernels  17.1 us (9%)
  local copies, waits for them, and re-layouts  3.71 us (2%)
    all_to_all x6, blocking collectives, exchange(): lax.all_to_all(x, ('cores', 'row'), 0, 0, tiled=True, axis_index_groups=g...  67.9 us
    ppermute x12, starting transfers between devices, over_far(): terms.append(lax.ppermute(x, 'row', pairs))  27.3 us
    all_to_all x2, blocking collectives, exchange(): return lax.all_to_all(x, 'row', 0, 0, tiled=True, axis_index_groups=blocks)  22.1 us
    ppermute x6, starting transfers between devices, swapped(): return lax.ppermute(x, 'tensor', [(0, 1), (1, 0)])  18.2 us
    ppermute x12, waiting for transfers between devices, over_far(): terms.append(lax.ppermute(x, 'row', pairs))  9.29 us
    pallas_call x1, Pallas kernels, shards(): call(factor_own, [square] * 2, [SMEM] + [HBM] * 2, scratch + [pltpu.VMEM(...  9.13 us
    ppermute x3, waiting for transfers between devices, shards(): sent = [lax.ppermute(tiles[k], 'cores', [(last, k)]) for k in range(last)]  3.96 us
  transfers between devices with their start and end apart: 22, of which 13 were waited for; matrix products, arithmetic and copies ran while one was open for 0% of the time, Pallas kernels for 7%

profile of v6, /device:TPU:1, one launch (start us, length us, event | category | flops | bytes accessed | tf_op | source)
XLA Modules:
  0.0 180.1 jit_solution(16019466757972723384)
XLA Ops:
  0.6 3.3 %collective-permute-start = (f32[4,256,256]{2,1,0:T(8,128)}, f32[4,256,256]{2,1,0:T(8,128)}, u32[]{:S(2)}, u32[]{:S(2)}) collective-permute-start(f32[4,256,256]{2,1,0:T(8,128)} %bitcast.19), channel_id=1, source_target_pairs={{0,1},{1,0},{2,3},{3,2},{4,5},{5,4},{6,7},{7,6},{8,9},{9,8},{10,11... | collective-permute-start | bytes 3145736 | tf_op jit(solution)/shard_map/ppermute | solution.py:257
  4.0 0.1 collective-permute-start.1
  4.1 1.2 copy-done
  5.3 0.4 shard_map.49
  5.7 1.0 collective-permute-done.1.up_other
  6.7 0.2 collective-permute-done.other
  7.0 0.9 copy-done.2
  7.9 2.2 %shard_map.50 = (bf16[256,1024]{1,0:T(8,128)(2,1)S(1)}, bf16[256,1024]{1,0:T(8,128)(2,1)S(1)}, bf16[256,512]{1,0:T(8,128)(2,1)S(1)}, bf16[256,512]{1,0:T(8,128)(...) custom-call(s32[1]{0:T(128)} %bitcast.3.which, f32[4,256,256]{2,1,0:T(8,128)S(1)} %bitcast.21, ...), custom_call_target="tpu_custom_call" | custom-call | tf_op jit(solution)/shard_map/pallas_call | solution.py:278
  10.1 1.7 shard_map.51.gram.kept
  11.8 0.9 shard_map.52
  12.7 12.0 %all_to_all.40 = f32[16,40,128]{2,1,0:T(8,128)S(1)} all-to-all(f32[16,40,128]{2,1,0:T(8,128)S(1)} %bitcast.38), channel_id=1, replica_groups={{0,2,4,6,8,10,12,14,64,66,68,70,72,74,76,78},{16,18,20,22,24,26,28,30,8..., dimensions={0} | all-to-all | bytes 655360 | tf_op jit(solution)/shard_map/all_to_all | solution.py:292
  24.7 6.1 %collective-permute-start.2 = (f32[40,128]{1,0:T(8,128)S(1)}, f32[40,128]{1,0:T(8,128)S(1)}, u32[]{:S(2)}, u32[]{:S(2)}) collective-permute-start(f32[40,128]{1,0:T(8,128)S(1)} %slice_reduce_fusion.2), channel_id=1, source_target_pairs={{0,32},{2,34},{4,36},{6,38},{8,40},{10,42},{12,44},{14,46},{16,48}... | collective-permute-start | bytes 61448 | tf_op jit(solution)/shard_map/ppermute | solution.py:300
  30.8 1.2 collective-permute-start.3
  32.1 2.4 %collective-permute-start.4 = (f32[40,128]{1,0:T(8,128)S(1)}, f32[40,128]{1,0:T(8,128)S(1)}, u32[]{:S(2)}, u32[]{:S(2)}) collective-permute-start(f32[40,128]{1,0:T(8,128)S(1)} %slice_reduce_fusion.2), channel_id=1, source_target_pairs={{0,48},{2,50},{4,52},{6,54},{8,56},{10,58},{12,60},{14,62},{16,0},... | collective-permute-start | bytes 61448 | tf_op jit(solution)/shard_map/ppermute | solution.py:300
  34.4 0.0 collective-permute-done.2
  34.4 1.3 collective-permute-done.3
  35.7 0.0 collective-permute-done.4
  35.7 10.2 %all_to_all.41 = f32[16,40,128]{2,1,0:T(8,128)S(1)} all-to-all(f32[16,40,128]{2,1,0:T(8,128)S(1)} %broadcast_in_dim.14), channel_id=1, replica_groups={{0,2,4,6,8,10,12,14,64,66,68,70,72,74,76,78},{16,18,20,22,24,26,28,30,8..., dimensions={0} | all-to-all | bytes 655360 | tf_op jit(solution)/shard_map/all_to_all | solution.py:292
  45.9 4.6 %collective-permute-start.5 = (f32[256,128]{1,0:T(8,128)S(1)}, f32[256,128]{1,0:T(8,128)S(1)}, u32[]{:S(2)}, u32[]{:S(2)}) collective-permute-start(f32[256,128]{1,0:T(8,128)S(1)} %slice.57), channel_id=1, source_target_pairs={{0,1},{1,0},{2,3},{3,2},{4,5},{5,4},{6,7},{7,6},{8,9},{9,8},{10,11... | collective-permute-start | bytes 393224 | tf_op jit(solution)/shard_map/ppermute | solution.py:257
  50.6 1.0 collective-permute-done.5.beside
  51.5 12.3 %all_to_all.42 = f32[16,40,128]{2,1,0:T(8,128)S(1)} all-to-all(f32[16,40,128]{2,1,0:T(8,128)S(1)} %bitcast.36), channel_id=1, replica_groups={{64,66,68,70,72,74,76,78,128,130,132,134,136,138,140,142},{80,82,84,86,..., dimensions={0} | all-to-all | bytes 655360 | tf_op jit(solution)/shard_map/all_to_all | solution.py:292
  63.9 1.9 %collective-permute-start.6 = (f32[40,128]{1,0:T(8,128)S(1)}, f32[40,128]{1,0:T(8,128)S(1)}, u32[]{:S(2)}, u32[]{:S(2)}) collective-permute-start(f32[40,128]{1,0:T(8,128)S(1)} %slice_reduce_fusion.1), channel_id=1, source_target_pairs={{0,32},{2,34},{4,36},{6,38},{8,40},{10,42},{12,44},{14,46},{16,48}... | collective-permute-start | bytes 61448 | tf_op jit(solution)/shard_map/ppermute | solution.py:300
  65.7 3.9 %collective-permute-start.7 = (f32[40,128]{1,0:T(8,128)S(1)}, f32[40,128]{1,0:T(8,128)S(1)}, u32[]{:S(2)}, u32[]{:S(2)}) collective-permute-start(f32[40,128]{1,0:T(8,128)S(1)} %slice_reduce_fusion.1), channel_id=1, source_target_pairs={{0,16},{2,18},{4,20},{6,22},{8,24},{10,26},{12,28},{14,30},{16,32}... | collective-permute-start | bytes 61448 | tf_op jit(solution)/shard_map/ppermute | solution.py:300
  69.6 0.0 collective-permute-start.8
  69.6 1.0 collective-permute-done.6
  70.6 0.1 collective-permute-done.7
  70.7 2.4 %collective-permute-done.8 = f32[40,128]{1,0:T(8,128)S(1)} collective-permute-done((f32[40,128]{1,0:T(8,128)S(1)}, f32[40,128]{1,0:T(8,128)S(1)}, u32[]{:S(2)}, u32[]{:S(2)}) %collective-permute-start.8) | collective-permute-done | bytes 20512 | tf_op jit(solution)/shard_map/ppermute | solution.py:300
  73.2 11.6 %all_to_all.43 = f32[16,40,128]{2,1,0:T(8,128)S(1)} all-to-all(f32[16,40,128]{2,1,0:T(8,128)S(1)} %broadcast_in_dim.15), channel_id=1, replica_groups={{64,66,68,70,72,74,76,78,128,130,132,134,136,138,140,142},{80,82,84,86,..., dimensions={0} | all-to-all | bytes 655360 | tf_op jit(solution)/shard_map/all_to_all | solution.py:292
  84.8 4.4 %collective-permute-start.9 = (f32[256,128]{1,0:T(8,128)S(1)}, f32[256,128]{1,0:T(8,128)S(1)}, u32[]{:S(2)}, u32[]{:S(2)}) collective-permute-start(f32[256,128]{1,0:T(8,128)S(1)} %slice.59), channel_id=1, source_target_pairs={{0,1},{1,0},{2,3},{3,2},{4,5},{5,4},{6,7},{7,6},{8,9},{9,8},{10,11... | collective-permute-start | bytes 393224 | tf_op jit(solution)/shard_map/ppermute | solution.py:257
  89.2 1.0 collective-permute-done.9.beside
  90.2 11.1 %all_to_all.44 = f32[16,40,128]{2,1,0:T(8,128)S(1)} all-to-all(f32[16,40,128]{2,1,0:T(8,128)S(1)} %bitcast.37), channel_id=1, replica_groups={{128,130,132,134,136,138,140,142,192,194,196,198,200,202,204,206},{144,..., dimensions={0} | all-to-all | bytes 655360 | tf_op jit(solution)/shard_map/all_to_all | solution.py:292
  101.3 0.8 collective-permute-start.10
  102.1 2.3 %collective-permute-start.11 = (f32[40,128]{1,0:T(8,128)S(1)}, f32[40,128]{1,0:T(8,128)S(1)}, u32[]{:S(2)}, u32[]{:S(2)}) collective-permute-start(f32[40,128]{1,0:T(8,128)S(1)} %slice_reduce_fusion), channel_id=1, source_target_pairs={{0,16},{2,18},{4,20},{6,22},{8,24},{10,26},{12,28},{14,30},{16,32}... | collective-permute-start | bytes 61448 | tf_op jit(solution)/shard_map/ppermute | solution.py:300
  104.4 1.5 collective-permute-start.12
  105.9 2.0 %collective-permute-done.10 = f32[40,128]{1,0:T(8,128)S(1)} collective-permute-done((f32[40,128]{1,0:T(8,128)S(1)}, f32[40,128]{1,0:T(8,128)S(1)}, u32[]{:S(2)}, u32[]{:S(2)}) %collective-permute-start.10) | collective-permute-done | bytes 20512 | tf_op jit(solution)/shard_map/ppermute | solution.py:300
  107.9 0.3 collective-permute-done.12
  108.3 10.6 %all_to_all.45 = f32[16,40,128]{2,1,0:T(8,128)S(1)} all-to-all(f32[16,40,128]{2,1,0:T(8,128)S(1)} %broadcast_in_dim.16), channel_id=1, replica_groups={{128,130,132,134,136,138,140,142,192,194,196,198,200,202,204,206},{144,..., dimensions={0} | all-to-all | bytes 655360 | tf_op jit(solution)/shard_map/all_to_all | solution.py:292
  118.9 3.7 %collective-permute-start.14 = (f32[256,128]{1,0:T(8,128)S(1)}, f32[256,128]{1,0:T(8,128)S(1)}, u32[]{:S(2)}, u32[]{:S(2)}) collective-permute-start(f32[256,128]{1,0:T(8,128)S(1)} %slice.61), channel_id=1, source_target_pairs={{0,1},{1,0},{2,3},{3,2},{4,5},{5,4},{6,7},{7,6},{8,9},{9,8},{10,11... | collective-permute-start | bytes 393224 | tf_op jit(solution)/shard_map/ppermute | solution.py:257
  122.6 0.1 pad_add_fusion.section
  122.7 9.1 %shard_map.57 = (f32[256,256]{1,0:T(8,128)S(1)}, f32[256,256]{1,0:T(8,128)S(1)}) custom-call(s32[2]{0:T(128)S(1)} %pad_add_fusion.section, f32[384,128]{1,0:T(8,128)S(1)} %get-tuple-element.37.kept, f32[640,128]{1,0:T(8,128)S(1)} %bitcast.24), custom_call_target="tpu_custom_call" | custom-call | tf_op jit(solution)/shard_map/pallas_call | solution.py:327
  131.8 0.0 copy-start.4
  131.8 0.7 copy-done.4
  132.5 10.2 %all_to_all.46 = f32[8,80,128]{2,1,0:T(8,128)S(1)} all-to-all(f32[8,80,128]{2,1,0:T(8,128)S(1)} %bitcast.35), channel_id=1, replica_groups={{0,2,4,6,8,10,12,14},{16,18,20,22,24,26,28,30},{32,34,36,38,40,42,44,46..., dimensions={0} | all-to-all | bytes 655360 | tf_op jit(solution)/shard_map/all_to_all | solution.py:289
  142.7 3.7 %collective-permute-start.15 = (f32[80,128]{1,0:T(8,128)S(1)}, f32[80,128]{1,0:T(8,128)S(1)}, u32[]{:S(2)}, u32[]{:S(2)}) collective-permute-start(f32[80,128]{1,0:T(8,128)S(1)} %reduce_sum.39), channel_id=1, source_target_pairs={{0,32},{2,34},{4,36},{6,38},{8,40},{10,42},{12,44},{14,46},{16,48}... | collective-permute-start | bytes 122888 | tf_op jit(solution)/shard_map/ppermute | solution.py:300
  146.4 0.9 collective-permute-start.16
  147.3 2.6 %collective-permute-start.17 = (f32[80,128]{1,0:T(8,128)S(1)}, f32[80,128]{1,0:T(8,128)S(1)}, u32[]{:S(2)}, u32[]{:S(2)}) collective-permute-start(f32[80,128]{1,0:T(8,128)S(1)} %reduce_sum.39), channel_id=1, source_target_pairs={{0,48},{2,50},{4,52},{6,54},{8,56},{10,58},{12,60},{14,62},{16,0},... | collective-permute-start | bytes 122888 | tf_op jit(solution)/shard_map/ppermute | solution.py:300
  150.0 2.2 %collective-permute-done.16 = f32[80,128]{1,0:T(8,128)S(1)} collective-permute-done((f32[80,128]{1,0:T(8,128)S(1)}, f32[80,128]{1,0:T(8,128)S(1)}, u32[]{:S(2)}, u32[]{:S(2)}) %collective-permute-start.16) | collective-permute-done | bytes 40992 | tf_op jit(solution)/shard_map/ppermute | solution.py:300
  152.2 0.0 collective-permute-done.17
  152.2 11.9 %all_to_all.47 = f32[8,80,128]{2,1,0:T(8,128)S(1)} all-to-all(f32[8,80,128]{2,1,0:T(8,128)S(1)} %broadcast_in_dim.17), channel_id=1, replica_groups={{0,2,4,6,8,10,12,14},{16,18,20,22,24,26,28,30},{32,34,36,38,40,42,44,46..., dimensions={0} | all-to-all | bytes 655360 | tf_op jit(solution)/shard_map/all_to_all | solution.py:289
  164.2 2.0 %collective-permute-start.18 = (f32[256,128]{1,0:T(8,128)S(1)}, f32[256,128]{1,0:T(8,128)S(1)}, u32[]{:S(2)}, u32[]{:S(2)}) collective-permute-start(f32[256,128]{1,0:T(8,128)S(1)} %slice.62), channel_id=1, source_target_pairs={{0,1},{1,0},{2,3},{3,2},{4,5},{5,4},{6,7},{7,6},{8,9},{9,8},{10,11... | collective-permute-start | bytes 393224 | tf_op jit(solution)/shard_map/ppermute | solution.py:257
  166.2 2.2 %collective-permute-start.13 = (f32[256,256]{1,0:T(8,128)S(1)}, f32[256,256]{1,0:T(8,128)S(1)}, u32[]{:S(2)}, u32[]{:S(2)}) collective-permute-start(f32[256,256]{1,0:T(8,128)S(1)} %copy-done.5), channel_id=1, source_target_pairs={{0,64},{64,128},{128,192},{1,65},{65,129},{129,193},{2,66},{66,130... | collective-permute-start | bytes 786440 | tf_op jit(solution)/shard_map/ppermute | solution.py:335
  168.4 0.1 pad_add_fusion.1.flags
  168.5 0.0 collective-permute-done.18.beside
  168.5 0.6 shard_map.60
  169.1 0.0 copy-start.3
  169.1 0.8 collective-permute-start.19
  169.9 0.7 collective-permute-start.20
  170.6 1.3 collective-permute-start.21
  171.9 1.3 collective-permute-done.13
  173.2 2.2 %shard_map.61 = f32[4,256,256]{2,1,0:T(8,128)} custom-call(f32[4,256,256]{2,1,0:T(8,128)S(1)} %bitcast.22, f32[256,256]{1,0:T(8,128)S(1)} %broadcast_select_fusion.upper, f32[256,256]{1,0:T(8,128)S(1)} %get-tuple-element.43.inverse), custom_call_target="tpu_custom_call" | custom-call | tf_op jit(solution)/shard_map/pallas_call | solution.py:344
  175.4 0.0 collective-permute-done.19
  175.4 0.0 collective-permute-done.20
  175.4 4.0 %collective-permute-done.21 = f32[64,512]{1,0:T(8,128)S(1)} collective-permute-done((f32[64,512]{1,0:T(8,128)S(1)}, f32[64,512]{1,0:T(8,128)S(1)}, u32[]{:S(2)}, u32[]{:S(2)}) %collective-permute-start.21) | collective-permute-done | bytes 131104 | tf_op jit(solution)/shard_map/ppermute | solution.py:343
  179.4 0.7 slice_bitcast_fusion
  (35 shorter events, 0.4 us)
Async XLA Ops:
  0.6 6.3 %collective-permute-start = (f32[4,256,256]{2,1,0:T(8,128)}, f32[4,256,256]{2,1,0:T(8,128)}, u32[]{:S(2)}, u32[]{:S(2)}) collective-permute-start(f32[4,256,256]{2,1,0:T(8,128)} %bitcast.19), channel_id=1, source_target_pairs={{0,1},{1,0},{2,3},{3,2},{4,5},{5,4},{6,7},{7,6},{8,9},{9,8},{10,11... | collective-permute-start | bytes 3145736 | tf_op jit(solution)/shard_map/ppermute | solution.py:257
  4.0 2.8 %collective-permute-start.1 = (f32[256,256]{1,0:T(8,128)}, f32[256,256]{1,0:T(8,128)S(1)}, u32[]{:S(2)}, u32[]{:S(2)}) collective-permute-start(f32[256,256]{1,0:T(8,128)} %bitcast.39), channel_id=1, source_target_pairs={{0,1},{1,0},{2,3},{3,2},{4,5},{5,4},{6,7},{7,6},{8,9},{9,8},{10,11... | collective-permute-start | bytes 786440 | tf_op jit(solution)/shard_map/ppermute | solution.py:257
  4.1 1.2 copy-start
  5.3 1.7 copy-start.1
  7.0 1.0 copy-start.2
  24.7 9.7 %collective-permute-start.2 = (f32[40,128]{1,0:T(8,128)S(1)}, f32[40,128]{1,0:T(8,128)S(1)}, u32[]{:S(2)}, u32[]{:S(2)}) collective-permute-start(f32[40,128]{1,0:T(8,128)S(1)} %slice_reduce_fusion.2), channel_id=1, source_target_pairs={{0,32},{2,34},{4,36},{6,38},{8,40},{10,42},{12,44},{14,46},{16,48}... | collective-permute-start | bytes 61448 | tf_op jit(solution)/shard_map/ppermute | solution.py:300
  30.8 4.8 %collective-permute-start.3 = (f32[40,128]{1,0:T(8,128)S(1)}, f32[40,128]{1,0:T(8,128)S(1)}, u32[]{:S(2)}, u32[]{:S(2)}) collective-permute-start(f32[40,128]{1,0:T(8,128)S(1)} %slice_reduce_fusion.2), channel_id=1, source_target_pairs={{0,16},{2,18},{4,20},{6,22},{8,24},{10,26},{12,28},{14,30},{16,32}... | collective-permute-start | bytes 61448 | tf_op jit(solution)/shard_map/ppermute | solution.py:300
  32.1 3.6 %collective-permute-start.4 = (f32[40,128]{1,0:T(8,128)S(1)}, f32[40,128]{1,0:T(8,128)S(1)}, u32[]{:S(2)}, u32[]{:S(2)}) collective-permute-start(f32[40,128]{1,0:T(8,128)S(1)} %slice_reduce_fusion.2), channel_id=1, source_target_pairs={{0,48},{2,50},{4,52},{6,54},{8,56},{10,58},{12,60},{14,62},{16,0},... | collective-permute-start | bytes 61448 | tf_op jit(solution)/shard_map/ppermute | solution.py:300
  45.9 5.6 %collective-permute-start.5 = (f32[256,128]{1,0:T(8,128)S(1)}, f32[256,128]{1,0:T(8,128)S(1)}, u32[]{:S(2)}, u32[]{:S(2)}) collective-permute-start(f32[256,128]{1,0:T(8,128)S(1)} %slice.57), channel_id=1, source_target_pairs={{0,1},{1,0},{2,3},{3,2},{4,5},{5,4},{6,7},{7,6},{8,9},{9,8},{10,11... | collective-permute-start | bytes 393224 | tf_op jit(solution)/shard_map/ppermute | solution.py:257
  63.9 6.7 %collective-permute-start.6 = (f32[40,128]{1,0:T(8,128)S(1)}, f32[40,128]{1,0:T(8,128)S(1)}, u32[]{:S(2)}, u32[]{:S(2)}) collective-permute-start(f32[40,128]{1,0:T(8,128)S(1)} %slice_reduce_fusion.1), channel_id=1, source_target_pairs={{0,32},{2,34},{4,36},{6,38},{8,40},{10,42},{12,44},{14,46},{16,48}... | collective-permute-start | bytes 61448 | tf_op jit(solution)/shard_map/ppermute | solution.py:300
  65.7 5.0 %collective-permute-start.7 = (f32[40,128]{1,0:T(8,128)S(1)}, f32[40,128]{1,0:T(8,128)S(1)}, u32[]{:S(2)}, u32[]{:S(2)}) collective-permute-start(f32[40,128]{1,0:T(8,128)S(1)} %slice_reduce_fusion.1), channel_id=1, source_target_pairs={{0,16},{2,18},{4,20},{6,22},{8,24},{10,26},{12,28},{14,30},{16,32}... | collective-permute-start | bytes 61448 | tf_op jit(solution)/shard_map/ppermute | solution.py:300
  69.6 3.5 %collective-permute-start.8 = (f32[40,128]{1,0:T(8,128)S(1)}, f32[40,128]{1,0:T(8,128)S(1)}, u32[]{:S(2)}, u32[]{:S(2)}) collective-permute-start(f32[40,128]{1,0:T(8,128)S(1)} %slice_reduce_fusion.1), channel_id=1, source_target_pairs={{0,48},{2,50},{4,52},{6,54},{8,56},{10,58},{12,60},{14,62},{16,0},... | collective-permute-start | bytes 61448 | tf_op jit(solution)/shard_map/ppermute | solution.py:300
  84.8 5.4 %collective-permute-start.9 = (f32[256,128]{1,0:T(8,128)S(1)}, f32[256,128]{1,0:T(8,128)S(1)}, u32[]{:S(2)}, u32[]{:S(2)}) collective-permute-start(f32[256,128]{1,0:T(8,128)S(1)} %slice.59), channel_id=1, source_target_pairs={{0,1},{1,0},{2,3},{3,2},{4,5},{5,4},{6,7},{7,6},{8,9},{9,8},{10,11... | collective-permute-start | bytes 393224 | tf_op jit(solution)/shard_map/ppermute | solution.py:257
  101.3 6.6 %collective-permute-start.10 = (f32[40,128]{1,0:T(8,128)S(1)}, f32[40,128]{1,0:T(8,128)S(1)}, u32[]{:S(2)}, u32[]{:S(2)}) collective-permute-start(f32[40,128]{1,0:T(8,128)S(1)} %slice_reduce_fusion), channel_id=1, source_target_pairs={{0,32},{2,34},{4,36},{6,38},{8,40},{10,42},{12,44},{14,46},{16,48}... | collective-permute-start | bytes 61448 | tf_op jit(solution)/shard_map/ppermute | solution.py:300
  102.1 5.9 %collective-permute-start.11 = (f32[40,128]{1,0:T(8,128)S(1)}, f32[40,128]{1,0:T(8,128)S(1)}, u32[]{:S(2)}, u32[]{:S(2)}) collective-permute-start(f32[40,128]{1,0:T(8,128)S(1)} %slice_reduce_fusion), channel_id=1, source_target_pairs={{0,16},{2,18},{4,20},{6,22},{8,24},{10,26},{12,28},{14,30},{16,32}... | collective-permute-start | bytes 61448 | tf_op jit(solution)/shard_map/ppermute | solution.py:300
  104.4 3.8 %collective-permute-start.12 = (f32[40,128]{1,0:T(8,128)S(1)}, f32[40,128]{1,0:T(8,128)S(1)}, u32[]{:S(2)}, u32[]{:S(2)}) collective-permute-start(f32[40,128]{1,0:T(8,128)S(1)} %slice_reduce_fusion), channel_id=1, source_target_pairs={{0,48},{2,50},{4,52},{6,54},{8,56},{10,58},{12,60},{14,62},{16,0},... | collective-permute-start | bytes 61448 | tf_op jit(solution)/shard_map/ppermute | solution.py:300
  118.9 13.7 %collective-permute-start.14 = (f32[256,128]{1,0:T(8,128)S(1)}, f32[256,128]{1,0:T(8,128)S(1)}, u32[]{:S(2)}, u32[]{:S(2)}) collective-permute-start(f32[256,128]{1,0:T(8,128)S(1)} %slice.61), channel_id=1, source_target_pairs={{0,1},{1,0},{2,3},{3,2},{4,5},{5,4},{6,7},{7,6},{8,9},{9,8},{10,11... | collective-permute-start | bytes 393224 | tf_op jit(solution)/shard_map/ppermute | solution.py:257
  131.8 0.7 copy-start.4
  142.7 7.3 %collective-permute-start.15 = (f32[80,128]{1,0:T(8,128)S(1)}, f32[80,128]{1,0:T(8,128)S(1)}, u32[]{:S(2)}, u32[]{:S(2)}) collective-permute-start(f32[80,128]{1,0:T(8,128)S(1)} %reduce_sum.39), channel_id=1, source_target_pairs={{0,32},{2,34},{4,36},{6,38},{8,40},{10,42},{12,44},{14,46},{16,48}... | collective-permute-start | bytes 122888 | tf_op jit(solution)/shard_map/ppermute | solution.py:300
  146.4 5.8 %collective-permute-start.16 = (f32[80,128]{1,0:T(8,128)S(1)}, f32[80,128]{1,0:T(8,128)S(1)}, u32[]{:S(2)}, u32[]{:S(2)}) collective-permute-start(f32[80,128]{1,0:T(8,128)S(1)} %reduce_sum.39), channel_id=1, source_target_pairs={{0,16},{2,18},{4,20},{6,22},{8,24},{10,26},{12,28},{14,30},{16,32}... | collective-permute-start | bytes 122888 | tf_op jit(solution)/shard_map/ppermute | solution.py:300
  147.3 4.8 %collective-permute-start.17 = (f32[80,128]{1,0:T(8,128)S(1)}, f32[80,128]{1,0:T(8,128)S(1)}, u32[]{:S(2)}, u32[]{:S(2)}) collective-permute-start(f32[80,128]{1,0:T(8,128)S(1)} %reduce_sum.39), channel_id=1, source_target_pairs={{0,48},{2,50},{4,52},{6,54},{8,56},{10,58},{12,60},{14,62},{16,0},... | collective-permute-start | bytes 122888 | tf_op jit(solution)/shard_map/ppermute | solution.py:300
  164.2 2.1 %copy-start.5 = (f32[256,256]{1,0:T(8,128)S(1)}, f32[256,256]{1,0:T(8,128)}, u32[]{:S(2)}) copy-start(f32[256,256]{1,0:T(8,128)} %copy-done.4) | copy-start | bytes 786436
  164.2 4.3 %collective-permute-start.18 = (f32[256,128]{1,0:T(8,128)S(1)}, f32[256,128]{1,0:T(8,128)S(1)}, u32[]{:S(2)}, u32[]{:S(2)}) collective-permute-start(f32[256,128]{1,0:T(8,128)S(1)} %slice.62), channel_id=1, source_target_pairs={{0,1},{1,0},{2,3},{3,2},{4,5},{5,4},{6,7},{7,6},{8,9},{9,8},{10,11... | collective-permute-start | bytes 393224 | tf_op jit(solution)/shard_map/ppermute | solution.py:257
  166.2 7.0 %collective-permute-start.13 = (f32[256,256]{1,0:T(8,128)S(1)}, f32[256,256]{1,0:T(8,128)S(1)}, u32[]{:S(2)}, u32[]{:S(2)}) collective-permute-start(f32[256,256]{1,0:T(8,128)S(1)} %copy-done.5), channel_id=1, source_target_pairs={{0,64},{64,128},{128,192},{1,65},{65,129},{129,193},{2,66},{66,130... | collective-permute-start | bytes 786440 | tf_op jit(solution)/shard_map/ppermute | solution.py:335
  169.1 4.1 %copy-start.3 = (f32[1,256,256]{2,1,0:T(8,128)S(1)}, f32[1,256,256]{2,1,0:T(8,128)}, u32[]{:S(2)}) copy-start(f32[1,256,256]{2,1,0:T(8,128)} %param.3) | copy-start | bytes 786436
  169.1 6.3 %collective-permute-start.19 = (f32[64,512]{1,0:T(8,128)S(1)}, f32[64,512]{1,0:T(8,128)S(1)}, u32[]{:S(2)}, u32[]{:S(2)}) collective-permute-start(f32[64,512]{1,0:T(8,128)S(1)} %get-tuple-element.47), channel_id=1, source_target_pairs={{192,128},{193,129},{194,130},{195,131},{196,132},{197,133},{198,1... | collective-permute-start | bytes 393224 | tf_op jit(solution)/shard_map/ppermute | solution.py:343
  169.9 5.5 %collective-permute-start.20 = (f32[64,512]{1,0:T(8,128)S(1)}, f32[64,512]{1,0:T(8,128)S(1)}, u32[]{:S(2)}, u32[]{:S(2)}) collective-permute-start(f32[64,512]{1,0:T(8,128)S(1)} %get-tuple-element.46), channel_id=1, source_target_pairs={{192,64},{193,65},{194,66},{195,67},{196,68},{197,69},{198,70},{19... | collective-permute-start | bytes 393224 | tf_op jit(solution)/shard_map/ppermute | solution.py:343
  170.6 8.7 %collective-permute-start.21 = (f32[64,512]{1,0:T(8,128)S(1)}, f32[64,512]{1,0:T(8,128)S(1)}, u32[]{:S(2)}, u32[]{:S(2)}) collective-permute-start(f32[64,512]{1,0:T(8,128)S(1)} %get-tuple-element.45), channel_id=1, source_target_pairs={{192,0},{193,1},{194,2},{195,3},{196,4},{197,5},{198,6},{199,7},{2... | collective-permute-start | bytes 393224 | tf_op jit(solution)/shard_map/ppermute | solution.py:343

commit v7 on v6

--- a/solution.py
+++ b/solution.py
@@ -10,7 +10,7 @@
 MODE = 128
 LANES = 128
 BLOCK = 64
-GROUP = 8
+GROUP = 16
 VMEM_LIMIT = 16 * 1024 * 1024
 F32 = jnp.float32
 BF16 = jnp.bfloat16
@@ -320,6 +320,8 @@
         count = near * (2 if pair else 1)
         arrived = exchange(partial.reshape(count, -1, half), pair)
         piece = over_far(arrived[:near].sum(axis=0))
+        if tick == last:
+            piece, u_before = lax.optimization_barrier((piece, u_before))
         copies = jnp.broadcast_to(piece[None], arrived.shape)
         state = exchange(copies, pair).reshape(partial.shape)
         beside = swapped(state[3 * half :])

time: 181 us -> 179 us (0.989)
  blocking collectives: 90 us -> 79 us
  waiting for transfers between devices: 17.7 us -> 23.5 us
  starting transfers between devices: 50.4 us -> 54.3 us
    all_to_all x2 -> x1, blocking collectives: 22.1 us -> 11.1 us  [exchange(): return lax.all_to_all(x, 'row', 0, 0, tiled=True, axis_index_groups=blocks)]
    all_to_all x0 -> x1, waiting for transfers between devices: none -> 4.89 us  [exchange(): return lax.all_to_all(x, 'row', 0, 0, tiled=True, axis_index_groups=blocks)]
    all_to_all x0 -> x1, starting transfers between devices: none -> 3.56 us  [exchange(): return lax.all_to_all(x, 'row', 0, 0, tiled=True, axis_index_groups=blocks)]
  transfers between devices with their start and end apart: 22 -> 23, of which waited for: 13 -> 14; matrix products, arithmetic and copies ran while one was open for 0% -> 0% of each run, Pallas kernels for 7% -> 6%
where the time goes in v7:
time: 179 us
  blocking collectives  79 us (44%)
  starting transfers between devices  54.3 us (30%)
  waiting for transfers between devices  23.5 us (13%)
  Pallas kernels  17.2 us (10%)
  local copies, waits for them, and re-layouts  3.47 us (2%)
    all_to_all x6, blocking collectives, exchange(): lax.all_to_all(x, ('cores', 'row'), 0, 0, tiled=True, axis_index_groups=g...  67.9 us
    ppermute x12, starting transfers between devices, over_far(): terms.append(lax.ppermute(x, 'row', pairs))  27.3 us
    ppermute x6, starting transfers between devices, swapped(): return lax.ppermute(x, 'tensor', [(0, 1), (1, 0)])  18.6 us
    all_to_all x1, blocking collectives, exchange(): return lax.all_to_all(x, 'row', 0, 0, tiled=True, axis_index_groups=blocks)  11.1 us
    ppermute x12, waiting for transfers between devices, over_far(): terms.append(lax.ppermute(x, 'row', pairs))  9.26 us
    pallas_call x1, Pallas kernels, shards(): call(factor_own, [square] * 2, [SMEM] + [HBM] * 2, scratch + [pltpu.VMEM(...  8.25 us
    ppermute x3, waiting for transfers between devices, shards(): sent = [lax.ppermute(tiles[k], 'cores', [(last, k)]) for k in range(last)]  5.29 us
    all_to_all x1, waiting for transfers between devices, exchange(): return lax.all_to_all(x, 'row', 0, 0, tiled=True, axis_index_groups=blocks)  4.89 us
  transfers between devices with their start and end apart: 23, of which 14 were waited for; matrix products, arithmetic and copies ran while one was open for 0% of the time, Pallas kernels for 6%

profile of v7, /device:TPU:1, one launch (start us, length us, event | category | flops | bytes accessed | tf_op | source)
XLA Modules:
  0.0 178.7 jit_solution(923399184177329663)
XLA Ops:
  0.6 3.3 %collective-permute-start = (f32[4,256,256]{2,1,0:T(8,128)}, f32[4,256,256]{2,1,0:T(8,128)}, u32[]{:S(2)}, u32[]{:S(2)}) collective-permute-start(f32[4,256,256]{2,1,0:T(8,128)} %bitcast.19), channel_id=1, source_target_pairs={{0,1},{1,0},{2,3},{3,2},{4,5},{5,4},{6,7},{7,6},{8,9},{9,8},{10,11... | collective-permute-start | bytes 3145736 | tf_op jit(solution)/shard_map/ppermute | solution.py:257
  4.0 0.1 collective-permute-start.1
  4.1 1.2 copy-done
  5.3 0.4 shard_map.49
  5.7 1.0 collective-permute-done.1.up_other
  6.7 0.2 collective-permute-done.other
  7.0 0.9 copy-done.2
  7.9 2.2 %shard_map.50 = (bf16[256,1024]{1,0:T(8,128)(2,1)S(1)}, bf16[256,1024]{1,0:T(8,128)(2,1)S(1)}, bf16[256,512]{1,0:T(8,128)(2,1)S(1)}, bf16[256,512]{1,0:T(8,128)(...) custom-call(s32[1]{0:T(128)} %bitcast.2.which, f32[4,256,256]{2,1,0:T(8,128)S(1)} %bitcast.21, ...), custom_call_target="tpu_custom_call" | custom-call | tf_op jit(solution)/shard_map/pallas_call | solution.py:278
  10.1 1.7 shard_map.51.gram.kept
  11.8 0.9 shard_map.52
  12.7 12.0 %all_to_all.40 = f32[16,40,128]{2,1,0:T(8,128)S(1)} all-to-all(f32[16,40,128]{2,1,0:T(8,128)S(1)} %bitcast.37), channel_id=1, replica_groups={{0,2,4,6,8,10,12,14,64,66,68,70,72,74,76,78},{16,18,20,22,24,26,28,30,8..., dimensions={0} | all-to-all | bytes 655360 | tf_op jit(solution)/shard_map/all_to_all | solution.py:292
  24.7 6.1 %collective-permute-start.2 = (f32[40,128]{1,0:T(8,128)S(1)}, f32[40,128]{1,0:T(8,128)S(1)}, u32[]{:S(2)}, u32[]{:S(2)}) collective-permute-start(f32[40,128]{1,0:T(8,128)S(1)} %slice_reduce_fusion.2), channel_id=1, source_target_pairs={{0,32},{2,34},{4,36},{6,38},{8,40},{10,42},{12,44},{14,46},{16,48}... | collective-permute-start | bytes 61448 | tf_op jit(solution)/shard_map/ppermute | solution.py:300
  30.8 1.2 collective-permute-start.3
  32.1 2.4 %collective-permute-start.4 = (f32[40,128]{1,0:T(8,128)S(1)}, f32[40,128]{1,0:T(8,128)S(1)}, u32[]{:S(2)}, u32[]{:S(2)}) collective-permute-start(f32[40,128]{1,0:T(8,128)S(1)} %slice_reduce_fusion.2), channel_id=1, source_target_pairs={{0,48},{2,50},{4,52},{6,54},{8,56},{10,58},{12,60},{14,62},{16,0},... | collective-permute-start | bytes 61448 | tf_op jit(solution)/shard_map/ppermute | solution.py:300
  34.4 0.0 collective-permute-done.2
  34.4 1.3 collective-permute-done.3
  35.7 0.0 collective-permute-done.4
  35.7 10.2 %all_to_all.41 = f32[16,40,128]{2,1,0:T(8,128)S(1)} all-to-all(f32[16,40,128]{2,1,0:T(8,128)S(1)} %broadcast_in_dim.14), channel_id=1, replica_groups={{0,2,4,6,8,10,12,14,64,66,68,70,72,74,76,78},{16,18,20,22,24,26,28,30,8..., dimensions={0} | all-to-all | bytes 655360 | tf_op jit(solution)/shard_map/all_to_all | solution.py:292
  45.9 4.6 %collective-permute-start.5 = (f32[256,128]{1,0:T(8,128)S(1)}, f32[256,128]{1,0:T(8,128)S(1)}, u32[]{:S(2)}, u32[]{:S(2)}) collective-permute-start(f32[256,128]{1,0:T(8,128)S(1)} %slice.57), channel_id=1, source_target_pairs={{0,1},{1,0},{2,3},{3,2},{4,5},{5,4},{6,7},{7,6},{8,9},{9,8},{10,11... | collective-permute-start | bytes 393224 | tf_op jit(solution)/shard_map/ppermute | solution.py:257
  50.6 1.0 collective-permute-done.5.beside
  51.5 12.3 %all_to_all.42 = f32[16,40,128]{2,1,0:T(8,128)S(1)} all-to-all(f32[16,40,128]{2,1,0:T(8,128)S(1)} %bitcast.35), channel_id=1, replica_groups={{64,66,68,70,72,74,76,78,128,130,132,134,136,138,140,142},{80,82,84,86,..., dimensions={0} | all-to-all | bytes 655360 | tf_op jit(solution)/shard_map/all_to_all | solution.py:292
  63.9 1.9 %collective-permute-start.6 = (f32[40,128]{1,0:T(8,128)S(1)}, f32[40,128]{1,0:T(8,128)S(1)}, u32[]{:S(2)}, u32[]{:S(2)}) collective-permute-start(f32[40,128]{1,0:T(8,128)S(1)} %slice_reduce_fusion.1), channel_id=1, source_target_pairs={{0,32},{2,34},{4,36},{6,38},{8,40},{10,42},{12,44},{14,46},{16,48}... | collective-permute-start | bytes 61448 | tf_op jit(solution)/shard_map/ppermute | solution.py:300
  65.7 3.9 %collective-permute-start.7 = (f32[40,128]{1,0:T(8,128)S(1)}, f32[40,128]{1,0:T(8,128)S(1)}, u32[]{:S(2)}, u32[]{:S(2)}) collective-permute-start(f32[40,128]{1,0:T(8,128)S(1)} %slice_reduce_fusion.1), channel_id=1, source_target_pairs={{0,16},{2,18},{4,20},{6,22},{8,24},{10,26},{12,28},{14,30},{16,32}... | collective-permute-start | bytes 61448 | tf_op jit(solution)/shard_map/ppermute | solution.py:300
  69.6 0.0 collective-permute-start.8
  69.6 1.0 collective-permute-done.6
  70.6 0.1 collective-permute-done.7
  70.7 2.4 %collective-permute-done.8 = f32[40,128]{1,0:T(8,128)S(1)} collective-permute-done((f32[40,128]{1,0:T(8,128)S(1)}, f32[40,128]{1,0:T(8,128)S(1)}, u32[]{:S(2)}, u32[]{:S(2)}) %collective-permute-start.8) | collective-permute-done | bytes 20512 | tf_op jit(solution)/shard_map/ppermute | solution.py:300
  73.2 11.6 %all_to_all.43 = f32[16,40,128]{2,1,0:T(8,128)S(1)} all-to-all(f32[16,40,128]{2,1,0:T(8,128)S(1)} %broadcast_in_dim.15), channel_id=1, replica_groups={{64,66,68,70,72,74,76,78,128,130,132,134,136,138,140,142},{80,82,84,86,..., dimensions={0} | all-to-all | bytes 655360 | tf_op jit(solution)/shard_map/all_to_all | solution.py:292
  84.8 4.4 %collective-permute-start.9 = (f32[256,128]{1,0:T(8,128)S(1)}, f32[256,128]{1,0:T(8,128)S(1)}, u32[]{:S(2)}, u32[]{:S(2)}) collective-permute-start(f32[256,128]{1,0:T(8,128)S(1)} %slice.59), channel_id=1, source_target_pairs={{0,1},{1,0},{2,3},{3,2},{4,5},{5,4},{6,7},{7,6},{8,9},{9,8},{10,11... | collective-permute-start | bytes 393224 | tf_op jit(solution)/shard_map/ppermute | solution.py:257
  89.2 1.0 collective-permute-done.9.beside
  90.2 11.1 %all_to_all.44 = f32[16,40,128]{2,1,0:T(8,128)S(1)} all-to-all(f32[16,40,128]{2,1,0:T(8,128)S(1)} %bitcast.36), channel_id=1, replica_groups={{128,130,132,134,136,138,140,142,192,194,196,198,200,202,204,206},{144,..., dimensions={0} | all-to-all | bytes 655360 | tf_op jit(solution)/shard_map/all_to_all | solution.py:292
  101.3 0.8 collective-permute-start.10
  102.1 2.3 %collective-permute-start.11 = (f32[40,128]{1,0:T(8,128)S(1)}, f32[40,128]{1,0:T(8,128)S(1)}, u32[]{:S(2)}, u32[]{:S(2)}) collective-permute-start(f32[40,128]{1,0:T(8,128)S(1)} %slice_reduce_fusion), channel_id=1, source_target_pairs={{0,16},{2,18},{4,20},{6,22},{8,24},{10,26},{12,28},{14,30},{16,32}... | collective-permute-start | bytes 61448 | tf_op jit(solution)/shard_map/ppermute | solution.py:300
  104.4 1.5 collective-permute-start.12
  105.9 2.0 %collective-permute-done.10 = f32[40,128]{1,0:T(8,128)S(1)} collective-permute-done((f32[40,128]{1,0:T(8,128)S(1)}, f32[40,128]{1,0:T(8,128)S(1)}, u32[]{:S(2)}, u32[]{:S(2)}) %collective-permute-start.10) | collective-permute-done | bytes 20512 | tf_op jit(solution)/shard_map/ppermute | solution.py:300
  107.9 0.0 collective-permute-done.11
  107.9 0.3 collective-permute-done.12
  108.3 10.6 %all_to_all.45 = f32[16,40,128]{2,1,0:T(8,128)S(1)} all-to-all(f32[16,40,128]{2,1,0:T(8,128)S(1)} %broadcast_in_dim.16), channel_id=1, replica_groups={{128,130,132,134,136,138,140,142,192,194,196,198,200,202,204,206},{144,..., dimensions={0} | all-to-all | bytes 655360 | tf_op jit(solution)/shard_map/all_to_all | solution.py:292
  118.9 3.7 %collective-permute-start.13 = (f32[256,128]{1,0:T(8,128)S(1)}, f32[256,128]{1,0:T(8,128)S(1)}, u32[]{:S(2)}, u32[]{:S(2)}) collective-permute-start(f32[256,128]{1,0:T(8,128)S(1)} %slice.61), channel_id=1, source_target_pairs={{0,1},{1,0},{2,3},{3,2},{4,5},{5,4},{6,7},{7,6},{8,9},{9,8},{10,11... | collective-permute-start | bytes 393224 | tf_op jit(solution)/shard_map/ppermute | solution.py:257
  122.6 0.1 pad_add_fusion.section
  122.7 8.2 %shard_map.57 = (f32[256,256]{1,0:T(8,128)S(1)}, f32[256,256]{1,0:T(8,128)S(1)}) custom-call(s32[2]{0:T(128)S(1)} %pad_add_fusion.section, f32[384,128]{1,0:T(8,128)S(1)} %get-tuple-element.39.kept, f32[640,128]{1,0:T(8,128)S(1)} %bitcast.24), custom_call_target="tpu_custom_call" | custom-call | tf_op jit(solution)/shard_map/pallas_call | solution.py:329
  131.0 0.2 shard_map.58.gram
  131.2 0.5 copy-done.4
  131.7 0.7 shard_map.59
  132.4 3.6 %all-to-all-start.6 = ((f32[8,80,128]{2,1,0:T(8,128)}), f32[8,80,128]{2,1,0:T(8,128)S(1)}, u32[]{:S(2)}, u32[]{:S(2)}) async-start(f32[8,80,128]{2,1,0:T(8,128)} %bitcast.10), calls=%async_computation.6 | async-start | bytes 655360 | tf_op jit(solution)/shard_map/all_to_all | solution.py:289
  136.0 0.0 copy-start.3
  136.0 2.3 %collective-permute-start.17 = (f32[256,256]{1,0:T(8,128)S(1)}, f32[256,256]{1,0:T(8,128)S(1)}, u32[]{:S(2)}, u32[]{:S(2)}) collective-permute-start(f32[256,256]{1,0:T(8,128)S(1)} %copy-done.5), channel_id=1, source_target_pairs={{0,64},{64,128},{128,192},{1,65},{65,129},{129,193},{2,66},{66,130... | collective-permute-start | bytes 786440 | tf_op jit(solution)/shard_map/ppermute | solution.py:337
  138.3 4.9 %all-to-all-done.6 = f32[8,80,128]{2,1,0:T(8,128)S(1)} async-done(((f32[8,80,128]{2,1,0:T(8,128)}), f32[8,80,128]{2,1,0:T(8,128)S(1)}, u32[]{:S(2)}, u32[]{:S(2)}) %all-to-all-start.6) | async-done | bytes 327712 | tf_op jit(solution)/shard_map/all_to_all | solution.py:289
  143.2 3.7 %collective-permute-start.14 = (f32[80,128]{1,0:T(8,128)S(1)}, f32[80,128]{1,0:T(8,128)S(1)}, u32[]{:S(2)}, u32[]{:S(2)}) collective-permute-start(f32[80,128]{1,0:T(8,128)S(1)} %reduce_sum.39), channel_id=1, source_target_pairs={{0,32},{2,34},{4,36},{6,38},{8,40},{10,42},{12,44},{14,46},{16,48}... | collective-permute-start | bytes 122888 | tf_op jit(solution)/shard_map/ppermute | solution.py:300
  146.9 0.9 collective-permute-start.15
  147.8 2.6 %collective-permute-start.16 = (f32[80,128]{1,0:T(8,128)S(1)}, f32[80,128]{1,0:T(8,128)S(1)}, u32[]{:S(2)}, u32[]{:S(2)}) collective-permute-start(f32[80,128]{1,0:T(8,128)S(1)} %reduce_sum.39), channel_id=1, source_target_pairs={{0,48},{2,50},{4,52},{6,54},{8,56},{10,58},{12,60},{14,62},{16,0},... | collective-permute-start | bytes 122888 | tf_op jit(solution)/shard_map/ppermute | solution.py:300
  150.5 2.2 %collective-permute-done.15 = f32[80,128]{1,0:T(8,128)S(1)} collective-permute-done((f32[80,128]{1,0:T(8,128)S(1)}, f32[80,128]{1,0:T(8,128)S(1)}, u32[]{:S(2)}, u32[]{:S(2)}) %collective-permute-start.15) | collective-permute-done | bytes 40992 | tf_op jit(solution)/shard_map/ppermute | solution.py:300
  152.7 0.0 collective-permute-done.16
  152.7 11.1 %all_to_all.46 = f32[8,80,128]{2,1,0:T(8,128)S(1)} all-to-all(f32[8,80,128]{2,1,0:T(8,128)S(1)} %broadcast_in_dim.17), channel_id=1, replica_groups={{0,2,4,6,8,10,12,14},{16,18,20,22,24,26,28,30},{32,34,36,38,40,42,44,46..., dimensions={0} | all-to-all | bytes 655360 | tf_op jit(solution)/shard_map/all_to_all | solution.py:289
  163.8 2.4 %collective-permute-start.18 = (f32[256,128]{1,0:T(8,128)S(1)}, f32[256,128]{1,0:T(8,128)S(1)}, u32[]{:S(2)}, u32[]{:S(2)}) collective-permute-start(f32[256,128]{1,0:T(8,128)S(1)} %slice.62), channel_id=1, source_target_pairs={{0,1},{1,0},{2,3},{3,2},{4,5},{5,4},{6,7},{7,6},{8,9},{9,8},{10,11... | collective-permute-start | bytes 393224 | tf_op jit(solution)/shard_map/ppermute | solution.py:257
  166.3 0.1 pad_add_fusion.1.flags
  166.3 0.9 collective-permute-done.18.beside
  167.2 0.6 shard_map.60
  167.8 0.7 collective-permute-start.19
  168.5 0.7 collective-permute-start.20
  169.2 1.3 collective-permute-start.21
  170.5 2.2 %shard_map.61 = f32[4,256,256]{2,1,0:T(8,128)} custom-call(f32[4,256,256]{2,1,0:T(8,128)S(1)} %bitcast.22, f32[256,256]{1,0:T(8,128)S(1)} %broadcast_select_fusion.upper, f32[256,256]{1,0:T(8,128)S(1)} %get-tuple-element.47.inverse), custom_call_target="tpu_custom_call" | custom-call | tf_op jit(solution)/shard_map/pallas_call | solution.py:346
  172.7 5.3 %collective-permute-done.21 = f32[64,512]{1,0:T(8,128)S(1)} collective-permute-done((f32[64,512]{1,0:T(8,128)S(1)}, f32[64,512]{1,0:T(8,128)S(1)}, u32[]{:S(2)}, u32[]{:S(2)}) %collective-permute-start.21) | collective-permute-done | bytes 131104 | tf_op jit(solution)/shard_map/ppermute | solution.py:345
  178.0 0.7 slice_bitcast_fusion
  (36 shorter events, 0.4 us)
Async XLA Ops:
  0.6 6.3 %collective-permute-start = (f32[4,256,256]{2,1,0:T(8,128)}, f32[4,256,256]{2,1,0:T(8,128)}, u32[]{:S(2)}, u32[]{:S(2)}) collective-permute-start(f32[4,256,256]{2,1,0:T(8,128)} %bitcast.19), channel_id=1, source_target_pairs={{0,1},{1,0},{2,3},{3,2},{4,5},{5,4},{6,7},{7,6},{8,9},{9,8},{10,11... | collective-permute-start | bytes 3145736 | tf_op jit(solution)/shard_map/ppermute | solution.py:257
  4.0 2.8 %collective-permute-start.1 = (f32[256,256]{1,0:T(8,128)}, f32[256,256]{1,0:T(8,128)S(1)}, u32[]{:S(2)}, u32[]{:S(2)}) collective-permute-start(f32[256,256]{1,0:T(8,128)} %bitcast.38), channel_id=1, source_target_pairs={{0,1},{1,0},{2,3},{3,2},{4,5},{5,4},{6,7},{7,6},{8,9},{9,8},{10,11... | collective-permute-start | bytes 786440 | tf_op jit(solution)/shard_map/ppermute | solution.py:257
  4.1 1.2 copy-start
  5.3 1.7 copy-start.1
  7.0 1.0 copy-start.2
  24.7 9.7 %collective-permute-start.2 = (f32[40,128]{1,0:T(8,128)S(1)}, f32[40,128]{1,0:T(8,128)S(1)}, u32[]{:S(2)}, u32[]{:S(2)}) collective-permute-start(f32[40,128]{1,0:T(8,128)S(1)} %slice_reduce_fusion.2), channel_id=1, source_target_pairs={{0,32},{2,34},{4,36},{6,38},{8,40},{10,42},{12,44},{14,46},{16,48}... | collective-permute-start | bytes 61448 | tf_op jit(solution)/shard_map/ppermute | solution.py:300
  30.8 4.8 %collective-permute-start.3 = (f32[40,128]{1,0:T(8,128)S(1)}, f32[40,128]{1,0:T(8,128)S(1)}, u32[]{:S(2)}, u32[]{:S(2)}) collective-permute-start(f32[40,128]{1,0:T(8,128)S(1)} %slice_reduce_fusion.2), channel_id=1, source_target_pairs={{0,16},{2,18},{4,20},{6,22},{8,24},{10,26},{12,28},{14,30},{16,32}... | collective-permute-start | bytes 61448 | tf_op jit(solution)/shard_map/ppermute | solution.py:300
  32.1 3.6 %collective-permute-start.4 = (f32[40,128]{1,0:T(8,128)S(1)}, f32[40,128]{1,0:T(8,128)S(1)}, u32[]{:S(2)}, u32[]{:S(2)}) collective-permute-start(f32[40,128]{1,0:T(8,128)S(1)} %slice_reduce_fusion.2), channel_id=1, source_target_pairs={{0,48},{2,50},{4,52},{6,54},{8,56},{10,58},{12,60},{14,62},{16,0},... | collective-permute-start | bytes 61448 | tf_op jit(solution)/shard_map/ppermute | solution.py:300
  45.9 5.6 %collective-permute-start.5 = (f32[256,128]{1,0:T(8,128)S(1)}, f32[256,128]{1,0:T(8,128)S(1)}, u32[]{:S(2)}, u32[]{:S(2)}) collective-permute-start(f32[256,128]{1,0:T(8,128)S(1)} %slice.57), channel_id=1, source_target_pairs={{0,1},{1,0},{2,3},{3,2},{4,5},{5,4},{6,7},{7,6},{8,9},{9,8},{10,11... | collective-permute-start | bytes 393224 | tf_op jit(solution)/shard_map/ppermute | solution.py:257
  63.9 6.7 %collective-permute-start.6 = (f32[40,128]{1,0:T(8,128)S(1)}, f32[40,128]{1,0:T(8,128)S(1)}, u32[]{:S(2)}, u32[]{:S(2)}) collective-permute-start(f32[40,128]{1,0:T(8,128)S(1)} %slice_reduce_fusion.1), channel_id=1, source_target_pairs={{0,32},{2,34},{4,36},{6,38},{8,40},{10,42},{12,44},{14,46},{16,48}... | collective-permute-start | bytes 61448 | tf_op jit(solution)/shard_map/ppermute | solution.py:300
  65.7 5.0 %collective-permute-start.7 = (f32[40,128]{1,0:T(8,128)S(1)}, f32[40,128]{1,0:T(8,128)S(1)}, u32[]{:S(2)}, u32[]{:S(2)}) collective-permute-start(f32[40,128]{1,0:T(8,128)S(1)} %slice_reduce_fusion.1), channel_id=1, source_target_pairs={{0,16},{2,18},{4,20},{6,22},{8,24},{10,26},{12,28},{14,30},{16,32}... | collective-permute-start | bytes 61448 | tf_op jit(solution)/shard_map/ppermute | solution.py:300
  69.6 3.5 %collective-permute-start.8 = (f32[40,128]{1,0:T(8,128)S(1)}, f32[40,128]{1,0:T(8,128)S(1)}, u32[]{:S(2)}, u32[]{:S(2)}) collective-permute-start(f32[40,128]{1,0:T(8,128)S(1)} %slice_reduce_fusion.1), channel_id=1, source_target_pairs={{0,48},{2,50},{4,52},{6,54},{8,56},{10,58},{12,60},{14,62},{16,0},... | collective-permute-start | bytes 61448 | tf_op jit(solution)/shard_map/ppermute | solution.py:300
  84.8 5.4 %collective-permute-start.9 = (f32[256,128]{1,0:T(8,128)S(1)}, f32[256,128]{1,0:T(8,128)S(1)}, u32[]{:S(2)}, u32[]{:S(2)}) collective-permute-start(f32[256,128]{1,0:T(8,128)S(1)} %slice.59), channel_id=1, source_target_pairs={{0,1},{1,0},{2,3},{3,2},{4,5},{5,4},{6,7},{7,6},{8,9},{9,8},{10,11... | collective-permute-start | bytes 393224 | tf_op jit(solution)/shard_map/ppermute | solution.py:257
  101.3 6.6 %collective-permute-start.10 = (f32[40,128]{1,0:T(8,128)S(1)}, f32[40,128]{1,0:T(8,128)S(1)}, u32[]{:S(2)}, u32[]{:S(2)}) collective-permute-start(f32[40,128]{1,0:T(8,128)S(1)} %slice_reduce_fusion), channel_id=1, source_target_pairs={{0,32},{2,34},{4,36},{6,38},{8,40},{10,42},{12,44},{14,46},{16,48}... | collective-permute-start | bytes 61448 | tf_op jit(solution)/shard_map/ppermute | solution.py:300
  102.1 5.9 %collective-permute-start.11 = (f32[40,128]{1,0:T(8,128)S(1)}, f32[40,128]{1,0:T(8,128)S(1)}, u32[]{:S(2)}, u32[]{:S(2)}) collective-permute-start(f32[40,128]{1,0:T(8,128)S(1)} %slice_reduce_fusion), channel_id=1, source_target_pairs={{0,16},{2,18},{4,20},{6,22},{8,24},{10,26},{12,28},{14,30},{16,32}... | collective-permute-start | bytes 61448 | tf_op jit(solution)/shard_map/ppermute | solution.py:300
  104.4 3.8 %collective-permute-start.12 = (f32[40,128]{1,0:T(8,128)S(1)}, f32[40,128]{1,0:T(8,128)S(1)}, u32[]{:S(2)}, u32[]{:S(2)}) collective-permute-start(f32[40,128]{1,0:T(8,128)S(1)} %slice_reduce_fusion), channel_id=1, source_target_pairs={{0,48},{2,50},{4,52},{6,54},{8,56},{10,58},{12,60},{14,62},{16,0},... | collective-permute-start | bytes 61448 | tf_op jit(solution)/shard_map/ppermute | solution.py:300
  118.9 12.8 %collective-permute-start.13 = (f32[256,128]{1,0:T(8,128)S(1)}, f32[256,128]{1,0:T(8,128)S(1)}, u32[]{:S(2)}, u32[]{:S(2)}) collective-permute-start(f32[256,128]{1,0:T(8,128)S(1)} %slice.61), channel_id=1, source_target_pairs={{0,1},{1,0},{2,3},{3,2},{4,5},{5,4},{6,7},{7,6},{8,9},{9,8},{10,11... | collective-permute-start | bytes 393224 | tf_op jit(solution)/shard_map/ppermute | solution.py:257
  130.9 0.7 copy-start.4
  132.4 3.6 %copy-start.5 = (f32[256,256]{1,0:T(8,128)S(1)}, f32[256,256]{1,0:T(8,128)}, u32[]{:S(2)}) copy-start(f32[256,256]{1,0:T(8,128)} %copy-done.4) | copy-start | bytes 786436
  132.4 10.8 %all-to-all-start.6 = ((f32[8,80,128]{2,1,0:T(8,128)}), f32[8,80,128]{2,1,0:T(8,128)S(1)}, u32[]{:S(2)}, u32[]{:S(2)}) async-start(f32[8,80,128]{2,1,0:T(8,128)} %bitcast.10), calls=%async_computation.6 | async-start | bytes 655360 | tf_op jit(solution)/shard_map/all_to_all | solution.py:289
  136.0 14.5 %copy-start.3 = (f32[1,256,256]{2,1,0:T(8,128)S(1)}, f32[1,256,256]{2,1,0:T(8,128)}, u32[]{:S(2)}) copy-start(f32[1,256,256]{2,1,0:T(8,128)} %param.3) | copy-start | bytes 786436
  136.0 14.5 %collective-permute-start.17 = (f32[256,256]{1,0:T(8,128)S(1)}, f32[256,256]{1,0:T(8,128)S(1)}, u32[]{:S(2)}, u32[]{:S(2)}) collective-permute-start(f32[256,256]{1,0:T(8,128)S(1)} %copy-done.5), channel_id=1, source_target_pairs={{0,64},{64,128},{128,192},{1,65},{65,129},{129,193},{2,66},{66,130... | collective-permute-start | bytes 786440 | tf_op jit(solution)/shard_map/ppermute | solution.py:337
  143.2 7.3 %collective-permute-start.14 = (f32[80,128]{1,0:T(8,128)S(1)}, f32[80,128]{1,0:T(8,128)S(1)}, u32[]{:S(2)}, u32[]{:S(2)}) collective-permute-start(f32[80,128]{1,0:T(8,128)S(1)} %reduce_sum.39), channel_id=1, source_target_pairs={{0,32},{2,34},{4,36},{6,38},{8,40},{10,42},{12,44},{14,46},{16,48}... | collective-permute-start | bytes 122888 | tf_op jit(solution)/shard_map/ppermute | solution.py:300
  146.9 5.8 %collective-permute-start.15 = (f32[80,128]{1,0:T(8,128)S(1)}, f32[80,128]{1,0:T(8,128)S(1)}, u32[]{:S(2)}, u32[]{:S(2)}) collective-permute-start(f32[80,128]{1,0:T(8,128)S(1)} %reduce_sum.39), channel_id=1, source_target_pairs={{0,16},{2,18},{4,20},{6,22},{8,24},{10,26},{12,28},{14,30},{16,32}... | collective-permute-start | bytes 122888 | tf_op jit(solution)/shard_map/ppermute | solution.py:300
  147.8 4.9 %collective-permute-start.16 = (f32[80,128]{1,0:T(8,128)S(1)}, f32[80,128]{1,0:T(8,128)S(1)}, u32[]{:S(2)}, u32[]{:S(2)}) collective-permute-start(f32[80,128]{1,0:T(8,128)S(1)} %reduce_sum.39), channel_id=1, source_target_pairs={{0,48},{2,50},{4,52},{6,54},{8,56},{10,58},{12,60},{14,62},{16,0},... | collective-permute-start | bytes 122888 | tf_op jit(solution)/shard_map/ppermute | solution.py:300
  163.8 3.4 %collective-permute-start.18 = (f32[256,128]{1,0:T(8,128)S(1)}, f32[256,128]{1,0:T(8,128)S(1)}, u32[]{:S(2)}, u32[]{:S(2)}) collective-permute-start(f32[256,128]{1,0:T(8,128)S(1)} %slice.62), channel_id=1, source_target_pairs={{0,1},{1,0},{2,3},{3,2},{4,5},{5,4},{6,7},{7,6},{8,9},{9,8},{10,11... | collective-permute-start | bytes 393224 | tf_op jit(solution)/shard_map/ppermute | solution.py:257
  167.8 4.9 %collective-permute-start.19 = (f32[64,512]{1,0:T(8,128)S(1)}, f32[64,512]{1,0:T(8,128)S(1)}, u32[]{:S(2)}, u32[]{:S(2)}) collective-permute-start(f32[64,512]{1,0:T(8,128)S(1)} %get-tuple-element.51), channel_id=1, source_target_pairs={{192,128},{193,129},{194,130},{195,131},{196,132},{197,133},{198,1... | collective-permute-start | bytes 393224 | tf_op jit(solution)/shard_map/ppermute | solution.py:345
  168.5 4.2 %collective-permute-start.20 = (f32[64,512]{1,0:T(8,128)S(1)}, f32[64,512]{1,0:T(8,128)S(1)}, u32[]{:S(2)}, u32[]{:S(2)}) collective-permute-start(f32[64,512]{1,0:T(8,128)S(1)} %get-tuple-element.50), channel_id=1, source_target_pairs={{192,64},{193,65},{194,66},{195,67},{196,68},{197,69},{198,70},{19... | collective-permute-start | bytes 393224 | tf_op jit(solution)/shard_map/ppermute | solution.py:345
  169.2 8.8 %collective-permute-start.21 = (f32[64,512]{1,0:T(8,128)S(1)}, f32[64,512]{1,0:T(8,128)S(1)}, u32[]{:S(2)}, u32[]{:S(2)}) collective-permute-start(f32[64,512]{1,0:T(8,128)S(1)} %get-tuple-element.49), channel_id=1, source_target_pairs={{192,0},{193,1},{194,2},{195,3},{196,4},{197,5},{198,6},{199,7},{2... | collective-permute-start | bytes 393224 | tf_op jit(solution)/shard_map/ppermute | solution.py:345

commit v8 on v7

--- a/solution.py
+++ b/solution.py
@@ -229,20 +229,23 @@
         pltpu.sync_copy(x, x_out)
 
 
-def factor_last(flags, state, beside, x_own, both, x_out, work):
-    rank = work.shape[0]
-
-    @pl.when(flags[0] == 0)
+def factor_last(place, state, x_own, u_out, x_out, work):
+    @pl.when(place[0] == 0)
     def _():
         x_out[...] = x_own[...]
 
-    @pl.when(flags[0] != 0)
-    def _():
-        first = flags[1] == 0
-        link = whole_link(first, state[3 * rank // 2 :, :], beside[...])
-        both[:, rank:] = jnp.where(first, link, link.T)
+    @pl.when(place[0] != 0)
+    def _():
         unpack_gram(state, work)
-        factorize(both, x_out, work)
+        factorize(u_out, x_out, work)
+
+
+def join(which, upper, state, beside, both):
+    rank = upper.shape[0]
+    first = which[0] == 0
+    link = whole_link(first, state[3 * rank // 2 :, :], beside[...])
+    both[:, :rank] = upper[...]
+    both[:, rank:] = jnp.where(first, link, link.T)
 
 
 def frame(scale, own, upper, inverse, out):
@@ -337,9 +340,12 @@
             u_before = lax.ppermute(u_own, "cores", [(k, k + 1) for k in range(last)])
             u_before = jnp.where(section == 0, up, u_before)
 
-    both, x_own = call(
-        factor_last, [((rank, 2 * rank), F32), square], [SMEM] + [VMEM] * 3, scratch
-    )(scalars(section == last, which), state, beside, x_own)
+    u_last, x_own = call(factor_last, [square] * 2, [SMEM] + [VMEM] * 2, scratch)(
+        scalars(section == last), state, x_own
+    )
+    (both,) = call(join, [((rank, 2 * rank), F32)], [SMEM] + [VMEM] * 3)(
+        scalars(which), u_last, state, beside
+    )
     share = rank // sections
     tiles = both.reshape(sections, share, 2 * rank)
     sent = [lax.ppermute(tiles[k], "cores", [(last, k)]) for k in range(last)]

time: 179 us -> 179 us (level)
  no operation moved by 1% of the time
where the time goes in v8:
time: 179 us; the launch traced here: 178 us
  blocking collectives  79 us (44%)
  starting transfers between devices  54.3 us (30%)
  waiting for transfers between devices  23.6 us (13%)
  Pallas kernels  16.8 us (9%)
  local copies, waits for them, and re-layouts  3.47 us (2%)
    all_to_all x6, blocking collectives, exchange(): lax.all_to_all(x, ('cores', 'row'), 0, 0, tiled=True, axis_index_groups=g...  67.9 us
    ppermute x12, starting transfers between devices, over_far(): terms.append(lax.ppermute(x, 'row', pairs))  27.3 us
    ppermute x6, starting transfers between devices, swapped(): return lax.ppermute(x, 'tensor', [(0, 1), (1, 0)])  18.6 us
    all_to_all x1, blocking collectives, exchange(): return lax.all_to_all(x, 'row', 0, 0, tiled=True, axis_index_groups=blocks)  11.1 us
    ppermute x12, waiting for transfers between devices, over_far(): terms.append(lax.ppermute(x, 'row', pairs))  9.26 us
    pallas_call x1, Pallas kernels, shards(): call(factor_own, [square] * 2, [SMEM] + [HBM] * 2, scratch + [pltpu.VMEM(...  8.25 us
    ppermute x3, waiting for transfers between devices, shards(): sent = [lax.ppermute(tiles[k], 'cores', [(last, k)]) for k in range(last)]  5.29 us
    all_to_all x1, waiting for transfers between devices, exchange(): return lax.all_to_all(x, 'row', 0, 0, tiled=True, axis_index_groups=blocks)  4.89 us
  transfers between devices with their start and end apart: 23, of which 14 were waited for; matrix products, arithmetic and copies ran while one was open for 0% of the time, Pallas kernels for 6%

profile of v8, /device:TPU:1, one launch (start us, length us, event | category | flops | bytes accessed | tf_op | source)
XLA Modules:
  0.0 178.3 jit_solution(10603505322050372689)
XLA Ops:
  0.6 3.3 %collective-permute-start = (f32[4,256,256]{2,1,0:T(8,128)}, f32[4,256,256]{2,1,0:T(8,128)}, u32[]{:S(2)}, u32[]{:S(2)}) collective-permute-start(f32[4,256,256]{2,1,0:T(8,128)} %bitcast.19), channel_id=1, source_target_pairs={{0,1},{1,0},{2,3},{3,2},{4,5},{5,4},{6,7},{7,6},{8,9},{9,8},{10,11... | collective-permute-start | bytes 3145736 | tf_op jit(solution)/shard_map/ppermute | solution.py:260
  4.0 0.1 collective-permute-start.1
  4.1 1.2 copy-done
  5.3 0.4 shard_map.49
  5.7 1.0 collective-permute-done.1.up_other
  6.7 0.2 collective-permute-done.other
  7.0 0.9 copy-done.2
  7.9 2.2 %shard_map.50 = (bf16[256,1024]{1,0:T(8,128)(2,1)S(1)}, bf16[256,1024]{1,0:T(8,128)(2,1)S(1)}, bf16[256,512]{1,0:T(8,128)(2,1)S(1)}, bf16[256,512]{1,0:T(8,128)(...) custom-call(s32[1]{0:T(128)} %bitcast.2.which, f32[4,256,256]{2,1,0:T(8,128)S(1)} %bitcast.21, ...), custom_call_target="tpu_custom_call" | custom-call | tf_op jit(solution)/shard_map/pallas_call | solution.py:281
  10.1 1.7 shard_map.51.gram.kept
  11.8 0.9 shard_map.52
  12.7 12.0 %all_to_all.40 = f32[16,40,128]{2,1,0:T(8,128)S(1)} all-to-all(f32[16,40,128]{2,1,0:T(8,128)S(1)} %bitcast.38), channel_id=1, replica_groups={{0,2,4,6,8,10,12,14,64,66,68,70,72,74,76,78},{16,18,20,22,24,26,28,30,8..., dimensions={0} | all-to-all | bytes 655360 | tf_op jit(solution)/shard_map/all_to_all | solution.py:295
  24.7 6.1 %collective-permute-start.2 = (f32[40,128]{1,0:T(8,128)S(1)}, f32[40,128]{1,0:T(8,128)S(1)}, u32[]{:S(2)}, u32[]{:S(2)}) collective-permute-start(f32[40,128]{1,0:T(8,128)S(1)} %slice_reduce_fusion.2), channel_id=1, source_target_pairs={{0,32},{2,34},{4,36},{6,38},{8,40},{10,42},{12,44},{14,46},{16,48}... | collective-permute-start | bytes 61448 | tf_op jit(solution)/shard_map/ppermute | solution.py:303
  30.8 1.2 collective-permute-start.3
  32.1 2.4 %collective-permute-start.4 = (f32[40,128]{1,0:T(8,128)S(1)}, f32[40,128]{1,0:T(8,128)S(1)}, u32[]{:S(2)}, u32[]{:S(2)}) collective-permute-start(f32[40,128]{1,0:T(8,128)S(1)} %slice_reduce_fusion.2), channel_id=1, source_target_pairs={{0,48},{2,50},{4,52},{6,54},{8,56},{10,58},{12,60},{14,62},{16,0},... | collective-permute-start | bytes 61448 | tf_op jit(solution)/shard_map/ppermute | solution.py:303
  34.4 0.0 collective-permute-done.2
  34.4 1.3 collective-permute-done.3
  35.7 0.0 collective-permute-done.4
  35.7 10.2 %all_to_all.41 = f32[16,40,128]{2,1,0:T(8,128)S(1)} all-to-all(f32[16,40,128]{2,1,0:T(8,128)S(1)} %broadcast_in_dim.14), channel_id=1, replica_groups={{0,2,4,6,8,10,12,14,64,66,68,70,72,74,76,78},{16,18,20,22,24,26,28,30,8..., dimensions={0} | all-to-all | bytes 655360 | tf_op jit(solution)/shard_map/all_to_all | solution.py:295
  45.9 4.6 %collective-permute-start.5 = (f32[256,128]{1,0:T(8,128)S(1)}, f32[256,128]{1,0:T(8,128)S(1)}, u32[]{:S(2)}, u32[]{:S(2)}) collective-permute-start(f32[256,128]{1,0:T(8,128)S(1)} %slice.57), channel_id=1, source_target_pairs={{0,1},{1,0},{2,3},{3,2},{4,5},{5,4},{6,7},{7,6},{8,9},{9,8},{10,11... | collective-permute-start | bytes 393224 | tf_op jit(solution)/shard_map/ppermute | solution.py:260
  50.6 1.0 collective-permute-done.5.beside
  51.5 12.3 %all_to_all.42 = f32[16,40,128]{2,1,0:T(8,128)S(1)} all-to-all(f32[16,40,128]{2,1,0:T(8,128)S(1)} %bitcast.36), channel_id=1, replica_groups={{64,66,68,70,72,74,76,78,128,130,132,134,136,138,140,142},{80,82,84,86,..., dimensions={0} | all-to-all | bytes 655360 | tf_op jit(solution)/shard_map/all_to_all | solution.py:295
  63.9 1.9 %collective-permute-start.6 = (f32[40,128]{1,0:T(8,128)S(1)}, f32[40,128]{1,0:T(8,128)S(1)}, u32[]{:S(2)}, u32[]{:S(2)}) collective-permute-start(f32[40,128]{1,0:T(8,128)S(1)} %slice_reduce_fusion.1), channel_id=1, source_target_pairs={{0,32},{2,34},{4,36},{6,38},{8,40},{10,42},{12,44},{14,46},{16,48}... | collective-permute-start | bytes 61448 | tf_op jit(solution)/shard_map/ppermute | solution.py:303
  65.7 3.9 %collective-permute-start.7 = (f32[40,128]{1,0:T(8,128)S(1)}, f32[40,128]{1,0:T(8,128)S(1)}, u32[]{:S(2)}, u32[]{:S(2)}) collective-permute-start(f32[40,128]{1,0:T(8,128)S(1)} %slice_reduce_fusion.1), channel_id=1, source_target_pairs={{0,16},{2,18},{4,20},{6,22},{8,24},{10,26},{12,28},{14,30},{16,32}... | collective-permute-start | bytes 61448 | tf_op jit(solution)/shard_map/ppermute | solution.py:303
  69.6 0.0 collective-permute-start.8
  69.6 1.0 collective-permute-done.6
  70.6 0.1 collective-permute-done.7
  70.7 2.4 %collective-permute-done.8 = f32[40,128]{1,0:T(8,128)S(1)} collective-permute-done((f32[40,128]{1,0:T(8,128)S(1)}, f32[40,128]{1,0:T(8,128)S(1)}, u32[]{:S(2)}, u32[]{:S(2)}) %collective-permute-start.8) | collective-permute-done | bytes 20512 | tf_op jit(solution)/shard_map/ppermute | solution.py:303
  73.2 11.6 %all_to_all.43 = f32[16,40,128]{2,1,0:T(8,128)S(1)} all-to-all(f32[16,40,128]{2,1,0:T(8,128)S(1)} %broadcast_in_dim.15), channel_id=1, replica_groups={{64,66,68,70,72,74,76,78,128,130,132,134,136,138,140,142},{80,82,84,86,..., dimensions={0} | all-to-all | bytes 655360 | tf_op jit(solution)/shard_map/all_to_all | solution.py:295
  84.8 4.4 %collective-permute-start.9 = (f32[256,128]{1,0:T(8,128)S(1)}, f32[256,128]{1,0:T(8,128)S(1)}, u32[]{:S(2)}, u32[]{:S(2)}) collective-permute-start(f32[256,128]{1,0:T(8,128)S(1)} %slice.59), channel_id=1, source_target_pairs={{0,1},{1,0},{2,3},{3,2},{4,5},{5,4},{6,7},{7,6},{8,9},{9,8},{10,11... | collective-permute-start | bytes 393224 | tf_op jit(solution)/shard_map/ppermute | solution.py:260
  89.2 1.0 collective-permute-done.9.beside
  90.2 11.1 %all_to_all.44 = f32[16,40,128]{2,1,0:T(8,128)S(1)} all-to-all(f32[16,40,128]{2,1,0:T(8,128)S(1)} %bitcast.37), channel_id=1, replica_groups={{128,130,132,134,136,138,140,142,192,194,196,198,200,202,204,206},{144,..., dimensions={0} | all-to-all | bytes 655360 | tf_op jit(solution)/shard_map/all_to_all | solution.py:295
  101.3 0.8 collective-permute-start.10
  102.1 2.3 %collective-permute-start.11 = (f32[40,128]{1,0:T(8,128)S(1)}, f32[40,128]{1,0:T(8,128)S(1)}, u32[]{:S(2)}, u32[]{:S(2)}) collective-permute-start(f32[40,128]{1,0:T(8,128)S(1)} %slice_reduce_fusion), channel_id=1, source_target_pairs={{0,16},{2,18},{4,20},{6,22},{8,24},{10,26},{12,28},{14,30},{16,32}... | collective-permute-start | bytes 61448 | tf_op jit(solution)/shard_map/ppermute | solution.py:303
  104.4 1.5 collective-permute-start.12
  105.9 2.0 %collective-permute-done.10 = f32[40,128]{1,0:T(8,128)S(1)} collective-permute-done((f32[40,128]{1,0:T(8,128)S(1)}, f32[40,128]{1,0:T(8,128)S(1)}, u32[]{:S(2)}, u32[]{:S(2)}) %collective-permute-start.10) | collective-permute-done | bytes 20512 | tf_op jit(solution)/shard_map/ppermute | solution.py:303
  107.9 0.3 collective-permute-done.12
  108.3 10.6 %all_to_all.45 = f32[16,40,128]{2,1,0:T(8,128)S(1)} all-to-all(f32[16,40,128]{2,1,0:T(8,128)S(1)} %broadcast_in_dim.16), channel_id=1, replica_groups={{128,130,132,134,136,138,140,142,192,194,196,198,200,202,204,206},{144,..., dimensions={0} | all-to-all | bytes 655360 | tf_op jit(solution)/shard_map/all_to_all | solution.py:295
  118.9 3.7 %collective-permute-start.13 = (f32[256,128]{1,0:T(8,128)S(1)}, f32[256,128]{1,0:T(8,128)S(1)}, u32[]{:S(2)}, u32[]{:S(2)}) collective-permute-start(f32[256,128]{1,0:T(8,128)S(1)} %slice.61), channel_id=1, source_target_pairs={{0,1},{1,0},{2,3},{3,2},{4,5},{5,4},{6,7},{7,6},{8,9},{9,8},{10,11... | collective-permute-start | bytes 393224 | tf_op jit(solution)/shard_map/ppermute | solution.py:260
  122.6 0.1 pad_add_fusion.section
  122.7 8.2 %shard_map.57 = (f32[256,256]{1,0:T(8,128)S(1)}, f32[256,256]{1,0:T(8,128)S(1)}) custom-call(s32[2]{0:T(128)S(1)} %pad_add_fusion.section, f32[384,128]{1,0:T(8,128)S(1)} %get-tuple-element.39.kept, f32[640,128]{1,0:T(8,128)S(1)} %bitcast.24), custom_call_target="tpu_custom_call" | custom-call | tf_op jit(solution)/shard_map/pallas_call | solution.py:332
  131.0 0.2 shard_map.58.gram
  131.2 0.5 copy-done.4
  131.7 0.7 shard_map.59
  132.4 3.6 %all-to-all-start.6 = ((f32[8,80,128]{2,1,0:T(8,128)}), f32[8,80,128]{2,1,0:T(8,128)S(1)}, u32[]{:S(2)}, u32[]{:S(2)}) async-start(f32[8,80,128]{2,1,0:T(8,128)} %bitcast.10), calls=%async_computation.6 | async-start | bytes 655360 | tf_op jit(solution)/shard_map/all_to_all | solution.py:292
  136.0 0.0 copy-start.3
  136.0 2.3 %collective-permute-start.17 = (f32[256,256]{1,0:T(8,128)S(1)}, f32[256,256]{1,0:T(8,128)S(1)}, u32[]{:S(2)}, u32[]{:S(2)}) collective-permute-start(f32[256,256]{1,0:T(8,128)S(1)} %copy-done.5), channel_id=1, source_target_pairs={{0,64},{64,128},{128,192},{1,65},{65,129},{129,193},{2,66},{66,130... | collective-permute-start | bytes 786440 | tf_op jit(solution)/shard_map/ppermute | solution.py:340
  138.3 4.9 %all-to-all-done.6 = f32[8,80,128]{2,1,0:T(8,128)S(1)} async-done(((f32[8,80,128]{2,1,0:T(8,128)}), f32[8,80,128]{2,1,0:T(8,128)S(1)}, u32[]{:S(2)}, u32[]{:S(2)}) %all-to-all-start.6) | async-done | bytes 327712 | tf_op jit(solution)/shard_map/all_to_all | solution.py:292
  143.2 3.7 %collective-permute-start.14 = (f32[80,128]{1,0:T(8,128)S(1)}, f32[80,128]{1,0:T(8,128)S(1)}, u32[]{:S(2)}, u32[]{:S(2)}) collective-permute-start(f32[80,128]{1,0:T(8,128)S(1)} %reduce_sum.39), channel_id=1, source_target_pairs={{0,32},{2,34},{4,36},{6,38},{8,40},{10,42},{12,44},{14,46},{16,48}... | collective-permute-start | bytes 122888 | tf_op jit(solution)/shard_map/ppermute | solution.py:303
  146.9 0.9 collective-permute-start.15
  147.8 2.6 %collective-permute-start.16 = (f32[80,128]{1,0:T(8,128)S(1)}, f32[80,128]{1,0:T(8,128)S(1)}, u32[]{:S(2)}, u32[]{:S(2)}) collective-permute-start(f32[80,128]{1,0:T(8,128)S(1)} %reduce_sum.39), channel_id=1, source_target_pairs={{0,48},{2,50},{4,52},{6,54},{8,56},{10,58},{12,60},{14,62},{16,0},... | collective-permute-start | bytes 122888 | tf_op jit(solution)/shard_map/ppermute | solution.py:303
  150.5 0.0 collective-permute-done.17
  150.5 0.0 collective-permute-done.14
  150.5 2.2 %collective-permute-done.15 = f32[80,128]{1,0:T(8,128)S(1)} collective-permute-done((f32[80,128]{1,0:T(8,128)S(1)}, f32[80,128]{1,0:T(8,128)S(1)}, u32[]{:S(2)}, u32[]{:S(2)}) %collective-permute-start.15) | collective-permute-done | bytes 40992 | tf_op jit(solution)/shard_map/ppermute | solution.py:303
  152.7 0.0 collective-permute-done.16
  152.7 11.1 %all_to_all.46 = f32[8,80,128]{2,1,0:T(8,128)S(1)} all-to-all(f32[8,80,128]{2,1,0:T(8,128)S(1)} %broadcast_in_dim.17), channel_id=1, replica_groups={{0,2,4,6,8,10,12,14},{16,18,20,22,24,26,28,30},{32,34,36,38,40,42,44,46..., dimensions={0} | all-to-all | bytes 655360 | tf_op jit(solution)/shard_map/all_to_all | solution.py:292
  163.8 2.4 %collective-permute-start.18 = (f32[256,128]{1,0:T(8,128)S(1)}, f32[256,128]{1,0:T(8,128)S(1)}, u32[]{:S(2)}, u32[]{:S(2)}) collective-permute-start(f32[256,128]{1,0:T(8,128)S(1)} %slice.62), channel_id=1, source_target_pairs={{0,1},{1,0},{2,3},{3,2},{4,5},{5,4},{6,7},{7,6},{8,9},{9,8},{10,11... | collective-permute-start | bytes 393224 | tf_op jit(solution)/shard_map/ppermute | solution.py:260
  166.3 1.0 collective-permute-done.18.beside
  167.2 0.1 shard_map.62
  167.4 0.7 collective-permute-start.19
  168.1 0.7 collective-permute-start.20
  168.8 1.3 collective-permute-start.21
  170.1 2.2 %shard_map.61 = f32[4,256,256]{2,1,0:T(8,128)} custom-call(f32[4,256,256]{2,1,0:T(8,128)S(1)} %bitcast.22, f32[256,256]{1,0:T(8,128)S(1)} %broadcast_select_fusion.upper, f32[256,256]{1,0:T(8,128)S(1)} %get-tuple-element.47.inverse), custom_call_target="tpu_custom_call" | custom-call | tf_op jit(solution)/shard_map/pallas_call | solution.py:352
  172.3 5.3 %collective-permute-done.21 = f32[64,512]{1,0:T(8,128)S(1)} collective-permute-done((f32[64,512]{1,0:T(8,128)S(1)}, f32[64,512]{1,0:T(8,128)S(1)}, u32[]{:S(2)}, u32[]{:S(2)}) %collective-permute-start.21) | collective-permute-done | bytes 131104 | tf_op jit(solution)/shard_map/ppermute | solution.py:351
  177.6 0.7 slice_bitcast_fusion
  (36 shorter events, 0.4 us)
Async XLA Ops:
  0.6 6.3 %collective-permute-start = (f32[4,256,256]{2,1,0:T(8,128)}, f32[4,256,256]{2,1,0:T(8,128)}, u32[]{:S(2)}, u32[]{:S(2)}) collective-permute-start(f32[4,256,256]{2,1,0:T(8,128)} %bitcast.19), channel_id=1, source_target_pairs={{0,1},{1,0},{2,3},{3,2},{4,5},{5,4},{6,7},{7,6},{8,9},{9,8},{10,11... | collective-permute-start | bytes 3145736 | tf_op jit(solution)/shard_map/ppermute | solution.py:260
  4.0 2.8 %collective-permute-start.1 = (f32[256,256]{1,0:T(8,128)}, f32[256,256]{1,0:T(8,128)S(1)}, u32[]{:S(2)}, u32[]{:S(2)}) collective-permute-start(f32[256,256]{1,0:T(8,128)} %bitcast.39), channel_id=1, source_target_pairs={{0,1},{1,0},{2,3},{3,2},{4,5},{5,4},{6,7},{7,6},{8,9},{9,8},{10,11... | collective-permute-start | bytes 786440 | tf_op jit(solution)/shard_map/ppermute | solution.py:260
  4.1 1.2 copy-start
  5.3 1.7 copy-start.1
  7.0 1.0 copy-start.2
  24.7 9.7 %collective-permute-start.2 = (f32[40,128]{1,0:T(8,128)S(1)}, f32[40,128]{1,0:T(8,128)S(1)}, u32[]{:S(2)}, u32[]{:S(2)}) collective-permute-start(f32[40,128]{1,0:T(8,128)S(1)} %slice_reduce_fusion.2), channel_id=1, source_target_pairs={{0,32},{2,34},{4,36},{6,38},{8,40},{10,42},{12,44},{14,46},{16,48}... | collective-permute-start | bytes 61448 | tf_op jit(solution)/shard_map/ppermute | solution.py:303
  30.8 4.8 %collective-permute-start.3 = (f32[40,128]{1,0:T(8,128)S(1)}, f32[40,128]{1,0:T(8,128)S(1)}, u32[]{:S(2)}, u32[]{:S(2)}) collective-permute-start(f32[40,128]{1,0:T(8,128)S(1)} %slice_reduce_fusion.2), channel_id=1, source_target_pairs={{0,16},{2,18},{4,20},{6,22},{8,24},{10,26},{12,28},{14,30},{16,32}... | collective-permute-start | bytes 61448 | tf_op jit(solution)/shard_map/ppermute | solution.py:303
  32.1 3.6 %collective-permute-start.4 = (f32[40,128]{1,0:T(8,128)S(1)}, f32[40,128]{1,0:T(8,128)S(1)}, u32[]{:S(2)}, u32[]{:S(2)}) collective-permute-start(f32[40,128]{1,0:T(8,128)S(1)} %slice_reduce_fusion.2), channel_id=1, source_target_pairs={{0,48},{2,50},{4,52},{6,54},{8,56},{10,58},{12,60},{14,62},{16,0},... | collective-permute-start | bytes 61448 | tf_op jit(solution)/shard_map/ppermute | solution.py:303
  45.9 5.6 %collective-permute-start.5 = (f32[256,128]{1,0:T(8,128)S(1)}, f32[256,128]{1,0:T(8,128)S(1)}, u32[]{:S(2)}, u32[]{:S(2)}) collective-permute-start(f32[256,128]{1,0:T(8,128)S(1)} %slice.57), channel_id=1, source_target_pairs={{0,1},{1,0},{2,3},{3,2},{4,5},{5,4},{6,7},{7,6},{8,9},{9,8},{10,11... | collective-permute-start | bytes 393224 | tf_op jit(solution)/shard_map/ppermute | solution.py:260
  63.9 6.7 %collective-permute-start.6 = (f32[40,128]{1,0:T(8,128)S(1)}, f32[40,128]{1,0:T(8,128)S(1)}, u32[]{:S(2)}, u32[]{:S(2)}) collective-permute-start(f32[40,128]{1,0:T(8,128)S(1)} %slice_reduce_fusion.1), channel_id=1, source_target_pairs={{0,32},{2,34},{4,36},{6,38},{8,40},{10,42},{12,44},{14,46},{16,48}... | collective-permute-start | bytes 61448 | tf_op jit(solution)/shard_map/ppermute | solution.py:303
  65.7 5.0 %collective-permute-start.7 = (f32[40,128]{1,0:T(8,128)S(1)}, f32[40,128]{1,0:T(8,128)S(1)}, u32[]{:S(2)}, u32[]{:S(2)}) collective-permute-start(f32[40,128]{1,0:T(8,128)S(1)} %slice_reduce_fusion.1), channel_id=1, source_target_pairs={{0,16},{2,18},{4,20},{6,22},{8,24},{10,26},{12,28},{14,30},{16,32}... | collective-permute-start | bytes 61448 | tf_op jit(solution)/shard_map/ppermute | solution.py:303
  69.6 3.5 %collective-permute-start.8 = (f32[40,128]{1,0:T(8,128)S(1)}, f32[40,128]{1,0:T(8,128)S(1)}, u32[]{:S(2)}, u32[]{:S(2)}) collective-permute-start(f32[40,128]{1,0:T(8,128)S(1)} %slice_reduce_fusion.1), channel_id=1, source_target_pairs={{0,48},{2,50},{4,52},{6,54},{8,56},{10,58},{12,60},{14,62},{16,0},... | collective-permute-start | bytes 61448 | tf_op jit(solution)/shard_map/ppermute | solution.py:303
  84.8 5.4 %collective-permute-start.9 = (f32[256,128]{1,0:T(8,128)S(1)}, f32[256,128]{1,0:T(8,128)S(1)}, u32[]{:S(2)}, u32[]{:S(2)}) collective-permute-start(f32[256,128]{1,0:T(8,128)S(1)} %slice.59), channel_id=1, source_target_pairs={{0,1},{1,0},{2,3},{3,2},{4,5},{5,4},{6,7},{7,6},{8,9},{9,8},{10,11... | collective-permute-start | bytes 393224 | tf_op jit(solution)/shard_map/ppermute | solution.py:260
  101.3 6.6 %collective-permute-start.10 = (f32[40,128]{1,0:T(8,128)S(1)}, f32[40,128]{1,0:T(8,128)S(1)}, u32[]{:S(2)}, u32[]{:S(2)}) collective-permute-start(f32[40,128]{1,0:T(8,128)S(1)} %slice_reduce_fusion), channel_id=1, source_target_pairs={{0,32},{2,34},{4,36},{6,38},{8,40},{10,42},{12,44},{14,46},{16,48}... | collective-permute-start | bytes 61448 | tf_op jit(solution)/shard_map/ppermute | solution.py:303
  102.1 5.9 %collective-permute-start.11 = (f32[40,128]{1,0:T(8,128)S(1)}, f32[40,128]{1,0:T(8,128)S(1)}, u32[]{:S(2)}, u32[]{:S(2)}) collective-permute-start(f32[40,128]{1,0:T(8,128)S(1)} %slice_reduce_fusion), channel_id=1, source_target_pairs={{0,16},{2,18},{4,20},{6,22},{8,24},{10,26},{12,28},{14,30},{16,32}... | collective-permute-start | bytes 61448 | tf_op jit(solution)/shard_map/ppermute | solution.py:303
  104.4 3.8 %collective-permute-start.12 = (f32[40,128]{1,0:T(8,128)S(1)}, f32[40,128]{1,0:T(8,128)S(1)}, u32[]{:S(2)}, u32[]{:S(2)}) collective-permute-start(f32[40,128]{1,0:T(8,128)S(1)} %slice_reduce_fusion), channel_id=1, source_target_pairs={{0,48},{2,50},{4,52},{6,54},{8,56},{10,58},{12,60},{14,62},{16,0},... | collective-permute-start | bytes 61448 | tf_op jit(solution)/shard_map/ppermute | solution.py:303
  118.9 12.8 %collective-permute-start.13 = (f32[256,128]{1,0:T(8,128)S(1)}, f32[256,128]{1,0:T(8,128)S(1)}, u32[]{:S(2)}, u32[]{:S(2)}) collective-permute-start(f32[256,128]{1,0:T(8,128)S(1)} %slice.61), channel_id=1, source_target_pairs={{0,1},{1,0},{2,3},{3,2},{4,5},{5,4},{6,7},{7,6},{8,9},{9,8},{10,11... | collective-permute-start | bytes 393224 | tf_op jit(solution)/shard_map/ppermute | solution.py:260
  130.9 0.7 copy-start.4
  132.4 3.6 %copy-start.5 = (f32[256,256]{1,0:T(8,128)S(1)}, f32[256,256]{1,0:T(8,128)}, u32[]{:S(2)}) copy-start(f32[256,256]{1,0:T(8,128)} %copy-done.4) | copy-start | bytes 786436
  132.4 10.8 %all-to-all-start.6 = ((f32[8,80,128]{2,1,0:T(8,128)}), f32[8,80,128]{2,1,0:T(8,128)S(1)}, u32[]{:S(2)}, u32[]{:S(2)}) async-start(f32[8,80,128]{2,1,0:T(8,128)} %bitcast.10), calls=%async_computation.6 | async-start | bytes 655360 | tf_op jit(solution)/shard_map/all_to_all | solution.py:292
  136.0 14.5 %copy-start.3 = (f32[1,256,256]{2,1,0:T(8,128)S(1)}, f32[1,256,256]{2,1,0:T(8,128)}, u32[]{:S(2)}) copy-start(f32[1,256,256]{2,1,0:T(8,128)} %param.3) | copy-start | bytes 786436
  136.0 14.5 %collective-permute-start.17 = (f32[256,256]{1,0:T(8,128)S(1)}, f32[256,256]{1,0:T(8,128)S(1)}, u32[]{:S(2)}, u32[]{:S(2)}) collective-permute-start(f32[256,256]{1,0:T(8,128)S(1)} %copy-done.5), channel_id=1, source_target_pairs={{0,64},{64,128},{128,192},{1,65},{65,129},{129,193},{2,66},{66,130... | collective-permute-start | bytes 786440 | tf_op jit(solution)/shard_map/ppermute | solution.py:340
  143.2 7.3 %collective-permute-start.14 = (f32[80,128]{1,0:T(8,128)S(1)}, f32[80,128]{1,0:T(8,128)S(1)}, u32[]{:S(2)}, u32[]{:S(2)}) collective-permute-start(f32[80,128]{1,0:T(8,128)S(1)} %reduce_sum.39), channel_id=1, source_target_pairs={{0,32},{2,34},{4,36},{6,38},{8,40},{10,42},{12,44},{14,46},{16,48}... | collective-permute-start | bytes 122888 | tf_op jit(solution)/shard_map/ppermute | solution.py:303
  146.9 5.8 %collective-permute-start.15 = (f32[80,128]{1,0:T(8,128)S(1)}, f32[80,128]{1,0:T(8,128)S(1)}, u32[]{:S(2)}, u32[]{:S(2)}) collective-permute-start(f32[80,128]{1,0:T(8,128)S(1)} %reduce_sum.39), channel_id=1, source_target_pairs={{0,16},{2,18},{4,20},{6,22},{8,24},{10,26},{12,28},{14,30},{16,32}... | collective-permute-start | bytes 122888 | tf_op jit(solution)/shard_map/ppermute | solution.py:303
  147.8 4.9 %collective-permute-start.16 = (f32[80,128]{1,0:T(8,128)S(1)}, f32[80,128]{1,0:T(8,128)S(1)}, u32[]{:S(2)}, u32[]{:S(2)}) collective-permute-start(f32[80,128]{1,0:T(8,128)S(1)} %reduce_sum.39), channel_id=1, source_target_pairs={{0,48},{2,50},{4,52},{6,54},{8,56},{10,58},{12,60},{14,62},{16,0},... | collective-permute-start | bytes 122888 | tf_op jit(solution)/shard_map/ppermute | solution.py:303
  163.8 3.4 %collective-permute-start.18 = (f32[256,128]{1,0:T(8,128)S(1)}, f32[256,128]{1,0:T(8,128)S(1)}, u32[]{:S(2)}, u32[]{:S(2)}) collective-permute-start(f32[256,128]{1,0:T(8,128)S(1)} %slice.62), channel_id=1, source_target_pairs={{0,1},{1,0},{2,3},{3,2},{4,5},{5,4},{6,7},{7,6},{8,9},{9,8},{10,11... | collective-permute-start | bytes 393224 | tf_op jit(solution)/shard_map/ppermute | solution.py:260
  167.4 4.9 %collective-permute-start.19 = (f32[64,512]{1,0:T(8,128)S(1)}, f32[64,512]{1,0:T(8,128)S(1)}, u32[]{:S(2)}, u32[]{:S(2)}) collective-permute-start(f32[64,512]{1,0:T(8,128)S(1)} %get-tuple-element.51), channel_id=1, source_target_pairs={{192,128},{193,129},{194,130},{195,131},{196,132},{197,133},{198,1... | collective-permute-start | bytes 393224 | tf_op jit(solution)/shard_map/ppermute | solution.py:351
  168.1 4.2 %collective-permute-start.20 = (f32[64,512]{1,0:T(8,128)S(1)}, f32[64,512]{1,0:T(8,128)S(1)}, u32[]{:S(2)}, u32[]{:S(2)}) collective-permute-start(f32[64,512]{1,0:T(8,128)S(1)} %get-tuple-element.50), channel_id=1, source_target_pairs={{192,64},{193,65},{194,66},{195,67},{196,68},{197,69},{198,70},{19... | collective-permute-start | bytes 393224 | tf_op jit(solution)/shard_map/ppermute | solution.py:351
  168.8 8.8 %collective-permute-start.21 = (f32[64,512]{1,0:T(8,128)S(1)}, f32[64,512]{1,0:T(8,128)S(1)}, u32[]{:S(2)}, u32[]{:S(2)}) collective-permute-start(f32[64,512]{1,0:T(8,128)S(1)} %get-tuple-element.49), channel_id=1, source_target_pairs={{192,0},{193,1},{194,2},{195,3},{196,4},{197,5},{198,6},{199,7},{2... | collective-permute-start | bytes 393224 | tf_op jit(solution)/shard_map/ppermute | solution.py:351
